TPU v7x, 256 devices: a whole 4x4x8 slice. The times are simulated.
256 devices in a mesh: section: 2 (over core), grp: 4 (over x), dev: 32 (over y, z).
Axes of the slice: x: 4, y: 4, z: 8, core: 2. Of those that a mesh axis runs over, the one named last changes fastest.
Arguments:
- frames: bfloat16 [4, 512, 512, 256], P('grp', 'dev', 'section'), may hold values from -6 to 6
- templates: bfloat16 [8192, 256], P('dev'), may hold values from -0.375 to 0.375
- pair_block: int32 [2, 4, 256], P('section', 'grp', 'dev'), may hold values from 0 to 63
- pair_tile: int32 [2, 4, 256], P('section', 'grp', 'dev'), may hold values from 0 to 3
- pair_count: int32 [2, 4, 32], P('section', 'grp', 'dev'), may hold values from 1 to 8, 128 in all within a row
- owner_order: int32 [8192], replicated, may hold values from 0 to 8191, each once
Outputs:
- quantities: float32 [4, 8192], P('grp', 'dev')
Inputs may be any that keep to these rules, and one draw needn't show every extreme that they name: `pair_count`: each device's count of live slots; the counts of one section half and run sum to half of all slots there, and one of them is 8. `owner_order`: A permutation of the precursors.
All inputs are finite; a program needn't handle non-finite values.
Results may differ from a plain program's by a relative error of at most 0.00037.
Values may be sent and summed in bfloat16 or wider, within the bound.
A program may use at most 64 MiB of HBM per device.

v0:
```python
import math

import jax
import jax.numpy as jnp
from jax import lax
from jax.sharding import PartitionSpec as P

MOB = 512
SCALES = 6
RAD = 4
TM = 64
PB = 128
PREC = 8192


retention_spread = 2.0


def extended(cells, sides, width):
    for axis, dim in sides:
        count = lax.axis_size(axis)
        ends = count - 1
        head = lax.slice_in_dim(cells, 0, width, axis=dim)
        tail = lax.slice_in_dim(cells, cells.shape[dim] - width, cells.shape[dim], axis=dim)
        cells = jnp.concatenate(
            [
                lax.ppermute(tail, axis, [(i, (i + 1) % count) for i in range(ends)]),
                cells,
                lax.ppermute(head, axis, [((i + 1) % count, i) for i in range(ends)]),
            ],
            axis=dim,
        )
    return cells


def retention_weights():
    bell_values = [
        math.exp(-0.5 * (offset / retention_spread) ** 2) for offset in range(-RAD, RAD + 1)
    ]
    bell_total = sum(bell_values)
    return [weight_value / bell_total for weight_value in bell_values]


def mobility_kernels(row_start, row_count):
    row_place = (row_start + jnp.arange(row_count, dtype=jnp.int32)).astype(jnp.float32)
    col_place = jnp.arange(MOB, dtype=jnp.int32).astype(jnp.float32)
    distance = row_place[:, None] - col_place[None, :]
    tables = []
    for level in range(SCALES):
        spread_scans = 2.0**level
        scaled = distance / spread_scans
        tables.append(
            (1.0 - scaled * scaled)
            * jnp.exp(-0.5 * scaled * scaled)
            / math.sqrt(0.75 * math.sqrt(math.pi) * spread_scans)
        )
    return jnp.stack(tables).astype(jnp.bfloat16)


def on_device(frames, templates, pair_block, pair_tile, pair_count, owner_order):
    section_index = lax.axis_index("section")
    weights = retention_weights()
    count_frames = frames.shape[1]
    mob_local = frames.shape[2]
    channels = frames.shape[3]
    framed = extended(frames, (("dev", 1),), RAD)
    padded = framed.astype(jnp.float32)
    smoothed = weights[0] * padded[:, 0:count_frames]
    for offset in range(1, 2 * RAD + 1):
        smoothed = smoothed + weights[offset] * padded[:, offset : offset + count_frames]
    smoothed = smoothed.astype(jnp.bfloat16)
    gathered = lax.all_gather(smoothed, "section", axis=2, tiled=True)
    kernels = mobility_kernels(section_index * mob_local, mob_local)
    wavelet_stack = jnp.einsum(
        "smn,fnc->smfc", kernels, gathered[0], preferred_element_type=jnp.float32
    ).astype(jnp.bfloat16)
    template_panel = lax.all_gather(templates, "dev", axis=0, tiled=True)
    blocks = template_panel.shape[0] // PB
    live_pairs = pair_count[0, 0, 0]
    block_ids = pair_block[0, 0]
    tile_ids = pair_tile[0, 0]

    def visit_pair(slot_index, totals):
        block_id = block_ids[slot_index]
        tile_id = tile_ids[slot_index]
        tile_cells = lax.dynamic_slice_in_dim(wavelet_stack, tile_id * TM, TM, 1).reshape(
            -1, channels
        )
        block_rows = lax.dynamic_slice_in_dim(template_panel, block_id * PB, PB, 0)
        scores = jnp.dot(tile_cells, block_rows.T, preferred_element_type=jnp.float32)
        response = jnp.mean(jnp.maximum(scores, 0.0), axis=0)
        block_hit = (jnp.arange(blocks, dtype=jnp.int32) == block_id).astype(jnp.float32)
        return totals + block_hit[:, None] * response[None, :]

    totals = lax.fori_loop(0, live_pairs, visit_pair, jnp.zeros((blocks, PB), jnp.float32))
    placed = jnp.zeros((PREC,), jnp.float32).at[owner_order].set(totals.reshape(-1))[None]
    summed = lax.psum(placed, "section")
    owned = lax.psum_scatter(summed, "dev", scatter_dimension=1, tiled=True)
    run_count = lax.axis_size("grp")
    run_mask = (jnp.arange(run_count, dtype=jnp.int32) == lax.axis_index("grp")).astype(jnp.float32)
    run_totals = lax.psum(run_mask * jnp.sum(owned), ("grp", "dev"))
    own_total = jnp.sum(run_totals * run_mask)
    factor = jnp.mean(run_totals) / own_total
    return owned * factor


def solution(mesh):
    placed = (
        P("grp", "dev", "section", None),
        P("dev", None),
        P("section", "grp", "dev"),
        P("section", "grp", "dev"),
        P("section", "grp", "dev"),
        P(),
    )
    return jax.shard_map(
        on_device, mesh=mesh, in_specs=placed, out_specs=P("grp", "dev"), check_vma=False
    )
```

profile of v0, /device:TPU:0, one launch (start us, length us, event | category | flops | bytes accessed | tf_op | source)
XLA Modules:
  0.0 833.5 jit_solution(16655650894832102042)
XLA Ops:
  7.8 2.1 collective-permute-start
  11.2 9.8 %collective-permute-done = bf16[1,4,256,256]{3,2,1,0:T(8,128)(2,1)S(1)} collective-permute-done((bf16[1,4,256,256]{3,2,1,0:T(8,128)(2,1)S(1)}, bf16[1,4,256,256]{3,2,1,0:T(8,128)(2,1)S(1)}, u32[]{:S(2)}, u32[]{:S(2)}) %collective-permute-start) | collective-permute-done | bytes 524320 | tf_op jit(solution)/shard_map/ppermute | solution.py:27
  21.1 4.3 collective-permute-done.1
  25.4 2.1 maximum_convert_fusion
  27.4 5.7 fusion.4
  35.6 19.7 %all-gather.3.cloned.1.call-done = bf16[1,16,512,256]{3,2,1,0:T(8,128)(2,1)} async-done(((bf16[1,16,256,256]{3,2,1,0:T(8,128)(2,1)}), bf16[1,16,512,256]{3,2,1,0:T(8,128)(2,1)}) %all-gather.3.cloned.1.call-update) | async-done | bytes 4194320 | tf_op jit(solution)/shard_map/all_gather | solution.py:72
  55.2 11.7 %convolution_convert_fusion = bf16[6,256,16,256]{3,1,2,0:T(8,128)(2,1)} fusion(bf16[1,16,512,256]{3,2,1,0:T(8,128)(2,1)} %all-gather.3.cloned.1.call-done, bf16[6,256,512]{2,1,0:T(8,128)(2,1)S(1)} %fusion.58), kind=kOutput, calls=%fused_computation.9 | convolution fusion | flops 6448742400 | bytes 18350080 | tf_op jit(solution)/shard_map/smn,fnc->smfc/dot_general | solution.py:74
  66.9 73.7 %all-gather.5.cloned.1.call-done = bf16[8192,256]{1,0:T(8,128)(2,1)} async-done(((bf16[256,256]{1,0:T(8,128)(2,1)}), bf16[8192,256]{1,0:T(8,128)(2,1)}) %all-gather.5.cloned.1.call-update) | async-done | bytes 4194320 | tf_op jit(solution)/shard_map/all_gather | solution.py:77
  140.7 41.0 %while.10 = (s32[]{:T(128)}, f32[64,128]{1,0:T(8,128)S(1)}, s32[]{:T(128)}, s32[8]{0:T(128)S(1)}, s32[8]{0:T(128)S(1)}, /*index=5*/bf16[6,256,16,256]{3,1,2,0:T(...) while((s32[]{:T(128)}, f32[64,128]{1,0:T(8,128)S(1)}, ...), condition=%wide.region_2.0_spmd, body=%wide.region_0.0_spmd.sunk | while | flops 404242560 | bytes 15862567 | solution.py:95
  142.5 2.3 constant_dynamic-slice_fusion.2
  144.8 1.9 copy.14
  147.9 2.2 fusion.70
  152.6 2.3 constant_dynamic-slice_fusion.2
  154.9 1.9 copy.14
  158.0 2.2 fusion.70
  162.7 2.3 constant_dynamic-slice_fusion.2
  168.0 2.2 fusion.70
  172.7 2.3 constant_dynamic-slice_fusion.2
  178.1 2.2 fusion.70
  181.7 30.5 %scatter_custom_fusion = f32[8192]{0:T(1024)S(1)} fusion(s32[8192]{0:T(1024)S(1)} %compare_select_fusion, f32[8192]{0:T(1024)S(1)} %bitcast.30, f32[]{:T(128)} %constant.32.clone.1), kind=kCustom, calls=%fused_computation.91 | custom fusion | bytes 32772 | tf_op jit(solution)/shard_map/scatter | solution.py:96
  212.2 2.6 copy.10
  214.8 258.0 %reduce-scatter.4.cloned.1.call-done = f32[256,1]{1,0:T(8,128)} async-done(((f32[8192,1]{1,0:T(8,128)}), f32[256,1]{1,0:T(8,128)}) %reduce-scatter.4.cloned.1.call-update) | async-done | bytes 1040
  473.8 2.5 psum.16
  477.5 346.8 %psum.15 = f32[4]{0:T(128)S(1)} all-reduce(f32[4]{0:T(128)S(1)} %compare_select_fusion.2), channel_id=1, replica_groups=mesh['section'=2,'grp'=4,'dev'=32] {'grp','dev'}, use_global_device_ids=true, to_apply=%region_7.0 | all-reduce | flops 4 | bytes 32 | tf_op jit(solution)/shard_map/psum | solution.py:101
  (51 shorter events, 19.4 us)
Async XLA Ops:
  6.5 48.7 %all-gather.3.cloned.1.call-start = ((), (), s32[]{:S(2)}) async-start(), calls=%async_computation.1 | async-start | bytes 6291456 | tf_op jit(solution)/shard_map/all_gather | solution.py:72
  7.8 13.3 %collective-permute-start = (bf16[1,4,256,256]{3,2,1,0:T(8,128)(2,1)S(1)}, bf16[1,4,256,256]{3,2,1,0:T(8,128)(2,1)S(1)}, u32[]{:S(2)}, u32[]{:S(2)}) collective-permute-start(bf16[1,4,256,256]{3,2,1,0:T(8,128)(2,1)S(1)} %get-tuple-element.74), channel_id=1, source_target_pairs={{0,1},{1,2},{2,3},{3,4},{4,5},{5,6},{6,7},{7,8},{8,9},{9,10},{10,1... | collective-permute-start | bytes 1572872 | tf_op jit(solution)/shard_map/ppermute | solution.py:27
  9.9 15.4 %collective-permute-start.1 = (bf16[1,4,256,256]{3,2,1,0:T(8,128)(2,1)S(1)}, bf16[1,4,256,256]{3,2,1,0:T(8,128)(2,1)S(1)}, u32[]{:S(2)}, u32[]{:S(2)}) collective-permute-start(bf16[1,4,256,256]{3,2,1,0:T(8,128)(2,1)S(1)} %get-tuple-element.75), channel_id=1, source_target_pairs={{1,0},{2,1},{3,2},{4,3},{5,4},{6,5},{7,6},{8,7},{9,8},{10,9},{11,1... | collective-permute-start | bytes 1572872 | tf_op jit(solution)/shard_map/ppermute | solution.py:29
  27.4 6.6 copy-start
  33.2 107.5 %all-gather.5.cloned.1.call-start = ((), (), s32[]{:S(2)}) async-start(), calls=%async_computation.2 | async-start | bytes 4325376 | tf_op jit(solution)/shard_map/all_gather | solution.py:77
  33.9 438.9 %reduce-scatter.4.cloned.1.call-start = ((), (), s32[]{:S(2)}) async-start(), calls=%async_computation.3 | async-start | bytes 4325376
  35.5 105.1 %copy-start.1 = (s32[1,1,8]{2,1,0:T(1,128)S(1)}, s32[1,1,8]{2,1,0:T(1,128)}, u32[]{:S(2)}) copy-start(s32[1,1,8]{2,1,0:T(1,128)} %param.10) | copy-start | bytes 100
  35.6 105.1 %copy-start.2 = (s32[1,1,8]{2,1,0:T(1,128)S(1)}, s32[1,1,8]{2,1,0:T(1,128)}, u32[]{:S(2)}) copy-start(s32[1,1,8]{2,1,0:T(1,128)} %param.11) | copy-start | bytes 100
Sparse Core Ops, SparseCore 0:
  33.3 21.9 all-gather.2
  57.8 82.8 all-gather.4
  214.9 257.8 reduce-scatter.3
where the time goes:
time: 835 us; the launch traced here: 834 us
  waiting for transfers between devices  366 us (44%)
  blocking collectives  349 us (42%)
  local copies, waits for them, and re-layouts  56.8 us (7%)
  matrix products  20.6 us (2%)
  between operations  14.6 us (2%)
  other arithmetic  14.4 us (2%)
    psum x1, blocking collectives, on_device(): run_totals = lax.psum(run_mask * jnp.sum(owned), ('grp', 'dev'))  347 us
    unnamed x4, waiting for transfers between devices  259 us
    all_gather x1, waiting for transfers between devices, on_device(): template_panel = lax.all_gather(templates, 'dev', axis=0, tiled=True)  73.7 us
    scatter x1, local copies, waits for them, and re-layouts, on_device(): jnp.zeros((PREC,), jnp.float32).at[owner_order].set(totals.reshape(-1))  30.5 us
    all_gather x1, waiting for transfers between devices, on_device(): gathered = lax.all_gather(smoothed, 'section', axis=2, tiled=True)  19.7 us
    dynamic_slice x8, local copies, waits for them, and re-layouts, visit_pair(): lax.dynamic_slice_in_dim(wavelet_stack, tile_id * TM, TM, 1)  16.8 us
  transfers between devices with their start and end apart: 5, of which 5 were waited for; matrix products, arithmetic and copies ran while one was open for 2% of the time, Pallas kernels for 0%

commit v1 on v0

--- a/solution.py
+++ b/solution.py
@@ -3,6 +3,8 @@
 import jax
 import jax.numpy as jnp
 from jax import lax
+from jax.experimental import pallas as pl
+from jax.experimental.pallas import tpu as pltpu
 from jax.sharding import PartitionSpec as P
 
 MOB = 512
@@ -72,36 +74,82 @@
     gathered = lax.all_gather(smoothed, "section", axis=2, tiled=True)
     kernels = mobility_kernels(section_index * mob_local, mob_local)
     wavelet_stack = jnp.einsum(
-        "smn,fnc->smfc", kernels, gathered[0], preferred_element_type=jnp.float32
+        "smn,fnc->sfmc", kernels, gathered[0], preferred_element_type=jnp.float32
     ).astype(jnp.bfloat16)
     template_panel = lax.all_gather(templates, "dev", axis=0, tiled=True)
-    blocks = template_panel.shape[0] // PB
+    slots = pair_block.shape[2]
     live_pairs = pair_count[0, 0, 0]
     block_ids = pair_block[0, 0]
     tile_ids = pair_tile[0, 0]
-
-    def visit_pair(slot_index, totals):
-        block_id = block_ids[slot_index]
-        tile_id = tile_ids[slot_index]
-        tile_cells = lax.dynamic_slice_in_dim(wavelet_stack, tile_id * TM, TM, 1).reshape(
-            -1, channels
-        )
-        block_rows = lax.dynamic_slice_in_dim(template_panel, block_id * PB, PB, 0)
-        scores = jnp.dot(tile_cells, block_rows.T, preferred_element_type=jnp.float32)
-        response = jnp.mean(jnp.maximum(scores, 0.0), axis=0)
-        block_hit = (jnp.arange(blocks, dtype=jnp.int32) == block_id).astype(jnp.float32)
-        return totals + block_hit[:, None] * response[None, :]
-
-    totals = lax.fori_loop(0, live_pairs, visit_pair, jnp.zeros((blocks, PB), jnp.float32))
-    placed = jnp.zeros((PREC,), jnp.float32).at[owner_order].set(totals.reshape(-1))[None]
-    summed = lax.psum(placed, "section")
-    owned = lax.psum_scatter(summed, "dev", scatter_dimension=1, tiled=True)
-    run_count = lax.axis_size("grp")
-    run_mask = (jnp.arange(run_count, dtype=jnp.int32) == lax.axis_index("grp")).astype(jnp.float32)
-    run_totals = lax.psum(run_mask * jnp.sum(owned), ("grp", "dev"))
-    own_total = jnp.sum(run_totals * run_mask)
+    responses = score_pairs(wavelet_stack, template_panel, tile_ids, block_ids, live_pairs)
+    precursors = block_ids[:, None] * PB + jnp.arange(PB, dtype=jnp.int32)[None, :]
+    positions = owner_order[precursors]
+    placed = jnp.zeros((PREC,), jnp.float32).at[positions.reshape(-1)].add(responses.reshape(-1))
+    dev_count = lax.axis_size("dev")
+    local_total = jnp.sum(responses)
+    payload = jnp.concatenate(
+        [
+            placed.reshape(dev_count, PREC // dev_count),
+            jnp.broadcast_to(local_total, (dev_count, 128)),
+        ],
+        axis=1,
+    )
+    reduced = lax.psum_scatter(payload, "dev", scatter_dimension=0, tiled=True)
+    reduced = lax.psum(reduced, "section")
+    owned = reduced[:, : PREC // dev_count]
+    own_total = reduced[0, PREC // dev_count]
+    run_totals = lax.all_gather(own_total, "grp")
     factor = jnp.mean(run_totals) / own_total
     return owned * factor
+
+
+def score_kernel(tile_ref, block_ref, count_ref, wave_ref, rows_ref, out_ref):
+    slot = pl.program_id(0)
+    live = slot < count_ref[0]
+
+    @pl.when(live)
+    def _():
+        rows = rows_ref[...]
+        acc = jnp.zeros((1, PB), jnp.float32)
+        for level in range(SCALES):
+            cells = wave_ref[level].reshape(-1, rows.shape[1])
+            scores = lax.dot_general(
+                cells, rows, (((1,), (1,)), ((), ())), preferred_element_type=jnp.float32
+            )
+            acc = acc + jnp.sum(jnp.maximum(scores, 0.0), axis=0, keepdims=True)
+        cell_count = SCALES * wave_ref.shape[1] * wave_ref.shape[2]
+        out_ref[0] = acc / cell_count
+
+    @pl.when(jnp.logical_not(live))
+    def _():
+        out_ref[0] = jnp.zeros((1, PB), jnp.float32)
+
+
+def score_pairs(wavelet_stack, template_panel, tile_ids, block_ids, live_pairs):
+    slots = tile_ids.shape[0]
+    scales, frames_local, mob_local, channels = wavelet_stack.shape
+
+    def last_live(k, count_ref):
+        return jnp.minimum(k, count_ref[0] - 1)
+
+    grid_spec = pltpu.PrefetchScalarGridSpec(
+        num_scalar_prefetch=3,
+        grid=(slots,),
+        in_specs=[
+            pl.BlockSpec(
+                (scales, frames_local, TM, channels),
+                lambda k, t, b, c: (0, 0, t[last_live(k, c)], 0),
+            ),
+            pl.BlockSpec((PB, channels), lambda k, t, b, c: (b[last_live(k, c)], 0)),
+        ],
+        out_specs=pl.BlockSpec((1, 1, PB), lambda k, t, b, c: (k, 0, 0)),
+    )
+    out = pl.pallas_call(
+        score_kernel,
+        grid_spec=grid_spec,
+        out_shape=jax.ShapeDtypeStruct((slots, 1, PB), jnp.float32),
+    )(tile_ids, block_ids, live_pairs.reshape(1), wavelet_stack, template_panel)
+    return out.reshape(slots, PB)
 
 
 def solution(mesh):

time: 835 us -> 327 us (0.39)
  the two profiles are of different devices: /device:TPU:0 before, /device:TPU:1 now
where the time goes in v1:
time: 327 us
  blocking collectives  153 us (47%)
  waiting for transfers between devices  97 us (30%)
  other arithmetic  16.4 us (5%)
  between operations  15.6 us (5%)
  Pallas kernels  14 us (4%)
  local copies, waits for them, and re-layouts  13.4 us (4%)
  matrix products  11.9 us (4%)
  starting transfers between devices  5.74 us (2%)
    unnamed x2, blocking collectives  119 us
    all_gather x1, waiting for transfers between devices, on_device(): template_panel = lax.all_gather(templates, 'dev', axis=0, tiled=True)  70.5 us
    psum x1, blocking collectives, on_device(): reduced = lax.psum(reduced, 'section')  33.3 us
    pallas_call x1, Pallas kernels, score_pairs(): pl.pallas_call(score_kernel, grid_spec=grid_spec, out_shape=jax.ShapeDtyp...  14 us
    all_gather x1, waiting for transfers between devices, on_device(): gathered = lax.all_gather(smoothed, 'section', axis=2, tiled=True)  12.4 us
    dot_general x1, matrix products, on_device(): jnp.einsum('smn,fnc->sfmc', kernels, gathered[0], preferred_element_type=...  11.9 us
    ppermute x1, waiting for transfers between devices, extended(): lax.ppermute(tail, axis, [(i, (i + 1) % count) for i in range(ends)])  9.24 us
  transfers between devices with their start and end apart: 4, of which 4 were waited for; matrix products, arithmetic and copies ran while one was open for 6% of the time, Pallas kernels for 0%

profile of v1, /device:TPU:1, one launch (start us, length us, event | category | flops | bytes accessed | tf_op | source)
XLA Modules:
  0.0 326.6 jit_solution(11887394414419073815)
XLA Ops:
  6.5 2.9 copy.15
  9.5 4.4 %collective-permute-start = (bf16[1,4,256,256]{2,3,1,0:T(8,128)(2,1)S(1)}, bf16[1,4,256,256]{2,3,1,0:T(8,128)(2,1)S(1)}, u32[]{:S(2)}, u32[]{:S(2)}) collective-permute-start(bf16[1,4,256,256]{2,3,1,0:T(8,128)(2,1)S(1)} %get-tuple-element.5), channel_id=1, source_target_pairs={{0,1},{1,2},{2,3},{3,4},{4,5},{5,6},{6,7},{7,8},{8,9},{9,10},{10,1... | collective-permute-start | bytes 1572872 | tf_op jit(solution)/shard_map/ppermute | solution.py:29
  13.9 1.3 collective-permute-start.1
  15.2 9.2 %collective-permute-done = bf16[1,4,256,256]{2,3,1,0:T(8,128)(2,1)S(1)} collective-permute-done((bf16[1,4,256,256]{2,3,1,0:T(8,128)(2,1)S(1)}, bf16[1,4,256,256]{2,3,1,0:T(8,128)(2,1)S(1)}, u32[]{:S(2)}, u32[]{:S(2)}) %collective-permute-start) | collective-permute-done | bytes 524320 | tf_op jit(solution)/shard_map/ppermute | solution.py:29
  24.4 4.2 %collective-permute-done.1 = bf16[1,4,256,256]{2,3,1,0:T(8,128)(2,1)S(1)} collective-permute-done((bf16[1,4,256,256]{2,3,1,0:T(8,128)(2,1)S(1)}, bf16[1,4,256,256]{2,3,1,0:T(8,128)(2,1)S(1)}, u32[]{:S(2)}, u32[]{:S(2)}) %collective-permute-start.1) | collective-permute-done | bytes 524320 | tf_op jit(solution)/shard_map/ppermute | solution.py:31
  29.1 5.7 %fusion.1 = bf16[1,16,256,256]{2,3,1,0:T(8,128)(2,1)} fusion(f32[1,24,256,256]{2,3,1,0:T(8,128)S(1)} %maximum_convert_fusion), kind=kLoop, calls=%fused_computation.5 | loop fusion | flops 18874368 | bytes 39845888 | tf_op jit(solution)/shard_map/convert_element_type | solution.py:73
  34.9 0.7 all-gather.6.cloned.1.call-update
  36.3 6.1 %gather_fusion = s32[1024]{0:T(1024)S(1)} fusion(s32[8192]{0:T(1024)S(1)} %copy-done, s32[1024]{0:T(1024)S(1)} %fusion.60), kind=kCustom, calls=%fused_computation | custom fusion | bytes 12288 | tf_op jit(solution)/shard_map/gather | solution.py:86
  42.5 0.6 dynamic-slice.1
  43.1 0.6 dynamic-slice
  45.2 12.4 %all-gather.4.cloned.1.call-done = bf16[1,16,512,256]{2,3,1,0:T(8,128)(2,1)} async-done(((bf16[1,16,256,256]{2,3,1,0:T(8,128)(2,1)}), bf16[1,16,512,256]{2,3,1,0:T(8,128)(2,1)}) %all-gather.4.cloned.1.call-update) | async-done | bytes 4194320 | tf_op jit(solution)/shard_map/all_gather | solution.py:74
  57.7 11.9 %convert_bitcast_fusion.wave_ref = bf16[6,16,256,256]{3,2,1,0:T(8,128)(2,1)} fusion(bf16[1,16,512,256]{2,3,1,0:T(8,128)(2,1)} %all-gather.4.cloned.1.call-done, bf16[6,256,512]{2,1,0:T(8,128)(2,1)S(1)} %fusion.55), kind=kOutput, calls=%fused_computation.2 | convolution fusion | flops 6448742400 | bytes 18350080 | tf_op jit(solution)/shard_map/smn,fnc->sfmc/dot_general | solution.py:76
  69.5 70.5 %all-gather.6.cloned.1.call-done.rows_ref = bf16[8192,256]{1,0:T(8,128)(2,1)} async-done(((bf16[256,256]{1,0:T(8,128)(2,1)}), bf16[8192,256]{1,0:T(8,128)(2,1)}) %all-gather.6.cloned.1.call-update) | async-done | bytes 4194320 | tf_op jit(solution)/shard_map/all_gather | solution.py:79
  140.0 14.0 %shard_map.64 = f32[8,1,128]{2,1,0:T(1,128)} custom-call(s32[8]{0:T(128)} %bitcast.32, s32[8]{0:T(128)} %bitcast.31, s32[1]{0:T(128)} %bitcast.27.count_ref, bf16[6,16,256,256]{3,2,1,0:T(8,128)(2,1)} %convert_bitcast_fusion.wave_ref, bf16[8192,256]{1,0:T(8,128)(2,1)} %all-gather.6.cloned.1.call-done.rows_ref), custom_call_target="tpu_custom_call" | custom-call | tf_op jit(solution)/shard_map/pallas_call | solution.py:147
  154.1 1.3 reduce_sum.18
  155.4 6.1 %scatter_custom_fusion = f32[8192]{0:T(1024)S(1)} fusion(s32[1024]{0:T(1024)S(1)} %bitcast.30, f32[1024]{0:T(1024)} %bitcast.29, f32[]{:T(128)} %constant.19.clone.1), kind=kCustom, calls=%fused_computation.84 | custom fusion | flops 1024 | bytes 33280 | tf_op jit(solution)/shard_map/scatter-add | solution.py:87
  161.5 0.7 concatenate.15
  162.1 110.2 %all-reduce.2 = f32[32,384]{1,0:T(8,128)S(1)} all-reduce(f32[32,384]{1,0:T(8,128)S(1)} %concatenate.15), channel_id=3, replica_groups=mesh['section'=2,'grp'=4,'dev'=32] {'dev'}, use_global_device_ids=true, to_apply=%region_2.0.clone | all-reduce | flops 12288 | bytes 98304
  272.4 0.6 constant_dynamic-slice_fusion
  273.0 33.3 %psum.7 = f32[1,384]{1,0:T(1,128)S(1)} all-reduce(f32[1,384]{1,0:T(1,128)S(1)} %constant_dynamic-slice_fusion), channel_id=1, replica_groups=mesh['section'=2,'grp'=4,'dev'=32] {'section'}, use_global_device_ids=true, to_apply=%region_3.0 | all-reduce | flops 384 | bytes 3072 | tf_op jit(solution)/shard_map/psum | solution.py:98
  306.8 1.3 bitcast_dynamic-update-slice_fusion
  308.1 9.0 %all-reduce.1 = f32[4]{0:T(128)S(1)} all-reduce(f32[4]{0:T(128)S(1)} %bitcast_dynamic-update-slice_fusion), channel_id=2, replica_groups=mesh['section'=2,'grp'=4,'dev'=32] {'grp'}, use_global_device_ids=true, to_apply=%add.1 | all-reduce | flops 4 | bytes 32
  317.1 0.7 reduce.2
  319.2 0.6 slice_multiply_fusion.9
  (27 shorter events, 2.7 us)
Async XLA Ops:
  6.5 29.8 %copy-start = (s32[8192]{0:T(1024)S(1)}, s32[8192]{0:T(1024)}, u32[]{:S(2)}) copy-start(s32[8192]{0:T(1024)} %param.11) | copy-start | bytes 98308
  6.5 51.1 %all-gather.4.cloned.1.call-start = ((), (), s32[]{:S(2)}) async-start(), calls=%async_computation | async-start | bytes 6291456 | tf_op jit(solution)/shard_map/all_gather | solution.py:74
  9.5 15.0 %collective-permute-start = (bf16[1,4,256,256]{2,3,1,0:T(8,128)(2,1)S(1)}, bf16[1,4,256,256]{2,3,1,0:T(8,128)(2,1)S(1)}, u32[]{:S(2)}, u32[]{:S(2)}) collective-permute-start(bf16[1,4,256,256]{2,3,1,0:T(8,128)(2,1)S(1)} %get-tuple-element.5), channel_id=1, source_target_pairs={{0,1},{1,2},{2,3},{3,4},{4,5},{5,6},{6,7},{7,8},{8,9},{9,10},{10,1... | collective-permute-start | bytes 1572872 | tf_op jit(solution)/shard_map/ppermute | solution.py:29
  13.9 14.7 %collective-permute-start.1 = (bf16[1,4,256,256]{2,3,1,0:T(8,128)(2,1)S(1)}, bf16[1,4,256,256]{2,3,1,0:T(8,128)(2,1)S(1)}, u32[]{:S(2)}, u32[]{:S(2)}) collective-permute-start(bf16[1,4,256,256]{2,3,1,0:T(8,128)(2,1)S(1)} %get-tuple-element.6), channel_id=1, source_target_pairs={{1,0},{2,1},{3,2},{4,3},{5,4},{6,5},{7,6},{8,7},{9,8},{10,9},{11,1... | collective-permute-start | bytes 1572872 | tf_op jit(solution)/shard_map/ppermute | solution.py:31
  29.1 7.2 %copy-start.1 = (s32[1,1,8]{2,1,0:T(1,128)S(1)}, s32[1,1,8]{2,1,0:T(1,128)}, u32[]{:S(2)}) copy-start(s32[1,1,8]{2,1,0:T(1,128)} %param.8) | copy-start | bytes 100
  34.8 7.7 %copy-start.3 = (u32[256]{0:T(256)S(1)}, u32[256]{0:T(256)}, u32[]{:S(2)}) copy-start(u32[256]{0:T(256)} %constant.92) | copy-start | bytes 3076
  34.8 8.3 %copy-start.2 = (u32[256]{0:T(256)S(1)}, u32[256]{0:T(256)}, u32[]{:S(2)}) copy-start(u32[256]{0:T(256)} %constant.86) | copy-start | bytes 3076
  34.8 105.2 %all-gather.6.cloned.1.call-start = ((), (), s32[]{:S(2)}) async-start(), calls=%async_computation.1 | async-start | bytes 4325376 | tf_op jit(solution)/shard_map/all_gather | solution.py:79
Sparse Core Ops, SparseCore 0:
  34.9 22.6 all-gather.3
  60.3 79.7 all-gather.5

commit v2 on v1

--- a/solution.py
+++ b/solution.py
@@ -1,3 +1,4 @@
+import functools
 import math
 
 import jax
@@ -89,18 +90,143 @@
     local_total = jnp.sum(responses)
     payload = jnp.concatenate(
         [
-            placed.reshape(dev_count, PREC // dev_count),
-            jnp.broadcast_to(local_total, (dev_count, 128)),
+            placed.reshape(dev_count, 1, PREC // dev_count),
+            jnp.broadcast_to(local_total, (dev_count, 1, 128)),
         ],
-        axis=1,
-    )
-    reduced = lax.psum_scatter(payload, "dev", scatter_dimension=0, tiled=True)
-    reduced = lax.psum(reduced, "section")
-    owned = reduced[:, : PREC // dev_count]
-    own_total = reduced[0, PREC // dev_count]
-    run_totals = lax.all_gather(own_total, "grp")
-    factor = jnp.mean(run_totals) / own_total
-    return owned * factor
+        axis=2,
+    )
+    return reduce_owned(payload)
+
+
+def reduce_kernel(sizes, payload_ref, out_ref, gathered, totals, send_sems, recv_sems, total_send, total_recv):
+    n_section, n_grp, n_dev = sizes
+    section = lax.axis_index("section")
+    grp = lax.axis_index("grp")
+    dev = lax.axis_index("dev")
+    me = section * n_dev + dev
+    peers = n_section * n_dev
+    owned_width = out_ref.shape[1]
+
+    barrier = pltpu.get_barrier_semaphore()
+
+    def greet(index, carry):
+        @pl.when(index != me)
+        def _():
+            pl.semaphore_signal(
+                barrier,
+                inc=1,
+                device_id=(index // n_dev, grp, index % n_dev),
+                device_id_type=pl.DeviceIdType.MESH,
+            )
+
+        return carry
+
+    lax.fori_loop(0, peers, greet, 0)
+    for step in range(1, n_grp):
+        pl.semaphore_signal(
+            barrier,
+            inc=1,
+            device_id=(section, (grp + step) % n_grp, dev),
+            device_id_type=pl.DeviceIdType.MESH,
+        )
+    pl.semaphore_wait(barrier, peers - 1 + n_grp - 1)
+
+    def chunk_copy(index):
+        return pltpu.make_async_remote_copy(
+            src_ref=payload_ref.at[index % n_dev],
+            dst_ref=gathered.at[me],
+            send_sem=send_sems.at[index],
+            recv_sem=recv_sems.at[me],
+            device_id=(index // n_dev, grp, index % n_dev),
+            device_id_type=pl.DeviceIdType.MESH,
+        )
+
+    def send(index, carry):
+        @pl.when(index != me)
+        def _():
+            chunk_copy(index).start()
+
+        return carry
+
+    lax.fori_loop(0, peers, send, 0)
+    gathered[me] = payload_ref[dev]
+
+    def arrive(index, carry):
+        @pl.when(index != me)
+        def _():
+            pltpu.make_async_remote_copy(
+                src_ref=payload_ref.at[0],
+                dst_ref=gathered.at[index],
+                send_sem=send_sems.at[index],
+                recv_sem=recv_sems.at[index],
+                device_id=(index // n_dev, grp, index % n_dev),
+                device_id_type=pl.DeviceIdType.MESH,
+            ).wait_recv()
+            chunk_copy(index).wait_send()
+
+        return carry
+
+    lax.fori_loop(0, peers, arrive, 0)
+
+    def accumulate(index, acc):
+        return acc + gathered[index]
+
+    summed = lax.fori_loop(0, peers, accumulate, jnp.zeros(gathered.shape[1:], jnp.float32))
+    totals[grp] = summed[:, owned_width:]
+
+    def total_copy(step):
+        target = (grp + step) % n_grp
+        return pltpu.make_async_remote_copy(
+            src_ref=totals.at[grp],
+            dst_ref=totals.at[grp],
+            send_sem=total_send.at[target],
+            recv_sem=total_recv.at[grp],
+            device_id=(section, target, dev),
+            device_id_type=pl.DeviceIdType.MESH,
+        )
+
+    for step in range(1, n_grp):
+        total_copy(step).start()
+    for step in range(1, n_grp):
+        source = (grp + step) % n_grp
+        pltpu.make_async_remote_copy(
+            src_ref=totals.at[source],
+            dst_ref=totals.at[source],
+            send_sem=total_send.at[source],
+            recv_sem=total_recv.at[source],
+            device_id=(section, source, dev),
+            device_id_type=pl.DeviceIdType.MESH,
+        ).wait_recv()
+        total_copy(step).wait_send()
+    run_sum = totals[0]
+    for index in range(1, n_grp):
+        run_sum = run_sum + totals[index]
+    own_total = summed[:, owned_width : owned_width + 1]
+    factor = (run_sum[:, 0:1] / n_grp) / own_total
+    out_ref[...] = summed[:, :owned_width] * factor
+
+
+def reduce_owned(payload):
+    sizes = (lax.axis_size("section"), lax.axis_size("grp"), lax.axis_size("dev"))
+    n_section, n_grp, n_dev = sizes
+    peers = n_section * n_dev
+    rows, one, width = payload.shape
+    owned_width = width - 128
+    return pl.pallas_call(
+        functools.partial(reduce_kernel, sizes),
+        out_shape=jax.ShapeDtypeStruct((1, owned_width), jnp.float32),
+        in_specs=[pl.BlockSpec(memory_space=pltpu.VMEM)],
+        out_specs=pl.BlockSpec(memory_space=pltpu.VMEM),
+        scratch_shapes=[
+            pltpu.VMEM((peers, 1, width), jnp.float32),
+            pltpu.VMEM((n_grp, 1, 128), jnp.float32),
+            pltpu.SemaphoreType.DMA((peers,)),
+            pltpu.SemaphoreType.DMA((peers,)),
+            pltpu.SemaphoreType.DMA((n_grp,)),
+            pltpu.SemaphoreType.DMA((n_grp,)),
+        ],
+        compiler_params=pltpu.CompilerParams(collective_id=0, has_side_effects=True),
+    )(payload)
 
 
 def score_kernel(tile_ref, block_ref, count_ref, wave_ref, rows_ref, out_ref):

time: 327 us -> 193 us (0.59)
  blocking collectives: 153 us -> 0 us
  Pallas kernels: 14 us -> 35.5 us
    unnamed x2 -> x0, blocking collectives: 119 us -> none
    psum x1 -> x0, blocking collectives: 33.3 us -> none  [on_device(): reduced = lax.psum(reduced, 'section')]
    pallas_call x0 -> x1, Pallas kernels: none -> 29.6 us  [reduce_owned(): pl.pallas_call(functools.partial(reduce_kernel, sizes), out_shape=jax.Sha...]
    pallas_call x1, Pallas kernels: 14 us -> 5.87 us  [score_pairs(): pl.pallas_call(score_kernel, grid_spec=grid_spec, out_shape=jax.ShapeDtyp...]
  transfers between devices with their start and end apart: 4 -> 4, of which waited for: 4 -> 4; matrix products, arithmetic and copies ran while one was open for 6% -> 10% of each run, Pallas kernels for 0% -> 0%
where the time goes in v2:
time: 193 us; the launch traced here: 192 us
  waiting for transfers between devices  98.3 us (51%)
  Pallas kernels  35.5 us (18%)
  other arithmetic  15.1 us (8%)
  between operations  14.2 us (7%)
  matrix products  11.8 us (6%)
  local copies, waits for them, and re-layouts  11.6 us (6%)
  starting transfers between devices  5.74 us (3%)
    all_gather x1, waiting for transfers between devices, on_device(): template_panel = lax.all_gather(templates, 'dev', axis=0, tiled=True)  70.6 us
    pallas_call x1, Pallas kernels, reduce_owned(): pl.pallas_call(functools.partial(reduce_kernel, sizes), out_shape=jax.Sha...  29.6 us
    all_gather x1, waiting for transfers between devices, on_device(): gathered = lax.all_gather(smoothed, 'section', axis=2, tiled=True)  13.6 us
    dot_general x1, matrix products, on_device(): jnp.einsum('smn,fnc->sfmc', kernels, gathered[0], preferred_element_type=...  11.8 us
    ppermute x1, waiting for transfers between devices, extended(): lax.ppermute(tail, axis, [(i, (i + 1) % count) for i in range(ends)])  9.24 us
    gather x1, local copies, waits for them, and re-layouts, on_device(): positions = owner_order[precursors]  6.15 us
    scatter-add x1, other arithmetic, on_device(): jnp.zeros((PREC,), jnp.float32).at[positions.reshape(-1)]  6.1 us
    pallas_call x1, Pallas kernels, score_pairs(): pl.pallas_call(score_kernel, grid_spec=grid_spec, out_shape=jax.ShapeDtyp...  5.87 us
  transfers between devices with their start and end apart: 4, of which 4 were waited for; matrix products, arithmetic and copies ran while one was open for 10% of the time, Pallas kernels for 0%

profile of v2, /device:TPU:1, one launch (start us, length us, event | category | flops | bytes accessed | tf_op | source)
XLA Modules:
  0.0 192.3 jit_solution(14590668435590730613)
XLA Ops:
  6.5 2.9 %copy.11 = bf16[1,16,256,256]{2,3,1,0:T(8,128)(2,1)S(1)} copy(bf16[1,16,256,256]{3,2,1,0:T(8,128)(2,1)} %param.6) | data formatting | bytes 4194304 | tf_op args[0]
  9.5 4.4 %collective-permute-start = (bf16[1,4,256,256]{2,3,1,0:T(8,128)(2,1)S(1)}, bf16[1,4,256,256]{2,3,1,0:T(8,128)(2,1)S(1)}, u32[]{:S(2)}, u32[]{:S(2)}) collective-permute-start(bf16[1,4,256,256]{2,3,1,0:T(8,128)(2,1)S(1)} %get-tuple-element.5), channel_id=1, source_target_pairs={{0,1},{1,2},{2,3},{3,4},{4,5},{5,6},{6,7},{7,8},{8,9},{9,10},{10,1... | collective-permute-start | bytes 1572872 | tf_op jit(solution)/shard_map/ppermute | solution.py:30
  13.9 1.3 collective-permute-start.1
  15.2 9.2 %collective-permute-done = bf16[1,4,256,256]{2,3,1,0:T(8,128)(2,1)S(1)} collective-permute-done((bf16[1,4,256,256]{2,3,1,0:T(8,128)(2,1)S(1)}, bf16[1,4,256,256]{2,3,1,0:T(8,128)(2,1)S(1)}, u32[]{:S(2)}, u32[]{:S(2)}) %collective-permute-start) | collective-permute-done | bytes 524320 | tf_op jit(solution)/shard_map/ppermute | solution.py:30
  24.4 4.2 %collective-permute-done.1 = bf16[1,4,256,256]{2,3,1,0:T(8,128)(2,1)S(1)} collective-permute-done((bf16[1,4,256,256]{2,3,1,0:T(8,128)(2,1)S(1)}, bf16[1,4,256,256]{2,3,1,0:T(8,128)(2,1)S(1)}, u32[]{:S(2)}, u32[]{:S(2)}) %collective-permute-start.1) | collective-permute-done | bytes 524320 | tf_op jit(solution)/shard_map/ppermute | solution.py:32
  28.6 0.5 maximum_convert_fusion
  29.1 5.7 %fusion.1 = bf16[1,16,256,256]{2,3,1,0:T(8,128)(2,1)} fusion(f32[1,24,256,256]{2,3,1,0:T(8,128)S(1)} %maximum_convert_fusion), kind=kLoop, calls=%fused_computation.5 | loop fusion | flops 18874368 | bytes 39845888 | tf_op jit(solution)/shard_map/convert_element_type | solution.py:74
  34.8 0.7 all-gather.5.cloned.1.call-update
  36.3 6.1 %gather_fusion = s32[1024]{0:T(1024)S(1)} fusion(s32[8192]{0:T(1024)S(1)} %copy-done, s32[1024]{0:T(1024)S(1)} %fusion.60), kind=kCustom, calls=%fused_computation | custom fusion | bytes 12288 | tf_op jit(solution)/shard_map/gather | solution.py:87
  42.5 0.2 fusion.56
  42.7 0.3 fusion.51
  43.0 0.3 fusion.52
  43.2 0.3 fusion.53
  43.5 0.3 fusion.54
  43.8 0.3 fusion.55
  44.0 13.6 %all-gather.3.cloned.1.call-done = bf16[1,16,512,256]{2,3,1,0:T(8,128)(2,1)} async-done(((bf16[1,16,256,256]{2,3,1,0:T(8,128)(2,1)}), bf16[1,16,512,256]{2,3,1,0:T(8,128)(2,1)}) %all-gather.3.cloned.1.call-update) | async-done | bytes 4194320 | tf_op jit(solution)/shard_map/all_gather | solution.py:75
  57.6 11.8 %convert_bitcast_fusion.wave_ref = bf16[6,16,256,256]{3,2,1,0:T(8,128)(2,1)} fusion(bf16[1,16,512,256]{2,3,1,0:T(8,128)(2,1)} %all-gather.3.cloned.1.call-done, bf16[6,256,512]{2,1,0:T(8,128)(2,1)S(1)} %fusion.55), kind=kOutput, calls=%fused_computation.2 | convolution fusion | flops 6448742400 | bytes 18350080 | tf_op jit(solution)/shard_map/smn,fnc->sfmc/dot_general | solution.py:77
  69.4 70.6 %all-gather.5.cloned.1.call-done.rows_ref = bf16[8192,256]{1,0:T(8,128)(2,1)} async-done(((bf16[256,256]{1,0:T(8,128)(2,1)}), bf16[8192,256]{1,0:T(8,128)(2,1)}) %all-gather.5.cloned.1.call-update) | async-done | bytes 4194320 | tf_op jit(solution)/shard_map/all_gather | solution.py:80
  140.0 5.9 %shard_map.64 = f32[8,1,128]{2,1,0:T(1,128)} custom-call(s32[8]{0:T(128)} %bitcast.29, s32[8]{0:T(128)} %bitcast.28, s32[1]{0:T(128)} %bitcast.23.count_ref, bf16[6,16,256,256]{3,2,1,0:T(8,128)(2,1)} %convert_bitcast_fusion.wave_ref, bf16[8192,256]{1,0:T(8,128)(2,1)} %all-gather.5.cloned.1.call-done.rows_ref), custom_call_target="tpu_custom_call" | custom-call | tf_op jit(solution)/shard_map/pallas_call | solution.py:273
  145.9 1.3 reduce_sum.9
  147.2 6.1 %scatter_custom_fusion = f32[8192]{0:T(1024)S(1)} fusion(s32[1024]{0:T(1024)S(1)} %bitcast.27, f32[1024]{0:T(1024)} %bitcast.26, f32[]{:T(128)} %constant.18.clone.1), kind=kCustom, calls=%fused_computation.84 | custom fusion | flops 1024 | bytes 33280 | tf_op jit(solution)/shard_map/scatter-add | solution.py:88
  153.3 1.3 concatenate.15.payload_ref
  154.6 29.6 %shard_map.65 = f32[1,256]{1,0:T(1,128)} custom-call(f32[32,1,384]{2,1,0:T(1,128)} %concatenate.15.payload_ref), custom_call_target="tpu_custom_call" | custom-call | tf_op jit(solution)/shard_map/pallas_call | solution.py:215
  184.2 1.2 copy.24
  (13 shorter events, 0.2 us)
Async XLA Ops:
  6.5 29.8 %copy-start = (s32[8192]{0:T(1024)S(1)}, s32[8192]{0:T(1024)}, u32[]{:S(2)}) copy-start(s32[8192]{0:T(1024)} %param.11) | copy-start | bytes 98308
  6.5 51.1 %all-gather.3.cloned.1.call-start = ((), (), s32[]{:S(2)}) async-start(), calls=%async_computation | async-start | bytes 6291456 | tf_op jit(solution)/shard_map/all_gather | solution.py:75
  9.5 15.0 %collective-permute-start = (bf16[1,4,256,256]{2,3,1,0:T(8,128)(2,1)S(1)}, bf16[1,4,256,256]{2,3,1,0:T(8,128)(2,1)S(1)}, u32[]{:S(2)}, u32[]{:S(2)}) collective-permute-start(bf16[1,4,256,256]{2,3,1,0:T(8,128)(2,1)S(1)} %get-tuple-element.5), channel_id=1, source_target_pairs={{0,1},{1,2},{2,3},{3,4},{4,5},{5,6},{6,7},{7,8},{8,9},{9,10},{10,1... | collective-permute-start | bytes 1572872 | tf_op jit(solution)/shard_map/ppermute | solution.py:30
  13.9 14.7 %collective-permute-start.1 = (bf16[1,4,256,256]{2,3,1,0:T(8,128)(2,1)S(1)}, bf16[1,4,256,256]{2,3,1,0:T(8,128)(2,1)S(1)}, u32[]{:S(2)}, u32[]{:S(2)}) collective-permute-start(bf16[1,4,256,256]{2,3,1,0:T(8,128)(2,1)S(1)} %get-tuple-element.6), channel_id=1, source_target_pairs={{1,0},{2,1},{3,2},{4,3},{5,4},{6,5},{7,6},{8,7},{9,8},{10,9},{11,1... | collective-permute-start | bytes 1572872 | tf_op jit(solution)/shard_map/ppermute | solution.py:32
  29.1 7.1 %copy-start.1 = (s32[1,1,8]{2,1,0:T(1,128)S(1)}, s32[1,1,8]{2,1,0:T(1,128)}, u32[]{:S(2)}) copy-start(s32[1,1,8]{2,1,0:T(1,128)} %param.8) | copy-start | bytes 100
  34.8 105.2 %all-gather.5.cloned.1.call-start = ((), (), s32[]{:S(2)}) async-start(), calls=%async_computation.1 | async-start | bytes 4325376 | tf_op jit(solution)/shard_map/all_gather | solution.py:80
Sparse Core Ops, SparseCore 0:
  34.9 22.6 all-gather.2
  60.2 79.7 all-gather.4

commit v3 on v2

--- a/solution.py
+++ b/solution.py
@@ -72,17 +72,32 @@
     for offset in range(1, 2 * RAD + 1):
         smoothed = smoothed + weights[offset] * padded[:, offset : offset + count_frames]
     smoothed = smoothed.astype(jnp.bfloat16)
-    gathered = lax.all_gather(smoothed, "section", axis=2, tiled=True)
+    section_count = lax.axis_size("section")
+    partner = lax.ppermute(
+        smoothed, "section", [(i, (i + 1) % section_count) for i in range(section_count)]
+    )
+    gathered = jnp.where(
+        section_index == 0,
+        jnp.concatenate([smoothed, partner], axis=2),
+        jnp.concatenate([partner, smoothed], axis=2),
+    )
     kernels = mobility_kernels(section_index * mob_local, mob_local)
     wavelet_stack = jnp.einsum(
         "smn,fnc->sfmc", kernels, gathered[0], preferred_element_type=jnp.float32
     ).astype(jnp.bfloat16)
-    template_panel = lax.all_gather(templates, "dev", axis=0, tiled=True)
+    half_rows = templates.shape[0] // 2
+    my_half = lax.dynamic_slice_in_dim(templates, section_index * half_rows, half_rows, 0)
+    my_rows = lax.all_gather(my_half, "dev", axis=0, tiled=True)
+    other_rows = lax.ppermute(
+        my_rows, "section", [(i, (i + 1) % section_count) for i in range(section_count)]
+    )
     slots = pair_block.shape[2]
     live_pairs = pair_count[0, 0, 0]
     block_ids = pair_block[0, 0]
     tile_ids = pair_tile[0, 0]
-    responses = score_pairs(wavelet_stack, template_panel, tile_ids, block_ids, live_pairs)
+    responses = score_pairs(
+        wavelet_stack, my_rows, other_rows, tile_ids, block_ids, live_pairs, section_index
+    )
     precursors = block_ids[:, None] * PB + jnp.arange(PB, dtype=jnp.int32)[None, :]
     positions = owner_order[precursors]
     placed = jnp.zeros((PREC,), jnp.float32).at[positions.reshape(-1)].add(responses.reshape(-1))
@@ -229,12 +244,12 @@
     )(payload)
 
 
-def score_kernel(tile_ref, block_ref, count_ref, wave_ref, rows_ref, out_ref):
+def score_kernel(tile_ref, block_ref, count_ref, section_ref, wave_ref, mine_ref, other_ref, out_ref):
     slot = pl.program_id(0)
     live = slot < count_ref[0]
-
-    @pl.when(live)
-    def _():
+    mine = block_ref[slot] % 2 == section_ref[0]
+
+    def score(rows_ref):
         rows = rows_ref[...]
         acc = jnp.zeros((1, PB), jnp.float32)
         for level in range(SCALES):
@@ -246,35 +261,55 @@
         cell_count = SCALES * wave_ref.shape[1] * wave_ref.shape[2]
         out_ref[0] = acc / cell_count
 
+    @pl.when(jnp.logical_and(live, mine))
+    def _():
+        score(mine_ref)
+
+    @pl.when(jnp.logical_and(live, jnp.logical_not(mine)))
+    def _():
+        score(other_ref)
+
     @pl.when(jnp.logical_not(live))
     def _():
         out_ref[0] = jnp.zeros((1, PB), jnp.float32)
 
 
-def score_pairs(wavelet_stack, template_panel, tile_ids, block_ids, live_pairs):
+def score_pairs(wavelet_stack, my_rows, other_rows, tile_ids, block_ids, live_pairs, section_index):
     slots = tile_ids.shape[0]
     scales, frames_local, mob_local, channels = wavelet_stack.shape
 
     def last_live(k, count_ref):
         return jnp.minimum(k, count_ref[0] - 1)
 
+    def rows_block(k, t, b, c, s):
+        return (b[last_live(k, c)] // 2, 0)
+
     grid_spec = pltpu.PrefetchScalarGridSpec(
-        num_scalar_prefetch=3,
+        num_scalar_prefetch=4,
         grid=(slots,),
         in_specs=[
             pl.BlockSpec(
                 (scales, frames_local, TM, channels),
-                lambda k, t, b, c: (0, 0, t[last_live(k, c)], 0),
+                lambda k, t, b, c, s: (0, 0, t[last_live(k, c)], 0),
             ),
-            pl.BlockSpec((PB, channels), lambda k, t, b, c: (b[last_live(k, c)], 0)),
+            pl.BlockSpec((PB, channels), rows_block),
+            pl.BlockSpec((PB, channels), rows_block),
         ],
-        out_specs=pl.BlockSpec((1, 1, PB), lambda k, t, b, c: (k, 0, 0)),
+        out_specs=pl.BlockSpec((1, 1, PB), lambda k, t, b, c, s: (k, 0, 0)),
     )
     out = pl.pallas_call(
         score_kernel,
         grid_spec=grid_spec,
         out_shape=jax.ShapeDtypeStruct((slots, 1, PB), jnp.float32),
-    )(tile_ids, block_ids, live_pairs.reshape(1), wavelet_stack, template_panel)
+    )(
+        tile_ids,
+        block_ids,
+        live_pairs.reshape(1),
+        section_index.astype(jnp.int32).reshape(1),
+        wavelet_stack,
+        my_rows,
+        other_rows,
+    )
     return out.reshape(slots, PB)
 
 

time: 193 us -> 171 us (0.89)
  waiting for transfers between devices: 98.3 us -> 53.6 us
  other arithmetic: 15.1 us -> 35.3 us
  starting transfers between devices: 5.74 us -> 11.9 us
  Pallas kernels: 35.5 us -> 31 us
    all_gather x2 -> x1, waiting for transfers between devices: 84.2 us -> 47.4 us  [on_device(): my_rows = lax.all_gather(my_half, 'dev', axis=0, tiled=True)]
    concatenate x0 -> x1, other arithmetic: none -> 16.2 us  [on_device(): jnp.concatenate([smoothed, partner], axis=2)]
    ppermute x1, waiting for transfers between devices: 9.24 us -> 1.72 us  [extended(): lax.ppermute(tail, axis, [(i, (i + 1) % count) for i in range(ends)])]
    ppermute x0 -> x2, starting transfers between devices: none -> 6.24 us  [the longest x1 4.56 us: on_device(): lax.ppermute(my_rows, 'section', [(i, (i + 1) % section_count) for i in r...]
    pallas_call x1, Pallas kernels: 29.6 us -> 25 us  [reduce_owned(): pl.pallas_call(functools.partial(reduce_kernel, sizes), out_shape=jax.Sha...]
    unnamed x5, other arithmetic: 1.23 us -> 4.75 us
    slice x1, local copies, waits for them, and re-layouts: 0.07 us -> 2.35 us  [extended(): lax.slice_in_dim(cells, cells.shape[dim] - width, cells.shape[dim], axis=...]
    unnamed x6 -> x11, local copies, waits for them, and re-layouts: 4.1 us -> 2.11 us
  transfers between devices with their start and end apart: 4 -> 5, of which waited for: 4 -> 3; matrix products, arithmetic and copies ran while one was open for 10% -> 28% of each run, Pallas kernels for 0% -> 0%
where the time goes in v3:
time: 171 us
  waiting for transfers between devices  53.6 us (31%)
  other arithmetic  35.3 us (21%)
  Pallas kernels  31 us (18%)
  between operations  14.2 us (8%)
  local copies, waits for them, and re-layouts  12.5 us (7%)
  matrix products  12.1 us (7%)
  starting transfers between devices  11.9 us (7%)
    all_gather x1, waiting for transfers between devices, on_device(): my_rows = lax.all_gather(my_half, 'dev', axis=0, tiled=True)  47.4 us
    pallas_call x1, Pallas kernels, reduce_owned(): pl.pallas_call(functools.partial(reduce_kernel, sizes), out_shape=jax.Sha...  25 us
    concatenate x1, other arithmetic, on_device(): jnp.concatenate([smoothed, partner], axis=2)  16.2 us
    dot_general x1, matrix products, on_device(): jnp.einsum('smn,fnc->sfmc', kernels, gathered[0], preferred_element_type=...  12.1 us
    gather x1, local copies, waits for them, and re-layouts, on_device(): positions = owner_order[precursors]  6.15 us
    scatter-add x1, other arithmetic, on_device(): jnp.zeros((PREC,), jnp.float32).at[positions.reshape(-1)]  6.1 us
    pallas_call x1, Pallas kernels, score_pairs(): pl.pallas_call(score_kernel, grid_spec=grid_spec, out_shape=jax.ShapeDtyp...  6.01 us
    convert_element_type x1, other arithmetic, on_device(): smoothed = smoothed.astype(jnp.bfloat16)  4.8 us
  transfers between devices with their start and end apart: 5, of which 3 were waited for; matrix products, arithmetic and copies ran while one was open for 28% of the time, Pallas kernels for 0%

profile of v3, /device:TPU:1, one launch (start us, length us, event | category | flops | bytes accessed | tf_op | source)
XLA Modules:
  0.0 170.7 jit_solution(2966153085014062002)
XLA Ops:
  8.1 2.4 %fusion.69 = (bf16[1,4,256,256]{3,2,1,0:T(8,128)(2,1)}, bf16[1,4,256,256]{3,2,1,0:T(8,128)(2,1)}) fusion(bf16[1,16,256,256]{3,2,1,0:T(8,128)(2,1)} %param.6), kind=kLoop, calls=%fused_computation.101 | loop fusion | bytes 2097152 | tf_op jit(solution)/shard_map/slice | solution.py:27
  10.4 4.4 %collective-permute-start = (bf16[1,4,256,256]{3,2,1,0:T(8,128)(2,1)}, bf16[1,4,256,256]{3,2,1,0:T(8,128)(2,1)S(1)}, u32[]{:S(2)}, u32[]{:S(2)}) collective-permute-start(bf16[1,4,256,256]{3,2,1,0:T(8,128)(2,1)} %get-tuple-element.5), channel_id=1, source_target_pairs={{0,1},{1,2},{2,3},{3,4},{4,5},{5,6},{6,7},{7,8},{8,9},{9,10},{10,1... | collective-permute-start | bytes 1572872 | tf_op jit(solution)/shard_map/ppermute | solution.py:30
  14.9 1.3 collective-permute-start.1
  16.9 6.1 %gather_fusion = s32[1024]{0:T(1024)S(1)} fusion(s32[8192]{0:T(1024)S(1)} %copy-done.2, s32[1024]{0:T(1024)S(1)} %fusion.67), kind=kCustom, calls=%fused_computation | custom fusion | bytes 12288 | tf_op jit(solution)/shard_map/gather | solution.py:102
  23.1 0.9 fusion.63
  24.0 1.7 %collective-permute-done = bf16[1,4,256,256]{3,2,1,0:T(8,128)(2,1)S(1)} collective-permute-done((bf16[1,4,256,256]{3,2,1,0:T(8,128)(2,1)}, bf16[1,4,256,256]{3,2,1,0:T(8,128)(2,1)S(1)}, u32[]{:S(2)}, u32[]{:S(2)}) %collective-permute-start) | collective-permute-done | bytes 524320 | tf_op jit(solution)/shard_map/ppermute | solution.py:30
  25.7 4.5 %collective-permute-done.1 = bf16[1,4,256,256]{3,2,1,0:T(8,128)(2,1)S(1)} collective-permute-done((bf16[1,4,256,256]{3,2,1,0:T(8,128)(2,1)}, bf16[1,4,256,256]{3,2,1,0:T(8,128)(2,1)S(1)}, u32[]{:S(2)}, u32[]{:S(2)}) %collective-permute-start.1) | collective-permute-done | bytes 524320 | tf_op jit(solution)/shard_map/ppermute | solution.py:32
  30.7 4.8 %fusion.1 = bf16[1,16,256,256]{3,2,1,0:T(8,128)(2,1)S(1)} fusion(f32[1,24,256,256]{3,2,1,0:T(8,128)S(1)} %maximum_convert_fusion), kind=kLoop, calls=%fused_computation.5 | loop fusion | flops 18874368 | bytes 39845888 | tf_op jit(solution)/shard_map/convert_element_type | solution.py:74
  35.5 1.7 collective-permute-start.2
  37.8 1.0 fusion.58
  38.8 1.0 fusion.59
  39.8 1.0 fusion.60
  40.7 0.9 fusion.61
  41.7 0.9 fusion.62
  42.6 47.4 %all-gather.2.cloned.1.call-done.mine_ref = bf16[4096,256]{1,0:T(8,128)(2,1)} async-done(((bf16[128,256]{1,0:T(8,128)(2,1)}), bf16[4096,256]{1,0:T(8,128)(2,1)}) %all-gather.2.cloned.1.call-update) | async-done | bytes 2097168 | tf_op jit(solution)/shard_map/all_gather | solution.py:90
  90.0 4.6 %collective-permute-start.3 = (bf16[4096,256]{1,0:T(8,128)(2,1)}, bf16[4096,256]{1,0:T(8,128)(2,1)}, u32[]{:S(2)}, u32[]{:S(2)}) collective-permute-start(bf16[4096,256]{1,0:T(8,128)(2,1)} %all-gather.2.cloned.1.call-done.mine_ref), channel_id=1, source_target_pairs={{0,128},{128,0},{1,129},{129,1},{2,130},{130,2},{3,131},{131,3},{4... | collective-permute-start | bytes 6291464 | tf_op jit(solution)/shard_map/ppermute | solution.py:91
  94.6 16.2 %fusion.70 = bf16[16,256,256]{2,1,0:T(8,128)(2,1)S(1)} fusion(f32[1,24,256,256]{3,2,1,0:T(8,128)} %copy-done.1), kind=kLoop, calls=%fused_computation.102 | loop fusion | flops 18874368 | bytes 39845888 | tf_op jit(solution)/shard_map/concatenate | solution.py:81
  110.8 12.1 %convert_bitcast_fusion.wave_ref = bf16[6,16,256,256]{3,2,1,0:T(8,128)(2,1)} fusion(bf16[16,256,256]{2,1,0:T(8,128)(2,1)} %bitcast.8, bf16[16,256,256]{2,1,0:T(8,128)(2,1)S(1)} %fusion.70, pred[]{:T(512)S(6)} %eq.3, bf16[6,256,512]{2,1,0:T(8,128)(2,1)S(1)} %copy-done.4), kind=kOutput, calls=%fused_computation.2 | convolution fusion | flops 6467616768 | bytes 18350080 | tf_op jit(solution)/shard_map/smn,fnc->sfmc/dot_general | solution.py:85
  122.9 6.0 %shard_map.64 = f32[8,1,128]{2,1,0:T(1,128)} custom-call(s32[8]{0:T(128)} %bitcast.32, s32[8]{0:T(128)} %bitcast.31, s32[1]{0:T(128)} %bitcast.26.count_ref, s32[1]{0:T(128)} %bitcast.6.section_ref, bf16[6,16,256,256]{3,2,1,0:T(8,128)(2,1)} %convert_bitcast_fusion.wave_ref, bf16[4096,256]{1,0:T(8,128)(2,1)} %all-gather.2.cloned.1.call-done.mine_ref, ...), custom_call_target="tpu_custom_call" | custom-call | tf_op jit(solution)/shard_map/pallas_call | solution.py:300
  128.9 1.3 reduce_sum.9
  130.2 6.1 %scatter_custom_fusion = f32[8192]{0:T(1024)S(1)} fusion(s32[1024]{0:T(1024)S(1)} %bitcast.30, f32[1024]{0:T(1024)} %bitcast.28, f32[]{:T(128)} %constant.18.clone.1), kind=kCustom, calls=%fused_computation.91 | custom fusion | flops 1024 | bytes 33280 | tf_op jit(solution)/shard_map/scatter-add | solution.py:103
  136.3 1.3 concatenate.35.payload_ref
  137.6 25.0 %shard_map.65 = f32[1,256]{1,0:T(1,128)} custom-call(f32[32,1,384]{2,1,0:T(1,128)} %concatenate.35.payload_ref), custom_call_target="tpu_custom_call" | custom-call | tf_op jit(solution)/shard_map/pallas_call | solution.py:230
  162.6 1.2 copy.22
  (21 shorter events, 2.8 us)
Async XLA Ops:
  6.5 0.9 copy-start
  6.5 23.7 %copy-start.3 = (bf16[1,16,256,256]{3,2,1,0:T(8,128)(2,1)S(1)}, bf16[1,16,256,256]{3,2,1,0:T(8,128)(2,1)}, u32[]{:S(2)}) copy-start(bf16[1,16,256,256]{3,2,1,0:T(8,128)(2,1)} %param.6) | copy-start | bytes 6291460
  6.5 10.4 %copy-start.2 = (s32[8192]{0:T(1024)S(1)}, s32[8192]{0:T(1024)}, u32[]{:S(2)}) copy-start(s32[8192]{0:T(1024)} %param.11) | copy-start | bytes 98308
  6.5 83.5 %all-gather.2.cloned.1.call-start = ((), (), s32[]{:S(2)}) async-start(), calls=%async_computation | async-start | bytes 2162688 | tf_op jit(solution)/shard_map/all_gather | solution.py:90
  10.4 15.3 %collective-permute-start = (bf16[1,4,256,256]{3,2,1,0:T(8,128)(2,1)}, bf16[1,4,256,256]{3,2,1,0:T(8,128)(2,1)S(1)}, u32[]{:S(2)}, u32[]{:S(2)}) collective-permute-start(bf16[1,4,256,256]{3,2,1,0:T(8,128)(2,1)} %get-tuple-element.5), channel_id=1, source_target_pairs={{0,1},{1,2},{2,3},{3,4},{4,5},{5,6},{6,7},{7,8},{8,9},{9,10},{10,1... | collective-permute-start | bytes 1572872 | tf_op jit(solution)/shard_map/ppermute | solution.py:30
  14.9 15.3 %collective-permute-start.1 = (bf16[1,4,256,256]{3,2,1,0:T(8,128)(2,1)}, bf16[1,4,256,256]{3,2,1,0:T(8,128)(2,1)S(1)}, u32[]{:S(2)}, u32[]{:S(2)}) collective-permute-start(bf16[1,4,256,256]{3,2,1,0:T(8,128)(2,1)} %get-tuple-element.6), channel_id=1, source_target_pairs={{1,0},{2,1},{3,2},{4,3},{5,4},{6,5},{7,6},{8,7},{9,8},{10,9},{11,1... | collective-permute-start | bytes 1572872 | tf_op jit(solution)/shard_map/ppermute | solution.py:32
  30.7 4.8 %copy-start.1 = (f32[1,24,256,256]{3,2,1,0:T(8,128)}, f32[1,24,256,256]{3,2,1,0:T(8,128)S(1)}, u32[]{:S(2)}) copy-start(f32[1,24,256,256]{3,2,1,0:T(8,128)S(1)} %maximum_convert_fusion) | copy-start | bytes 18874372
  35.5 75.3 %collective-permute-start.2 = (bf16[1,16,256,256]{3,2,1,0:T(8,128)(2,1)S(1)}, bf16[1,16,256,256]{3,2,1,0:T(8,128)(2,1)}, u32[]{:S(2)}, u32[]{:S(2)}) collective-permute-start(bf16[1,16,256,256]{3,2,1,0:T(8,128)(2,1)S(1)} %fusion.1), channel_id=1, source_target_pairs={{0,128},{128,0},{1,129},{129,1},{2,130},{130,2},{3,131},{131,3},{4... | collective-permute-start | bytes 6291464 | tf_op jit(solution)/shard_map/ppermute | solution.py:76
  90.0 20.8 %copy-start.4 = (bf16[6,256,512]{2,1,0:T(8,128)(2,1)S(1)}, bf16[6,256,512]{2,1,0:T(8,128)(2,1)}, u32[]{:S(2)}) copy-start(bf16[6,256,512]{2,1,0:T(8,128)(2,1)} %fusion.62) | copy-start | bytes 4718596
  90.0 32.9 %collective-permute-start.3 = (bf16[4096,256]{1,0:T(8,128)(2,1)}, bf16[4096,256]{1,0:T(8,128)(2,1)}, u32[]{:S(2)}, u32[]{:S(2)}) collective-permute-start(bf16[4096,256]{1,0:T(8,128)(2,1)} %all-gather.2.cloned.1.call-done.mine_ref), channel_id=1, source_target_pairs={{0,128},{128,0},{1,129},{129,1},{2,130},{130,2},{3,131},{131,3},{4... | collective-permute-start | bytes 6291464 | tf_op jit(solution)/shard_map/ppermute | solution.py:91
Sparse Core Ops, SparseCore 0:
  10.0 79.9 all-gather.1

commit v4 on v3

--- a/solution.py
+++ b/solution.py
@@ -14,6 +14,7 @@
 TM = 64
 PB = 128
 PREC = 8192
+DEV = ("dy", "dz")
 
 
 retention_spread = 2.0
@@ -44,9 +45,9 @@
     return [weight_value / bell_total for weight_value in bell_values]
 
 
-def mobility_kernels(row_start, row_count):
+def mobility_kernels(row_start, row_count, col_start):
     row_place = (row_start + jnp.arange(row_count, dtype=jnp.int32)).astype(jnp.float32)
-    col_place = jnp.arange(MOB, dtype=jnp.int32).astype(jnp.float32)
+    col_place = ((col_start + jnp.arange(MOB, dtype=jnp.int32)) % MOB).astype(jnp.float32)
     distance = row_place[:, None] - col_place[None, :]
     tables = []
     for level in range(SCALES):
@@ -66,7 +67,7 @@
     count_frames = frames.shape[1]
     mob_local = frames.shape[2]
     channels = frames.shape[3]
-    framed = extended(frames, (("dev", 1),), RAD)
+    framed = extended(frames, ((DEV, 1),), RAD)
     padded = framed.astype(jnp.float32)
     smoothed = weights[0] * padded[:, 0:count_frames]
     for offset in range(1, 2 * RAD + 1):
@@ -76,18 +77,15 @@
     partner = lax.ppermute(
         smoothed, "section", [(i, (i + 1) % section_count) for i in range(section_count)]
     )
-    gathered = jnp.where(
-        section_index == 0,
-        jnp.concatenate([smoothed, partner], axis=2),
-        jnp.concatenate([partner, smoothed], axis=2),
-    )
-    kernels = mobility_kernels(section_index * mob_local, mob_local)
+    gathered = jnp.concatenate([smoothed, partner], axis=2)
+    kernels = mobility_kernels(section_index * mob_local, mob_local, section_index * mob_local)
     wavelet_stack = jnp.einsum(
         "smn,fnc->sfmc", kernels, gathered[0], preferred_element_type=jnp.float32
     ).astype(jnp.bfloat16)
     half_rows = templates.shape[0] // 2
     my_half = lax.dynamic_slice_in_dim(templates, section_index * half_rows, half_rows, 0)
-    my_rows = lax.all_gather(my_half, "dev", axis=0, tiled=True)
+    my_rows = lax.all_gather(my_half, "dz", axis=0, tiled=True)
+    my_rows = lax.all_gather(my_rows, "dy", axis=0, tiled=True)
     other_rows = lax.ppermute(
         my_rows, "section", [(i, (i + 1) % section_count) for i in range(section_count)]
     )
@@ -101,7 +99,7 @@
     precursors = block_ids[:, None] * PB + jnp.arange(PB, dtype=jnp.int32)[None, :]
     positions = owner_order[precursors]
     placed = jnp.zeros((PREC,), jnp.float32).at[positions.reshape(-1)].add(responses.reshape(-1))
-    dev_count = lax.axis_size("dev")
+    dev_count = lax.axis_size(DEV)
     local_total = jnp.sum(responses)
     payload = jnp.concatenate(
         [
@@ -114,10 +112,13 @@
 
 
 def reduce_kernel(sizes, payload_ref, out_ref, gathered, totals, send_sems, recv_sems, total_send, total_recv):
-    n_section, n_grp, n_dev = sizes
+    n_section, n_grp, n_dy, n_dz = sizes
+    n_dev = n_dy * n_dz
     section = lax.axis_index("section")
     grp = lax.axis_index("grp")
-    dev = lax.axis_index("dev")
+    dy = lax.axis_index("dy")
+    dz = lax.axis_index("dz")
+    dev = dy * n_dz + dz
     me = section * n_dev + dev
     peers = n_section * n_dev
     owned_width = out_ref.shape[1]
@@ -130,7 +131,7 @@
             pl.semaphore_signal(
                 barrier,
                 inc=1,
-                device_id=(index // n_dev, grp, index % n_dev),
+                device_id=(index // n_dev, grp, index % n_dev // n_dz, index % n_dz),
                 device_id_type=pl.DeviceIdType.MESH,
             )
 
@@ -141,7 +142,7 @@
         pl.semaphore_signal(
             barrier,
             inc=1,
-            device_id=(section, (grp + step) % n_grp, dev),
+            device_id=(section, (grp + step) % n_grp, dy, dz),
             device_id_type=pl.DeviceIdType.MESH,
         )
     pl.semaphore_wait(barrier, peers - 1 + n_grp - 1)
@@ -152,7 +153,7 @@
             dst_ref=gathered.at[me],
             send_sem=send_sems.at[index],
             recv_sem=recv_sems.at[me],
-            device_id=(index // n_dev, grp, index % n_dev),
+            device_id=(index // n_dev, grp, index % n_dev // n_dz, index % n_dz),
             device_id_type=pl.DeviceIdType.MESH,
         )
 
@@ -174,7 +175,7 @@
                 dst_ref=gathered.at[index],
                 send_sem=send_sems.at[index],
                 recv_sem=recv_sems.at[index],
-                device_id=(index // n_dev, grp, index % n_dev),
+                device_id=(index // n_dev, grp, index % n_dev // n_dz, index % n_dz),
                 device_id_type=pl.DeviceIdType.MESH,
             ).wait_recv()
             chunk_copy(index).wait_send()
@@ -196,7 +197,7 @@
             dst_ref=totals.at[grp],
             send_sem=total_send.at[target],
             recv_sem=total_recv.at[grp],
-            device_id=(section, target, dev),
+            device_id=(section, target, dy, dz),
             device_id_type=pl.DeviceIdType.MESH,
         )
 
@@ -209,7 +210,7 @@
             dst_ref=totals.at[source],
             send_sem=total_send.at[source],
             recv_sem=total_recv.at[source],
-            device_id=(section, source, dev),
+            device_id=(section, source, dy, dz),
             device_id_type=pl.DeviceIdType.MESH,
         ).wait_recv()
         total_copy(step).wait_send()
@@ -222,9 +223,9 @@
 
 
 def reduce_owned(payload):
-    sizes = (lax.axis_size("section"), lax.axis_size("grp"), lax.axis_size("dev"))
-    n_section, n_grp, n_dev = sizes
-    peers = n_section * n_dev
+    sizes = (lax.axis_size("section"), lax.axis_size("grp"), lax.axis_size("dy"), lax.axis_size("dz"))
+    n_section, n_grp, n_dy, n_dz = sizes
+    peers = n_section * n_dy * n_dz
     rows, one, width = payload.shape
     owned_width = width - 128
     return pl.pallas_call(
@@ -314,14 +315,20 @@
 
 
 def solution(mesh):
+    section_count, grp_count, dev_count = mesh.devices.shape
+    dz_count = 8 if dev_count % 8 == 0 else dev_count
+    split_mesh = jax.sharding.Mesh(
+        mesh.devices.reshape(section_count, grp_count, dev_count // dz_count, dz_count),
+        ("section", "grp", "dy", "dz"),
+    )
     placed = (
-        P("grp", "dev", "section", None),
-        P("dev", None),
-        P("section", "grp", "dev"),
-        P("section", "grp", "dev"),
-        P("section", "grp", "dev"),
+        P("grp", DEV, "section", None),
+        P(DEV, None),
+        P("section", "grp", DEV),
+        P("section", "grp", DEV),
+        P("section", "grp", DEV),
         P(),
     )
     return jax.shard_map(
-        on_device, mesh=mesh, in_specs=placed, out_specs=P("grp", "dev"), check_vma=False
-    )
+        on_device, mesh=split_mesh, in_specs=placed, out_specs=P("grp", DEV), check_vma=False
+    )

time: 171 us -> 153 us (0.89)
  waiting for transfers between devices: 53.6 us -> 16.4 us
  blocking collectives: 0 us -> 33.4 us
  other arithmetic: 35.3 us -> 18.4 us
  Pallas kernels: 31 us -> 32.9 us
  starting transfers between devices: 11.9 us -> 13.7 us
    all_gather x0 -> x1, blocking collectives: none -> 33.4 us  [on_device(): my_rows = lax.all_gather(my_half, 'dz', axis=0, tiled=True)]
    all_gather x1, waiting for transfers between devices: 47.4 us -> 16.4 us  [on_device(): my_rows = lax.all_gather(my_rows, 'dy', axis=0, tiled=True)]
    concatenate x1 -> x0, other arithmetic: 16.2 us -> none  [on_device(): jnp.concatenate([smoothed, partner], axis=2)]
    ppermute x1, starting transfers between devices: 1.68 us -> 7.35 us  [on_device(): lax.ppermute(smoothed, 'section', [(i, (i + 1) % section_count) for i in...]
    ppermute x1, waiting for transfers between devices: 4.47 us -> 0.01 us  [extended(): lax.ppermute(head, axis, [((i + 1) % count, i) for i in range(ends)])]
    ppermute x1, starting transfers between devices: 4.56 us -> 0.68 us  [on_device(): lax.ppermute(my_rows, 'section', [(i, (i + 1) % section_count) for i in r...]
    unnamed x11 -> x8, local copies, waits for them, and re-layouts: 2.11 us -> 4.13 us
    ppermute x1, waiting for transfers between devices: 1.72 us -> 0.01 us  [extended(): lax.ppermute(tail, axis, [(i, (i + 1) % count) for i in range(ends)])]
  transfers between devices with their start and end apart: 5 -> 5, of which waited for: 3 -> 1; matrix products, arithmetic and copies ran while one was open for 28% -> 19% of each run, Pallas kernels for 0% -> 0%
where the time goes in v4:
time: 153 us
  blocking collectives  33.4 us (22%)
  Pallas kernels  32.9 us (22%)
  other arithmetic  18.4 us (12%)
  waiting for transfers between devices  16.4 us (11%)
  between operations  14.2 us (9%)
  starting transfers between devices  13.7 us (9%)
  local copies, waits for them, and re-layouts  12.6 us (8%)
  matrix products  11.3 us (7%)
    all_gather x1, blocking collectives, on_device(): my_rows = lax.all_gather(my_half, 'dz', axis=0, tiled=True)  33.4 us
    pallas_call x1, Pallas kernels, reduce_owned(): pl.pallas_call(functools.partial(reduce_kernel, sizes), out_shape=jax.Sha...  26.1 us
    all_gather x1, waiting for transfers between devices, on_device(): my_rows = lax.all_gather(my_rows, 'dy', axis=0, tiled=True)  16.4 us
    dot_general x1, matrix products, on_device(): jnp.einsum('smn,fnc->sfmc', kernels, gathered[0], preferred_element_type=...  11.3 us
    ppermute x1, starting transfers between devices, on_device(): lax.ppermute(smoothed, 'section', [(i, (i + 1) % section_count) for i in...  7.35 us
    pallas_call x1, Pallas kernels, score_pairs(): pl.pallas_call(score_kernel, grid_spec=grid_spec, out_shape=jax.ShapeDtyp...  6.83 us
    gather x1, local copies, waits for them, and re-layouts, on_device(): positions = owner_order[precursors]  6.15 us
    scatter-add x1, other arithmetic, on_device(): jnp.zeros((PREC,), jnp.float32).at[positions.reshape(-1)]  6.1 us
  transfers between devices with their start and end apart: 5, of which 1 were waited for; matrix products, arithmetic and copies ran while one was open for 19% of the time, Pallas kernels for 0%

profile of v4, /device:TPU:1, one launch (start us, length us, event | category | flops | bytes accessed | tf_op | source)
XLA Modules:
  0.0 153.0 jit_solution(8438044927536822989)
XLA Ops:
  6.5 2.9 %copy.11 = bf16[1,16,256,256]{2,3,1,0:T(8,128)(2,1)S(1)} copy(bf16[1,16,256,256]{3,2,1,0:T(8,128)(2,1)} %param.6) | data formatting | bytes 4194304 | tf_op args[0]
  9.4 1.1 fusion.65
  10.5 4.4 %collective-permute-start = (bf16[1,4,256,256]{2,3,1,0:T(8,128)(2,1)}, bf16[1,4,256,256]{2,3,1,0:T(8,128)(2,1)S(1)}, u32[]{:S(2)}, u32[]{:S(2)}) collective-permute-start(bf16[1,4,256,256]{2,3,1,0:T(8,128)(2,1)} %get-tuple-element.5), channel_id=1, source_target_pairs={{0,1},{1,2},{2,3},{3,4},{4,5},{5,6},{6,7},{7,8},{8,9},{9,10},{10,1... | collective-permute-start | bytes 1572872 | tf_op jit(solution)/shard_map/ppermute | solution.py:31
  14.9 1.3 collective-permute-start.1
  16.2 33.4 %all_gather.6 = bf16[1024,256]{1,0:T(8,128)(2,1)} all-gather(bf16[128,256]{1,0:T(8,128)(2,1)S(1)} %constant_dynamic-slice_fusion), channel_id=1, replica_groups=mesh['section'=2,'grp'=4,'dy'=4,'dz'=8] {'dz'}, dimensions={0}, use_global_device_ids=true | all-gather | bytes 589824 | tf_op jit(solution)/shard_map/all_gather | solution.py:87
  49.7 0.5 maximum_convert_fusion
  50.2 4.7 %fusion.1 = bf16[1,16,256,256]{2,3,1,0:T(8,128)(2,1)S(1)} fusion(f32[1,24,256,256]{2,3,1,0:T(8,128)S(1)} %maximum_convert_fusion), kind=kLoop, calls=%fused_computation.5 | loop fusion | flops 18874368 | bytes 39845888 | tf_op jit(solution)/shard_map/convert_element_type | solution.py:75
  54.9 7.3 %collective-permute-start.2 = (bf16[1,16,256,256]{2,3,1,0:T(8,128)(2,1)S(1)}, bf16[1,16,256,256]{2,3,1,0:T(8,128)(2,1)}, u32[]{:S(2)}, u32[]{:S(2)}) collective-permute-start(bf16[1,16,256,256]{2,3,1,0:T(8,128)(2,1)S(1)} %fusion.1), channel_id=1, source_target_pairs={{0,128},{128,0},{1,129},{129,1},{2,130},{130,2},{3,131},{131,3},{4... | collective-permute-start | bytes 6291464 | tf_op jit(solution)/shard_map/ppermute | solution.py:77
  62.4 6.1 %gather_fusion = s32[1024]{0:T(1024)S(1)} fusion(s32[8192]{0:T(1024)S(1)} %copy-done.1, s32[1024]{0:T(1024)S(1)} %fusion.61), kind=kCustom, calls=%fused_computation | custom fusion | bytes 12288 | tf_op jit(solution)/shard_map/gather | solution.py:100
  68.5 0.9 fusion.57
  69.5 0.9 fusion.52
  70.4 1.0 fusion.53
  71.4 1.0 fusion.54
  72.4 0.9 fusion.55
  73.3 16.4 %all-gather.2.cloned.1.call-done.mine_ref = bf16[4096,256]{1,0:T(8,128)(2,1)} async-done(((bf16[1024,256]{1,0:T(8,128)(2,1)}), bf16[4096,256]{1,0:T(8,128)(2,1)}) %all-gather.2.cloned.1.call-update) | async-done | bytes 2097168 | tf_op jit(solution)/shard_map/all_gather | solution.py:88
  89.7 0.7 collective-permute-start.3
  91.1 0.9 fusion.56
  92.0 11.3 %convert_bitcast_fusion.wave_ref = bf16[6,16,256,256]{3,2,1,0:T(8,128)(2,1)} fusion(bf16[1,16,256,256]{2,3,1,0:T(8,128)(2,1)} %collective-permute-done.2, bf16[1,16,256,256]{2,3,1,0:T(8,128)(2,1)S(1)} %fusion.1, bf16[6,256,512]{2,1,0:T(8,128)(2,1)} %fusion.56), kind=kOutput, calls=%fused_computation.2 | convolution fusion | flops 6457131008 | bytes 18350080 | tf_op jit(solution)/shard_map/smn,fnc->sfmc/dot_general | solution.py:82
  103.3 6.8 %shard_map.64 = f32[8,1,128]{2,1,0:T(1,128)} custom-call(s32[8]{0:T(128)} %bitcast.30, s32[8]{0:T(128)} %bitcast.29, s32[1]{0:T(128)} %bitcast.24.count_ref, s32[1]{0:T(128)} %bitcast.6.section_ref, bf16[6,16,256,256]{3,2,1,0:T(8,128)(2,1)} %convert_bitcast_fusion.wave_ref, bf16[4096,256]{1,0:T(8,128)(2,1)} %all-gather.2.cloned.1.call-done.mine_ref, ...), custom_call_target="tpu_custom_call" | custom-call | tf_op jit(solution)/shard_map/pallas_call | solution.py:301
  110.1 1.3 reduce_sum.9
  111.4 6.1 %scatter_custom_fusion = f32[8192]{0:T(1024)S(1)} fusion(s32[1024]{0:T(1024)S(1)} %bitcast.28, f32[1024]{0:T(1024)} %bitcast.26, f32[]{:T(128)} %constant.32.clone.1), kind=kCustom, calls=%fused_computation.86 | custom fusion | flops 1024 | bytes 33280 | tf_op jit(solution)/shard_map/scatter-add | solution.py:101
  117.5 1.3 concatenate.19.payload_ref
  118.8 26.1 %shard_map.65 = f32[1,256]{1,0:T(1,128)} custom-call(f32[32,1,384]{2,1,0:T(1,128)} %concatenate.19.payload_ref), custom_call_target="tpu_custom_call" | custom-call | tf_op jit(solution)/shard_map/pallas_call | solution.py:231
  144.9 1.2 copy.24
  (18 shorter events, 0.2 us)
Async XLA Ops:
  6.5 9.7 %copy-start = (bf16[256,256]{1,0:T(8,128)(2,1)S(1)}, bf16[256,256]{1,0:T(8,128)(2,1)}, u32[]{:S(2)}) copy-start(bf16[256,256]{1,0:T(8,128)(2,1)} %param.7) | copy-start | bytes 393220
  6.5 83.2 %all-gather.2.cloned.1.call-start = ((), (), s32[]{:S(2)}) async-start(), calls=%async_computation | async-start | bytes 2621440 | tf_op jit(solution)/shard_map/all_gather | solution.py:88
  10.5 39.1 %collective-permute-start = (bf16[1,4,256,256]{2,3,1,0:T(8,128)(2,1)}, bf16[1,4,256,256]{2,3,1,0:T(8,128)(2,1)S(1)}, u32[]{:S(2)}, u32[]{:S(2)}) collective-permute-start(bf16[1,4,256,256]{2,3,1,0:T(8,128)(2,1)} %get-tuple-element.5), channel_id=1, source_target_pairs={{0,1},{1,2},{2,3},{3,4},{4,5},{5,6},{6,7},{7,8},{8,9},{9,10},{10,1... | collective-permute-start | bytes 1572872 | tf_op jit(solution)/shard_map/ppermute | solution.py:31
  14.9 34.8 %collective-permute-start.1 = (bf16[1,4,256,256]{2,3,1,0:T(8,128)(2,1)}, bf16[1,4,256,256]{2,3,1,0:T(8,128)(2,1)S(1)}, u32[]{:S(2)}, u32[]{:S(2)}) collective-permute-start(bf16[1,4,256,256]{2,3,1,0:T(8,128)(2,1)} %get-tuple-element.6), channel_id=1, source_target_pairs={{1,0},{2,1},{3,2},{4,3},{5,4},{6,5},{7,6},{8,7},{9,8},{10,9},{11,1... | collective-permute-start | bytes 1572872 | tf_op jit(solution)/shard_map/ppermute | solution.py:33
  50.1 12.1 %copy-start.2 = (s32[1,1,8]{2,1,0:T(1,128)S(1)}, s32[1,1,8]{2,1,0:T(1,128)}, u32[]{:S(2)}) copy-start(s32[1,1,8]{2,1,0:T(1,128)} %param.8) | copy-start | bytes 100
  50.2 12.2 %copy-start.1 = (s32[8192]{0:T(1024)S(1)}, s32[8192]{0:T(1024)}, u32[]{:S(2)}) copy-start(s32[8192]{0:T(1024)} %param.11) | copy-start | bytes 98308
  54.9 37.1 %collective-permute-start.2 = (bf16[1,16,256,256]{2,3,1,0:T(8,128)(2,1)S(1)}, bf16[1,16,256,256]{2,3,1,0:T(8,128)(2,1)}, u32[]{:S(2)}, u32[]{:S(2)}) collective-permute-start(bf16[1,16,256,256]{2,3,1,0:T(8,128)(2,1)S(1)} %fusion.1), channel_id=1, source_target_pairs={{0,128},{128,0},{1,129},{129,1},{2,130},{130,2},{3,131},{131,3},{4... | collective-permute-start | bytes 6291464 | tf_op jit(solution)/shard_map/ppermute | solution.py:77
  89.7 13.6 %collective-permute-start.3 = (bf16[4096,256]{1,0:T(8,128)(2,1)}, bf16[4096,256]{1,0:T(8,128)(2,1)}, u32[]{:S(2)}, u32[]{:S(2)}) collective-permute-start(bf16[4096,256]{1,0:T(8,128)(2,1)} %all-gather.2.cloned.1.call-done.mine_ref), channel_id=1, source_target_pairs={{0,128},{128,0},{1,129},{129,1},{2,130},{130,2},{3,131},{131,3},{4... | collective-permute-start | bytes 6291464 | tf_op jit(solution)/shard_map/ppermute | solution.py:89
Sparse Core Ops, SparseCore 0:
  49.8 39.9 all-gather.1

commit v5 on v4

--- a/solution.py
+++ b/solution.py
@@ -84,8 +84,7 @@
     ).astype(jnp.bfloat16)
     half_rows = templates.shape[0] // 2
     my_half = lax.dynamic_slice_in_dim(templates, section_index * half_rows, half_rows, 0)
-    my_rows = lax.all_gather(my_half, "dz", axis=0, tiled=True)
-    my_rows = lax.all_gather(my_rows, "dy", axis=0, tiled=True)
+    my_rows = gather_rows(my_half)
     other_rows = lax.ppermute(
         my_rows, "section", [(i, (i + 1) % section_count) for i in range(section_count)]
     )
@@ -245,6 +244,93 @@
     )(payload)
 
 
+def gather_kernel(sizes, half_ref, out_ref, own_sem, z_send, z_recv, y_send, y_recv):
+    n_dy, n_dz = sizes
+    section = lax.axis_index("section")
+    grp = lax.axis_index("grp")
+    dy = lax.axis_index("dy")
+    dz = lax.axis_index("dz")
+    dev = dy * n_dz + dz
+
+    barrier = pltpu.get_barrier_semaphore()
+    for step in range(1, n_dz):
+        pl.semaphore_signal(
+            barrier,
+            inc=1,
+            device_id=(section, grp, dy, (dz + step) % n_dz),
+            device_id_type=pl.DeviceIdType.MESH,
+        )
+    for step in range(1, n_dy):
+        pl.semaphore_signal(
+            barrier,
+            inc=1,
+            device_id=(section, grp, (dy + step) % n_dy, dz),
+            device_id_type=pl.DeviceIdType.MESH,
+        )
+    pl.semaphore_wait(barrier, n_dz - 1 + n_dy - 1)
+
+    own = pltpu.make_async_copy(half_ref, out_ref.at[dev], own_sem)
+    own.start()
+
+    def z_copy(target, source):
+        return pltpu.make_async_remote_copy(
+            src_ref=half_ref,
+            dst_ref=out_ref.at[dy * n_dz + source],
+            send_sem=z_send.at[target],
+            recv_sem=z_recv.at[source],
+            device_id=(section, grp, dy, target),
+            device_id_type=pl.DeviceIdType.MESH,
+        )
+
+    for step in range(1, n_dz):
+        z_copy((dz + step) % n_dz, dz).start()
+    own.wait()
+    for step in range(1, n_dz):
+        source = (dz + n_dz - step) % n_dz
+        z_copy(source, source).wait_recv()
+    for step in range(1, n_dz):
+        z_copy((dz + step) % n_dz, dz).wait_send()
+
+    def y_copy(target, source):
+        return pltpu.make_async_remote_copy(
+            src_ref=out_ref.at[pl.ds(source * n_dz, n_dz)],
+            dst_ref=out_ref.at[pl.ds(source * n_dz, n_dz)],
+            send_sem=y_send.at[target],
+            recv_sem=y_recv.at[source],
+            device_id=(section, grp, target, dz),
+            device_id_type=pl.DeviceIdType.MESH,
+        )
+
+    for step in range(1, n_dy):
+        y_copy((dy + step) % n_dy, dy).start()
+    for step in range(1, n_dy):
+        source = (dy + n_dy - step) % n_dy
+        y_copy(source, source).wait_recv()
+    for step in range(1, n_dy):
+        y_copy((dy + step) % n_dy, dy).wait_send()
+
+
+def gather_rows(half):
+    sizes = (lax.axis_size("dy"), lax.axis_size("dz"))
+    n_dy, n_dz = sizes
+    rows, channels = half.shape
+    out = pl.pallas_call(
+        functools.partial(gather_kernel, sizes),
+        out_shape=jax.ShapeDtypeStruct((n_dy * n_dz, rows, channels), half.dtype),
+        in_specs=[pl.BlockSpec(memory_space=pltpu.VMEM)],
+        out_specs=pl.BlockSpec(memory_space=pltpu.VMEM),
+        scratch_shapes=[
+            pltpu.SemaphoreType.DMA(()),
+            pltpu.SemaphoreType.DMA((n_dz,)),
+            pltpu.SemaphoreType.DMA((n_dz,)),
+            pltpu.SemaphoreType.DMA((n_dy,)),
+            pltpu.SemaphoreType.DMA((n_dy,)),
+        ],
+        compiler_params=pltpu.CompilerParams(collective_id=1, has_side_effects=True),
+    )(half)
+    return out.reshape(n_dy * n_dz * rows, channels)
+
+
 def score_kernel(tile_ref, block_ref, count_ref, section_ref, wave_ref, mine_ref, other_ref, out_ref):
     slot = pl.program_id(0)
     live = slot < count_ref[0]

time: 153 us -> 134 us (0.88)
  Pallas kernels: 32.9 us -> 86.1 us
  blocking collectives: 33.4 us -> 0 us
  waiting for transfers between devices: 16.4 us -> 0.01 us
  between operations: 14.2 us -> 0.82 us
  starting transfers between devices: 13.7 us -> 8.33 us
  other arithmetic: 18.4 us -> 14.2 us
    pallas_call x0 -> x1, Pallas kernels: none -> 52.2 us  [gather_rows(): pl.pallas_call(functools.partial(gather_kernel, sizes), out_shape=jax.Sha...]
    all_gather x1 -> x0, blocking collectives: 33.4 us -> none  [on_device(): my_rows = lax.all_gather(my_half, 'dz', axis=0, tiled=True)]
    all_gather x1 -> x0, waiting for transfers between devices: 16.4 us -> none  [on_device(): my_rows = lax.all_gather(my_rows, 'dy', axis=0, tiled=True)]
    ppermute x1, starting transfers between devices: 7.35 us -> 0.3 us  [on_device(): lax.ppermute(smoothed, 'section', [(i, (i + 1) % section_count) for i in...]
    unnamed x5, other arithmetic: 4.76 us -> 1.23 us
    ppermute x1, starting transfers between devices: 0.68 us -> 2.34 us  [on_device(): lax.ppermute(my_rows, 'section', [(i, (i + 1) % section_count) for i in r...]
  transfers between devices with their start and end apart: 5 -> 4, of which waited for: 1 -> 0; matrix products, arithmetic and copies ran while one was open for 19% -> 19% of each run, Pallas kernels for 0% -> 39%
where the time goes in v5:
time: 134 us
  Pallas kernels  86.1 us (64%)
  other arithmetic  14.2 us (11%)
  local copies, waits for them, and re-layouts  13.2 us (10%)
  matrix products  11.2 us (8%)
  starting transfers between devices  8.33 us (6%)
    pallas_call x1, Pallas kernels, gather_rows(): pl.pallas_call(functools.partial(gather_kernel, sizes), out_shape=jax.Sha...  52.2 us
    pallas_call x1, Pallas kernels, reduce_owned(): pl.pallas_call(functools.partial(reduce_kernel, sizes), out_shape=jax.Sha...  27 us
    dot_general x1, matrix products, on_device(): jnp.einsum('smn,fnc->sfmc', kernels, gathered[0], preferred_element_type=...  11.2 us
    pallas_call x1, Pallas kernels, score_pairs(): pl.pallas_call(score_kernel, grid_spec=grid_spec, out_shape=jax.ShapeDtyp...  6.91 us
    gather x1, local copies, waits for them, and re-layouts, on_device(): positions = owner_order[precursors]  6.15 us
    scatter-add x1, other arithmetic, on_device(): jnp.zeros((PREC,), jnp.float32).at[positions.reshape(-1)]  6.1 us
    convert_element_type x1, other arithmetic, on_device(): smoothed = smoothed.astype(jnp.bfloat16)  4.75 us
    ppermute x1, starting transfers between devices, extended(): lax.ppermute(tail, axis, [(i, (i + 1) % count) for i in range(ends)])  4.39 us
  transfers between devices with their start and end apart: 4, of which 0 were waited for; matrix products, arithmetic and copies ran while one was open for 19% of the time, Pallas kernels for 39%

profile of v5, /device:TPU:1, one launch (start us, length us, event | category | flops | bytes accessed | tf_op | source)
XLA Modules:
  0.0 134.0 jit_solution(6634952672063980775)
XLA Ops:
  0.0 2.9 %copy.11 = bf16[1,16,256,256]{2,3,1,0:T(8,128)(2,1)S(1)} copy(bf16[1,16,256,256]{3,2,1,0:T(8,128)(2,1)} %param.6) | data formatting | bytes 4194304 | tf_op args[0]
  2.9 1.0 fusion.65
  3.9 4.4 %collective-permute-start = (bf16[1,4,256,256]{2,3,1,0:T(8,128)(2,1)}, bf16[1,4,256,256]{2,3,1,0:T(8,128)(2,1)S(1)}, u32[]{:S(2)}, u32[]{:S(2)}) collective-permute-start(bf16[1,4,256,256]{2,3,1,0:T(8,128)(2,1)} %get-tuple-element.5), channel_id=1, source_target_pairs={{0,1},{1,2},{2,3},{3,4},{4,5},{5,6},{6,7},{7,8},{8,9},{9,10},{10,1... | collective-permute-start | bytes 1572872 | tf_op jit(solution)/shard_map/ppermute | solution.py:31
  8.3 1.3 collective-permute-start.1
  9.6 0.6 constant_dynamic-slice_fusion.half_ref
  10.3 52.2 %shard_map.64 = bf16[32,128,256]{2,1,0:T(8,128)(2,1)} custom-call(bf16[128,256]{1,0:T(8,128)(2,1)} %constant_dynamic-slice_fusion.half_ref), custom_call_target="tpu_custom_call" | custom-call | tf_op jit(solution)/shard_map/pallas_call | solution.py:317
  62.5 2.3 %collective-permute-start.3 = (bf16[4096,256]{1,0:T(8,128)(2,1)}, bf16[4096,256]{1,0:T(8,128)(2,1)}, u32[]{:S(2)}, u32[]{:S(2)}) collective-permute-start(bf16[4096,256]{1,0:T(8,128)(2,1)} %bitcast.26), channel_id=1, source_target_pairs={{0,128},{128,0},{1,129},{129,1},{2,130},{130,2},{3,131},{131,3},{4... | collective-permute-start | bytes 6291464 | tf_op jit(solution)/shard_map/ppermute | solution.py:88
  64.9 0.5 maximum_convert_fusion
  65.4 4.7 %fusion.1 = bf16[1,16,256,256]{2,3,1,0:T(8,128)(2,1)S(1)} fusion(f32[1,24,256,256]{2,3,1,0:T(8,128)S(1)} %maximum_convert_fusion), kind=kLoop, calls=%fused_computation.5 | loop fusion | flops 18874368 | bytes 39845888 | tf_op jit(solution)/shard_map/convert_element_type | solution.py:75
  70.1 0.3 collective-permute-start.2
  70.5 6.1 %gather_fusion = s32[1024]{0:T(1024)S(1)} fusion(s32[8192]{0:T(1024)S(1)} %copy-done.1, s32[1024]{0:T(1024)S(1)} %fusion.61), kind=kCustom, calls=%fused_computation | custom fusion | bytes 12288 | tf_op jit(solution)/shard_map/gather | solution.py:99
  76.7 0.2 fusion.57
  76.9 0.3 fusion.52
  77.2 0.3 fusion.53
  77.5 0.3 fusion.54
  77.7 0.3 fusion.55
  78.6 0.3 fusion.56
  78.9 11.2 %convert_bitcast_fusion.wave_ref = bf16[6,16,256,256]{3,2,1,0:T(8,128)(2,1)} fusion(bf16[1,16,256,256]{2,3,1,0:T(8,128)(2,1)} %collective-permute-done.2, bf16[1,16,256,256]{2,3,1,0:T(8,128)(2,1)S(1)} %fusion.1, bf16[6,256,512]{2,1,0:T(8,128)(2,1)S(1)} %fusion.56), kind=kOutput, calls=%fused_computation.2 | convolution fusion | flops 6457131008 | bytes 18350080 | tf_op jit(solution)/shard_map/smn,fnc->sfmc/dot_general | solution.py:82
  90.2 6.9 %shard_map.65 = f32[8,1,128]{2,1,0:T(1,128)} custom-call(s32[8]{0:T(128)} %bitcast.33, s32[8]{0:T(128)} %bitcast.32, s32[1]{0:T(128)} %bitcast.25.count_ref, s32[1]{0:T(128)} %bitcast.6.section_ref, bf16[6,16,256,256]{3,2,1,0:T(8,128)(2,1)} %convert_bitcast_fusion.wave_ref, bf16[4096,256]{1,0:T(8,128)(2,1)} %bitcast.27, ...), custom_call_target="tpu_custom_call" | custom-call | tf_op jit(solution)/shard_map/pallas_call | solution.py:387
  97.1 1.3 reduce_sum.9
  98.3 6.1 %scatter_custom_fusion = f32[8192]{0:T(1024)S(1)} fusion(s32[1024]{0:T(1024)S(1)} %bitcast.31, f32[1024]{0:T(1024)} %bitcast.29, f32[]{:T(128)} %constant.32.clone.1), kind=kCustom, calls=%fused_computation.86 | custom fusion | flops 1024 | bytes 33280 | tf_op jit(solution)/shard_map/scatter-add | solution.py:100
  104.5 1.3 concatenate.19.payload_ref
  105.7 27.0 %shard_map.66 = f32[1,256]{1,0:T(1,128)} custom-call(f32[32,1,384]{2,1,0:T(1,128)} %concatenate.19.payload_ref), custom_call_target="tpu_custom_call" | custom-call | tf_op jit(solution)/shard_map/pallas_call | solution.py:230
  132.8 1.2 copy.24
  (15 shorter events, 0.1 us)
Async XLA Ops:
  0.0 9.6 %copy-start = (bf16[256,256]{1,0:T(8,128)(2,1)S(1)}, bf16[256,256]{1,0:T(8,128)(2,1)}, u32[]{:S(2)}) copy-start(bf16[256,256]{1,0:T(8,128)(2,1)} %param.7) | copy-start | bytes 393220
  3.9 60.9 %collective-permute-start = (bf16[1,4,256,256]{2,3,1,0:T(8,128)(2,1)}, bf16[1,4,256,256]{2,3,1,0:T(8,128)(2,1)S(1)}, u32[]{:S(2)}, u32[]{:S(2)}) collective-permute-start(bf16[1,4,256,256]{2,3,1,0:T(8,128)(2,1)} %get-tuple-element.5), channel_id=1, source_target_pairs={{0,1},{1,2},{2,3},{3,4},{4,5},{5,6},{6,7},{7,8},{8,9},{9,10},{10,1... | collective-permute-start | bytes 1572872 | tf_op jit(solution)/shard_map/ppermute | solution.py:31
  8.3 56.5 %collective-permute-start.1 = (bf16[1,4,256,256]{2,3,1,0:T(8,128)(2,1)}, bf16[1,4,256,256]{2,3,1,0:T(8,128)(2,1)S(1)}, u32[]{:S(2)}, u32[]{:S(2)}) collective-permute-start(bf16[1,4,256,256]{2,3,1,0:T(8,128)(2,1)} %get-tuple-element.6), channel_id=1, source_target_pairs={{1,0},{2,1},{3,2},{4,3},{5,4},{6,5},{7,6},{8,7},{9,8},{10,9},{11,1... | collective-permute-start | bytes 1572872 | tf_op jit(solution)/shard_map/ppermute | solution.py:33
  62.5 27.6 %collective-permute-start.3 = (bf16[4096,256]{1,0:T(8,128)(2,1)}, bf16[4096,256]{1,0:T(8,128)(2,1)}, u32[]{:S(2)}, u32[]{:S(2)}) collective-permute-start(bf16[4096,256]{1,0:T(8,128)(2,1)} %bitcast.26), channel_id=1, source_target_pairs={{0,128},{128,0},{1,129},{129,1},{2,130},{130,2},{3,131},{131,3},{4... | collective-permute-start | bytes 6291464 | tf_op jit(solution)/shard_map/ppermute | solution.py:88
  65.3 5.1 %copy-start.2 = (s32[1,1,8]{2,1,0:T(1,128)S(1)}, s32[1,1,8]{2,1,0:T(1,128)}, u32[]{:S(2)}) copy-start(s32[1,1,8]{2,1,0:T(1,128)} %param.8) | copy-start | bytes 100
  65.4 5.2 %copy-start.1 = (s32[8192]{0:T(1024)S(1)}, s32[8192]{0:T(1024)}, u32[]{:S(2)}) copy-start(s32[8192]{0:T(1024)} %param.11) | copy-start | bytes 98308
  70.1 8.8 %collective-permute-start.2 = (bf16[1,16,256,256]{2,3,1,0:T(8,128)(2,1)S(1)}, bf16[1,16,256,256]{2,3,1,0:T(8,128)(2,1)}, u32[]{:S(2)}, u32[]{:S(2)}) collective-permute-start(bf16[1,16,256,256]{2,3,1,0:T(8,128)(2,1)S(1)} %fusion.1), channel_id=1, source_target_pairs={{0,128},{128,0},{1,129},{129,1},{2,130},{130,2},{3,131},{131,3},{4... | collective-permute-start | bytes 6291464 | tf_op jit(solution)/shard_map/ppermute | solution.py:77

commit v6 on v4

--- a/solution.py
+++ b/solution.py
@@ -84,8 +84,7 @@
     ).astype(jnp.bfloat16)
     half_rows = templates.shape[0] // 2
     my_half = lax.dynamic_slice_in_dim(templates, section_index * half_rows, half_rows, 0)
-    my_rows = lax.all_gather(my_half, "dz", axis=0, tiled=True)
-    my_rows = lax.all_gather(my_rows, "dy", axis=0, tiled=True)
+    my_rows = gather_rows(my_half)
     other_rows = lax.ppermute(
         my_rows, "section", [(i, (i + 1) % section_count) for i in range(section_count)]
     )
@@ -245,6 +244,68 @@
     )(payload)
 
 
+def gather_kernel(sizes, half_ref, out_ref, own_sem, send_sems, recv_sems):
+    n_dy, n_dz = sizes
+    n_dev = n_dy * n_dz
+    section = lax.axis_index("section")
+    grp = lax.axis_index("grp")
+    dev = lax.axis_index("dy") * n_dz + lax.axis_index("dz")
+
+    def peer(index):
+        return (section, grp, index // n_dz, index % n_dz)
+
+    barrier = pltpu.get_barrier_semaphore()
+    for step in range(1, n_dev):
+        pl.semaphore_signal(
+            barrier,
+            inc=1,
+            device_id=peer((dev + step) % n_dev),
+            device_id_type=pl.DeviceIdType.MESH,
+        )
+    pl.semaphore_wait(barrier, n_dev - 1)
+
+    own = pltpu.make_async_copy(half_ref, out_ref.at[dev], own_sem)
+    own.start()
+
+    def row_copy(target, source):
+        return pltpu.make_async_remote_copy(
+            src_ref=half_ref,
+            dst_ref=out_ref.at[source],
+            send_sem=send_sems.at[target],
+            recv_sem=recv_sems.at[source],
+            device_id=peer(target),
+            device_id_type=pl.DeviceIdType.MESH,
+        )
+
+    for step in range(1, n_dev):
+        row_copy((dev + step) % n_dev, dev).start()
+    own.wait()
+    for step in range(1, n_dev):
+        source = (dev + n_dev - step) % n_dev
+        row_copy(source, source).wait_recv()
+    for step in range(1, n_dev):
+        row_copy((dev + step) % n_dev, dev).wait_send()
+
+
+def gather_rows(half):
+    sizes = (lax.axis_size("dy"), lax.axis_size("dz"))
+    n_dy, n_dz = sizes
+    rows, channels = half.shape
+    out = pl.pallas_call(
+        functools.partial(gather_kernel, sizes),
+        out_shape=jax.ShapeDtypeStruct((n_dy * n_dz, rows, channels), half.dtype),
+        in_specs=[pl.BlockSpec(memory_space=pltpu.VMEM)],
+        out_specs=pl.BlockSpec(memory_space=pltpu.VMEM),
+        scratch_shapes=[
+            pltpu.SemaphoreType.DMA(()),
+            pltpu.SemaphoreType.DMA((n_dy * n_dz,)),
+            pltpu.SemaphoreType.DMA((n_dy * n_dz,)),
+        ],
+        compiler_params=pltpu.CompilerParams(collective_id=1, has_side_effects=True),
+    )(half)
+    return out.reshape(n_dy * n_dz * rows, channels)
+
+
 def score_kernel(tile_ref, block_ref, count_ref, section_ref, wave_ref, mine_ref, other_ref, out_ref):
     slot = pl.program_id(0)
     live = slot < count_ref[0]

time: 153 us -> 145 us (0.948)
  Pallas kernels: 32.9 us -> 97.5 us
  blocking collectives: 33.4 us -> 0 us
  waiting for transfers between devices: 16.4 us -> 0.01 us
  between operations: 14.2 us -> 0.82 us
  starting transfers between devices: 13.7 us -> 7.2 us
  other arithmetic: 18.4 us -> 14.2 us
    pallas_call x0 -> x1, Pallas kernels: none -> 60.5 us  [gather_rows(): pl.pallas_call(functools.partial(gather_kernel, sizes), out_shape=jax.Sha...]
    all_gather x1 -> x0, blocking collectives: 33.4 us -> none  [on_device(): my_rows = lax.all_gather(my_half, 'dz', axis=0, tiled=True)]
    all_gather x1 -> x0, waiting for transfers between devices: 16.4 us -> none  [on_device(): my_rows = lax.all_gather(my_rows, 'dy', axis=0, tiled=True)]
    pallas_call x1, Pallas kernels: 6.83 us -> 14.5 us  [score_pairs(): pl.pallas_call(score_kernel, grid_spec=grid_spec, out_shape=jax.ShapeDtyp...]
    ppermute x1, starting transfers between devices: 7.35 us -> 0.3 us  [on_device(): lax.ppermute(smoothed, 'section', [(i, (i + 1) % section_count) for i in...]
    pallas_call x1, Pallas kernels: 26.1 us -> 22.5 us  [reduce_owned(): pl.pallas_call(functools.partial(reduce_kernel, sizes), out_shape=jax.Sha...]
    unnamed x5, other arithmetic: 4.76 us -> 1.23 us
  transfers between devices with their start and end apart: 5 -> 4, of which waited for: 1 -> 0; matrix products, arithmetic and copies ran while one was open for 19% -> 17% of each run, Pallas kernels for 0% -> 42%
where the time goes in v6:
time: 145 us; the launch traced here: 144 us
  Pallas kernels  97.5 us (67%)
  other arithmetic  14.2 us (10%)
  local copies, waits for them, and re-layouts  13.2 us (9%)
  matrix products  11.2 us (8%)
  starting transfers between devices  7.2 us (5%)
    pallas_call x1, Pallas kernels, gather_rows(): pl.pallas_call(functools.partial(gather_kernel, sizes), out_shape=jax.Sha...  60.5 us
    pallas_call x1, Pallas kernels, reduce_owned(): pl.pallas_call(functools.partial(reduce_kernel, sizes), out_shape=jax.Sha...  22.5 us
    pallas_call x1, Pallas kernels, score_pairs(): pl.pallas_call(score_kernel, grid_spec=grid_spec, out_shape=jax.ShapeDtyp...  14.5 us
    dot_general x1, matrix products, on_device(): jnp.einsum('smn,fnc->sfmc', kernels, gathered[0], preferred_element_type=...  11.2 us
    gather x1, local copies, waits for them, and re-layouts, on_device(): positions = owner_order[precursors]  6.15 us
    scatter-add x1, other arithmetic, on_device(): jnp.zeros((PREC,), jnp.float32).at[positions.reshape(-1)]  6.1 us
    convert_element_type x1, other arithmetic, on_device(): smoothed = smoothed.astype(jnp.bfloat16)  4.75 us
    ppermute x1, starting transfers between devices, extended(): lax.ppermute(tail, axis, [(i, (i + 1) % count) for i in range(ends)])  4.39 us
  transfers between devices with their start and end apart: 4, of which 0 were waited for; matrix products, arithmetic and copies ran while one was open for 17% of the time, Pallas kernels for 42%

profile of v6, /device:TPU:1, one launch (start us, length us, event | category | flops | bytes accessed | tf_op | source)
XLA Modules:
  0.0 144.2 jit_solution(5248722873114626120)
XLA Ops:
  0.0 2.9 %copy.11 = bf16[1,16,256,256]{2,3,1,0:T(8,128)(2,1)S(1)} copy(bf16[1,16,256,256]{3,2,1,0:T(8,128)(2,1)} %param.6) | data formatting | bytes 4194304 | tf_op args[0]
  2.9 1.0 fusion.65
  3.9 4.4 %collective-permute-start = (bf16[1,4,256,256]{2,3,1,0:T(8,128)(2,1)}, bf16[1,4,256,256]{2,3,1,0:T(8,128)(2,1)S(1)}, u32[]{:S(2)}, u32[]{:S(2)}) collective-permute-start(bf16[1,4,256,256]{2,3,1,0:T(8,128)(2,1)} %get-tuple-element.5), channel_id=1, source_target_pairs={{0,1},{1,2},{2,3},{3,4},{4,5},{5,6},{6,7},{7,8},{8,9},{9,10},{10,1... | collective-permute-start | bytes 1572872 | tf_op jit(solution)/shard_map/ppermute | solution.py:31
  8.3 1.3 collective-permute-start.1
  9.6 0.6 constant_dynamic-slice_fusion.half_ref
  10.3 60.5 %shard_map.64 = bf16[32,128,256]{2,1,0:T(8,128)(2,1)} custom-call(bf16[128,256]{1,0:T(8,128)(2,1)} %constant_dynamic-slice_fusion.half_ref), custom_call_target="tpu_custom_call" | custom-call | tf_op jit(solution)/shard_map/pallas_call | solution.py:294
  70.8 1.2 collective-permute-start.3
  72.0 0.5 maximum_convert_fusion
  72.5 4.7 %fusion.1 = bf16[1,16,256,256]{2,3,1,0:T(8,128)(2,1)S(1)} fusion(f32[1,24,256,256]{2,3,1,0:T(8,128)S(1)} %maximum_convert_fusion), kind=kLoop, calls=%fused_computation.5 | loop fusion | flops 18874368 | bytes 39845888 | tf_op jit(solution)/shard_map/convert_element_type | solution.py:75
  77.2 0.3 collective-permute-start.2
  77.6 6.1 %gather_fusion = s32[1024]{0:T(1024)S(1)} fusion(s32[8192]{0:T(1024)S(1)} %copy-done.1, s32[1024]{0:T(1024)S(1)} %fusion.61), kind=kCustom, calls=%fused_computation | custom fusion | bytes 12288 | tf_op jit(solution)/shard_map/gather | solution.py:99
  83.8 0.2 fusion.57
  84.0 0.3 fusion.52
  84.3 0.3 fusion.53
  84.6 0.3 fusion.54
  84.8 0.3 fusion.55
  85.7 0.3 fusion.56
  86.0 11.2 %convert_bitcast_fusion.wave_ref = bf16[6,16,256,256]{3,2,1,0:T(8,128)(2,1)} fusion(bf16[1,16,256,256]{2,3,1,0:T(8,128)(2,1)} %collective-permute-done.2, bf16[1,16,256,256]{2,3,1,0:T(8,128)(2,1)S(1)} %fusion.1, bf16[6,256,512]{2,1,0:T(8,128)(2,1)S(1)} %fusion.56), kind=kOutput, calls=%fused_computation.2 | convolution fusion | flops 6457131008 | bytes 18350080 | tf_op jit(solution)/shard_map/smn,fnc->sfmc/dot_general | solution.py:82
  97.2 14.5 %shard_map.65 = f32[8,1,128]{2,1,0:T(1,128)} custom-call(s32[8]{0:T(128)} %bitcast.33, s32[8]{0:T(128)} %bitcast.32, s32[1]{0:T(128)} %bitcast.25.count_ref, s32[1]{0:T(128)} %bitcast.6.section_ref, bf16[6,16,256,256]{3,2,1,0:T(8,128)(2,1)} %convert_bitcast_fusion.wave_ref, bf16[4096,256]{1,0:T(8,128)(2,1)} %bitcast.27, ...), custom_call_target="tpu_custom_call" | custom-call | tf_op jit(solution)/shard_map/pallas_call | solution.py:362
  111.7 1.3 reduce_sum.9
  113.0 6.1 %scatter_custom_fusion = f32[8192]{0:T(1024)S(1)} fusion(s32[1024]{0:T(1024)S(1)} %bitcast.31, f32[1024]{0:T(1024)} %bitcast.29, f32[]{:T(128)} %constant.32.clone.1), kind=kCustom, calls=%fused_computation.86 | custom fusion | flops 1024 | bytes 33280 | tf_op jit(solution)/shard_map/scatter-add | solution.py:100
  119.1 1.3 concatenate.19.payload_ref
  120.4 22.5 %shard_map.66 = f32[1,256]{1,0:T(1,128)} custom-call(f32[32,1,384]{2,1,0:T(1,128)} %concatenate.19.payload_ref), custom_call_target="tpu_custom_call" | custom-call | tf_op jit(solution)/shard_map/pallas_call | solution.py:230
  143.0 1.2 copy.24
  (15 shorter events, 0.1 us)
Async XLA Ops:
  0.0 9.6 %copy-start = (bf16[256,256]{1,0:T(8,128)(2,1)S(1)}, bf16[256,256]{1,0:T(8,128)(2,1)}, u32[]{:S(2)}) copy-start(bf16[256,256]{1,0:T(8,128)(2,1)} %param.7) | copy-start | bytes 393220
  3.9 68.0 %collective-permute-start = (bf16[1,4,256,256]{2,3,1,0:T(8,128)(2,1)}, bf16[1,4,256,256]{2,3,1,0:T(8,128)(2,1)S(1)}, u32[]{:S(2)}, u32[]{:S(2)}) collective-permute-start(bf16[1,4,256,256]{2,3,1,0:T(8,128)(2,1)} %get-tuple-element.5), channel_id=1, source_target_pairs={{0,1},{1,2},{2,3},{3,4},{4,5},{5,6},{6,7},{7,8},{8,9},{9,10},{10,1... | collective-permute-start | bytes 1572872 | tf_op jit(solution)/shard_map/ppermute | solution.py:31
  8.3 63.6 %collective-permute-start.1 = (bf16[1,4,256,256]{2,3,1,0:T(8,128)(2,1)}, bf16[1,4,256,256]{2,3,1,0:T(8,128)(2,1)S(1)}, u32[]{:S(2)}, u32[]{:S(2)}) collective-permute-start(bf16[1,4,256,256]{2,3,1,0:T(8,128)(2,1)} %get-tuple-element.6), channel_id=1, source_target_pairs={{1,0},{2,1},{3,2},{4,3},{5,4},{6,5},{7,6},{8,7},{9,8},{10,9},{11,1... | collective-permute-start | bytes 1572872 | tf_op jit(solution)/shard_map/ppermute | solution.py:33
  70.8 26.5 %collective-permute-start.3 = (bf16[4096,256]{1,0:T(8,128)(2,1)}, bf16[4096,256]{1,0:T(8,128)(2,1)}, u32[]{:S(2)}, u32[]{:S(2)}) collective-permute-start(bf16[4096,256]{1,0:T(8,128)(2,1)} %bitcast.26), channel_id=1, source_target_pairs={{0,128},{128,0},{1,129},{129,1},{2,130},{130,2},{3,131},{131,3},{4... | collective-permute-start | bytes 6291464 | tf_op jit(solution)/shard_map/ppermute | solution.py:88
  72.4 5.1 %copy-start.2 = (s32[1,1,8]{2,1,0:T(1,128)S(1)}, s32[1,1,8]{2,1,0:T(1,128)}, u32[]{:S(2)}) copy-start(s32[1,1,8]{2,1,0:T(1,128)} %param.8) | copy-start | bytes 100
  72.5 5.2 %copy-start.1 = (s32[8192]{0:T(1024)S(1)}, s32[8192]{0:T(1024)}, u32[]{:S(2)}) copy-start(s32[8192]{0:T(1024)} %param.11) | copy-start | bytes 98308
  77.2 8.8 %collective-permute-start.2 = (bf16[1,16,256,256]{2,3,1,0:T(8,128)(2,1)S(1)}, bf16[1,16,256,256]{2,3,1,0:T(8,128)(2,1)}, u32[]{:S(2)}, u32[]{:S(2)}) collective-permute-start(bf16[1,16,256,256]{2,3,1,0:T(8,128)(2,1)S(1)} %fusion.1), channel_id=1, source_target_pairs={{0,128},{128,0},{1,129},{129,1},{2,130},{130,2},{3,131},{131,3},{4... | collective-permute-start | bytes 6291464 | tf_op jit(solution)/shard_map/ppermute | solution.py:77

commit v7 on v5

--- a/solution.py
+++ b/solution.py
@@ -63,28 +63,12 @@
 
 def on_device(frames, templates, pair_block, pair_tile, pair_count, owner_order):
     section_index = lax.axis_index("section")
-    weights = retention_weights()
-    count_frames = frames.shape[1]
     mob_local = frames.shape[2]
-    channels = frames.shape[3]
-    framed = extended(frames, ((DEV, 1),), RAD)
-    padded = framed.astype(jnp.float32)
-    smoothed = weights[0] * padded[:, 0:count_frames]
-    for offset in range(1, 2 * RAD + 1):
-        smoothed = smoothed + weights[offset] * padded[:, offset : offset + count_frames]
-    smoothed = smoothed.astype(jnp.bfloat16)
     section_count = lax.axis_size("section")
-    partner = lax.ppermute(
-        smoothed, "section", [(i, (i + 1) % section_count) for i in range(section_count)]
-    )
-    gathered = jnp.concatenate([smoothed, partner], axis=2)
     kernels = mobility_kernels(section_index * mob_local, mob_local, section_index * mob_local)
-    wavelet_stack = jnp.einsum(
-        "smn,fnc->sfmc", kernels, gathered[0], preferred_element_type=jnp.float32
-    ).astype(jnp.bfloat16)
     half_rows = templates.shape[0] // 2
     my_half = lax.dynamic_slice_in_dim(templates, section_index * half_rows, half_rows, 0)
-    my_rows = gather_rows(my_half)
+    my_rows, wavelet_stack = frame_work(frames[0], kernels, my_half)
     other_rows = lax.ppermute(
         my_rows, "section", [(i, (i + 1) % section_count) for i in range(section_count)]
     )
@@ -244,13 +228,38 @@
     )(payload)
 
 
-def gather_kernel(sizes, half_ref, out_ref, own_sem, z_send, z_recv, y_send, y_recv):
-    n_dy, n_dz = sizes
+def frame_kernel(
+    sizes,
+    frames_ref,
+    kernels_ref,
+    half_ref,
+    out_ref,
+    wave_ref,
+    halo_left,
+    halo_right,
+    own_scans,
+    partner_scans,
+    own_sem,
+    z_send,
+    z_recv,
+    y_send,
+    y_recv,
+    halo_send,
+    halo_recv,
+    swap_send,
+    swap_recv,
+):
+    n_section, n_dy, n_dz = sizes
+    n_dev = n_dy * n_dz
     section = lax.axis_index("section")
     grp = lax.axis_index("grp")
     dy = lax.axis_index("dy")
     dz = lax.axis_index("dz")
     dev = dy * n_dz + dz
+    partner_section = (section + 1) % n_section
+
+    def dev_peer(index):
+        return (section, grp, index // n_dz, index % n_dz)
 
     barrier = pltpu.get_barrier_semaphore()
     for step in range(1, n_dz):
@@ -267,7 +276,31 @@
             device_id=(section, grp, (dy + step) % n_dy, dz),
             device_id_type=pl.DeviceIdType.MESH,
         )
-    pl.semaphore_wait(barrier, n_dz - 1 + n_dy - 1)
+    pl.semaphore_signal(
+        barrier,
+        inc=1,
+        device_id=(partner_section, grp, dy, dz),
+        device_id_type=pl.DeviceIdType.MESH,
+    )
+    has_left = dev > 0
+    has_right = dev < n_dev - 1
+    far_left = jnp.logical_and(has_left, dz == 0)
+    far_right = jnp.logical_and(has_right, dz == n_dz - 1)
+
+    @pl.when(far_left)
+    def _():
+        pl.semaphore_signal(
+            barrier, inc=1, device_id=dev_peer(dev - 1), device_id_type=pl.DeviceIdType.MESH
+        )
+
+    @pl.when(far_right)
+    def _():
+        pl.semaphore_signal(
+            barrier, inc=1, device_id=dev_peer(dev + 1), device_id_type=pl.DeviceIdType.MESH
+        )
+
+    extra = far_left.astype(jnp.int32) + far_right.astype(jnp.int32)
+    pl.semaphore_wait(barrier, n_dz - 1 + n_dy - 1 + 1 + extra)
 
     own = pltpu.make_async_copy(half_ref, out_ref.at[dev], own_sem)
     own.start()
@@ -284,6 +317,95 @@
 
     for step in range(1, n_dz):
         z_copy((dz + step) % n_dz, dz).start()
+
+    count_frames = frames_ref.shape[0]
+
+    def to_left():
+        return pltpu.make_async_remote_copy(
+            src_ref=frames_ref.at[pl.ds(0, RAD)],
+            dst_ref=halo_right,
+            send_sem=halo_send.at[0],
+            recv_sem=halo_recv.at[1],
+            device_id=dev_peer(dev - 1),
+            device_id_type=pl.DeviceIdType.MESH,
+        )
+
+    def to_right():
+        return pltpu.make_async_remote_copy(
+            src_ref=frames_ref.at[pl.ds(count_frames - RAD, RAD)],
+            dst_ref=halo_left,
+            send_sem=halo_send.at[1],
+            recv_sem=halo_recv.at[0],
+            device_id=dev_peer(dev + 1),
+            device_id_type=pl.DeviceIdType.MESH,
+        )
+
+    @pl.when(has_left)
+    def _():
+        to_left().start()
+
+    @pl.when(has_right)
+    def _():
+        to_right().start()
+
+    @pl.when(jnp.logical_not(has_left))
+    def _():
+        halo_left[...] = jnp.zeros(halo_left.shape, halo_left.dtype)
+
+    @pl.when(jnp.logical_not(has_right))
+    def _():
+        halo_right[...] = jnp.zeros(halo_right.shape, halo_right.dtype)
+
+    @pl.when(has_left)
+    def _():
+        to_right_of_left = pltpu.make_async_remote_copy(
+            src_ref=frames_ref.at[pl.ds(0, RAD)],
+            dst_ref=halo_left,
+            send_sem=halo_send.at[1],
+            recv_sem=halo_recv.at[0],
+            device_id=dev_peer(dev - 1),
+            device_id_type=pl.DeviceIdType.MESH,
+        )
+        to_right_of_left.wait_recv()
+        to_left().wait_send()
+
+    @pl.when(has_right)
+    def _():
+        to_left_of_right = pltpu.make_async_remote_copy(
+            src_ref=frames_ref.at[pl.ds(0, RAD)],
+            dst_ref=halo_right,
+            send_sem=halo_send.at[0],
+            recv_sem=halo_recv.at[1],
+            device_id=dev_peer(dev + 1),
+            device_id_type=pl.DeviceIdType.MESH,
+        )
+        to_left_of_right.wait_recv()
+        to_right().wait_send()
+
+    weights = retention_weights()
+
+    def padded_frame(place):
+        if place < RAD:
+            return halo_left[place]
+        if place < RAD + count_frames:
+            return frames_ref[place - RAD]
+        return halo_right[place - RAD - count_frames]
+
+    for frame in range(count_frames):
+        total = weights[0] * padded_frame(frame).astype(jnp.float32)
+        for offset in range(1, 2 * RAD + 1):
+            total = total + weights[offset] * padded_frame(frame + offset).astype(jnp.float32)
+        own_scans[frame] = total.astype(own_scans.dtype)
+
+    swap = pltpu.make_async_remote_copy(
+        src_ref=own_scans,
+        dst_ref=partner_scans,
+        send_sem=swap_send,
+        recv_sem=swap_recv,
+        device_id=(partner_section, grp, dy, dz),
+        device_id_type=pl.DeviceIdType.MESH,
+    )
+    swap.start()
     own.wait()
     for step in range(1, n_dz):
         source = (dz + n_dz - step) % n_dz
@@ -303,6 +425,22 @@
 
     for step in range(1, n_dy):
         y_copy((dy + step) % n_dy, dy).start()
+    swap.wait()
+
+    half = own_scans.shape[1]
+
+    def level_frame(frame, carry):
+        for level in range(SCALES):
+            table = kernels_ref[level]
+            acc = jnp.dot(table[:, :half], own_scans[frame], preferred_element_type=jnp.float32)
+            acc = acc + jnp.dot(
+                table[:, half:], partner_scans[frame], preferred_element_type=jnp.float32
+            )
+            wave_ref[level, frame] = acc.astype(wave_ref.dtype)
+        return carry
+
+    lax.fori_loop(0, count_frames, level_frame, 0)
+
     for step in range(1, n_dy):
         source = (dy + n_dy - step) % n_dy
         y_copy(source, source).wait_recv()
@@ -310,25 +448,39 @@
         y_copy((dy + step) % n_dy, dy).wait_send()
 
 
-def gather_rows(half):
-    sizes = (lax.axis_size("dy"), lax.axis_size("dz"))
-    n_dy, n_dz = sizes
+def frame_work(frames, kernels, half):
+    sizes = (lax.axis_size("section"), lax.axis_size("dy"), lax.axis_size("dz"))
+    n_section, n_dy, n_dz = sizes
     rows, channels = half.shape
-    out = pl.pallas_call(
-        functools.partial(gather_kernel, sizes),
-        out_shape=jax.ShapeDtypeStruct((n_dy * n_dz, rows, channels), half.dtype),
-        in_specs=[pl.BlockSpec(memory_space=pltpu.VMEM)],
-        out_specs=pl.BlockSpec(memory_space=pltpu.VMEM),
+    count_frames, mob_local, _ = frames.shape
+    rows_out, wave = pl.pallas_call(
+        functools.partial(frame_kernel, sizes),
+        out_shape=(
+            jax.ShapeDtypeStruct((n_dy * n_dz, rows, channels), half.dtype),
+            jax.ShapeDtypeStruct((SCALES, count_frames, mob_local, channels), jnp.bfloat16),
+        ),
+        in_specs=[pl.BlockSpec(memory_space=pltpu.VMEM)] * 3,
+        out_specs=(pl.BlockSpec(memory_space=pltpu.VMEM), pl.BlockSpec(memory_space=pltpu.VMEM)),
         scratch_shapes=[
+            pltpu.VMEM((RAD, mob_local, channels), frames.dtype),
+            pltpu.VMEM((RAD, mob_local, channels), frames.dtype),
+            pltpu.VMEM((count_frames, mob_local, channels), jnp.bfloat16),
+            pltpu.VMEM((count_frames, mob_local, channels), jnp.bfloat16),
             pltpu.SemaphoreType.DMA(()),
             pltpu.SemaphoreType.DMA((n_dz,)),
             pltpu.SemaphoreType.DMA((n_dz,)),
             pltpu.SemaphoreType.DMA((n_dy,)),
             pltpu.SemaphoreType.DMA((n_dy,)),
+            pltpu.SemaphoreType.DMA((2,)),
+            pltpu.SemaphoreType.DMA((2,)),
+            pltpu.SemaphoreType.DMA(()),
+            pltpu.SemaphoreType.DMA(()),
         ],
-        compiler_params=pltpu.CompilerParams(collective_id=1, has_side_effects=True),
-    )(half)
-    return out.reshape(n_dy * n_dz * rows, channels)
+        compiler_params=pltpu.CompilerParams(
+            collective_id=1, has_side_effects=True, vmem_limit_bytes=56 * 1024 * 1024
+        ),
+    )(frames, kernels, half)
+    return rows_out.reshape(n_dy * n_dz * rows, channels), wave
 
 
 def score_kernel(tile_ref, block_ref, count_ref, section_ref, wave_ref, mine_ref, other_ref, out_ref):

time: 134 us -> 123 us (0.918)
  Pallas kernels: 86.1 us -> 100 us
  matrix products: 11.2 us -> 0 us
  starting transfers between devices: 8.33 us -> 1.66 us
  other arithmetic: 14.2 us -> 8.98 us
  local copies, waits for them, and re-layouts: 13.2 us -> 11.1 us
    pallas_call x1, Pallas kernels: 52.2 us -> 68.3 us  [frame_work(): pl.pallas_call(functools.partial(frame_kernel, sizes), out_shape=(jax.Sha...]
    dot_general x1 -> x0, matrix products: 11.2 us -> none  [on_device(): jnp.einsum('smn,fnc->sfmc', kernels, gathered[0], preferred_element_type=...]
    ppermute x3 -> x0, starting transfers between devices: 5.98 us -> none  [the longest x1 4.39 us: extended(): lax.ppermute(tail, axis, [(i, (i + 1) % count) for i in range(ends)])]
    convert_element_type x2 -> x0, other arithmetic: 5.22 us -> none  [the longest x1 4.75 us: on_device(): smoothed = smoothed.astype(jnp.bfloat16)]
    pallas_call x1, Pallas kernels: 27 us -> 23.3 us  [reduce_owned(): pl.pallas_call(functools.partial(reduce_kernel, sizes), out_shape=jax.Sha...]
    pallas_call x1, Pallas kernels: 6.91 us -> 8.32 us  [score_pairs(): pl.pallas_call(score_kernel, grid_spec=grid_spec, out_shape=jax.ShapeDtyp...]
    unnamed x8 -> x11, local copies, waits for them, and re-layouts: 4.13 us -> 3 us
  transfers between devices with their start and end apart: 4 -> 1, of which waited for: 0 -> 0; matrix products, arithmetic and copies ran while one was open for 19% -> 5% of each run, Pallas kernels for 39% -> 0%
where the time goes in v7:
time: 123 us
  Pallas kernels  100 us (81%)
  local copies, waits for them, and re-layouts  11.1 us (9%)
  other arithmetic  8.98 us (7%)
  starting transfers between devices  1.66 us (1%)
    pallas_call x1, Pallas kernels, frame_work(): pl.pallas_call(functools.partial(frame_kernel, sizes), out_shape=(jax.Sha...  68.3 us
    pallas_call x1, Pallas kernels, reduce_owned(): pl.pallas_call(functools.partial(reduce_kernel, sizes), out_shape=jax.Sha...  23.3 us
    pallas_call x1, Pallas kernels, score_pairs(): pl.pallas_call(score_kernel, grid_spec=grid_spec, out_shape=jax.ShapeDtyp...  8.32 us
    gather x1, local copies, waits for them, and re-layouts, on_device(): positions = owner_order[precursors]  6.15 us
    scatter-add x1, other arithmetic, on_device(): jnp.zeros((PREC,), jnp.float32).at[positions.reshape(-1)]  6.1 us
    unnamed x11, local copies, waits for them, and re-layouts  3 us
  transfers between devices with their start and end apart: 1, of which 0 were waited for; matrix products, arithmetic and copies ran while one was open for 5% of the time, Pallas kernels for 0%

profile of v7, /device:TPU:1, one launch (start us, length us, event | category | flops | bytes accessed | tf_op | source)
XLA Modules:
  0.0 122.5 jit_solution(7001191112196663622)
XLA Ops:
  0.0 0.0 copy-start
  0.0 0.2 fusion.45
  0.3 0.3 fusion.40
  0.5 0.3 fusion.41
  0.8 0.3 fusion.42
  1.0 0.3 fusion.43
  1.3 0.3 fusion.44.kernels_ref
  1.6 0.0 copy-start.2
  1.6 0.0 copy-done
  1.6 0.7 constant_dynamic-slice_fusion.half_ref
  2.3 0.5 copy-done.2
  2.7 68.3 %shard_map.64 = (bf16[32,128,256]{2,1,0:T(8,128)(2,1)}, bf16[6,16,256,256]{3,2,1,0:T(8,128)(2,1)}) custom-call(bf16[16,256,256]{2,1,0:T(8,128)(2,1)} %bitcast.18, bf16[6,256,512]{2,1,0:T(8,128)(2,1)} %copy-done.2, bf16[128,256]{1,0:T(8,128)(2,1)} %constant_dynamic-slice_fusion.half_ref), custom_call_target="tpu_custom_call" | custom-call | tf_op jit(solution)/shard_map/pallas_call | solution.py:456
  71.1 1.7 %collective-permute-start = (bf16[4096,256]{1,0:T(8,128)(2,1)}, bf16[4096,256]{1,0:T(8,128)(2,1)S(1)}, u32[]{:S(2)}, u32[]{:S(2)}) collective-permute-start(bf16[4096,256]{1,0:T(8,128)(2,1)} %bitcast.16), channel_id=1, source_target_pairs={{0,128},{128,0},{1,129},{129,1},{2,130},{130,2},{3,131},{131,3},{4... | collective-permute-start | bytes 6291464 | tf_op jit(solution)/shard_map/ppermute | solution.py:72
  73.4 0.0 copy-done.4
  73.4 0.1 fusion.49
  73.5 6.1 %gather_fusion = s32[1024]{0:T(1024)S(1)} fusion(s32[8192]{0:T(1024)S(1)} %copy-done.1, s32[1024]{0:T(1024)S(1)} %fusion.49), kind=kCustom, calls=%fused_computation | custom fusion | bytes 12288 | tf_op jit(solution)/shard_map/gather | solution.py:83
  79.7 0.0 collective-permute-done.other_ref
  79.7 1.3 %copy-done.3 = bf16[4096,256]{1,0:T(8,128)(2,1)} copy-done((bf16[4096,256]{1,0:T(8,128)(2,1)}, bf16[4096,256]{1,0:T(8,128)(2,1)S(1)}, u32[]{:S(2)}) %copy-start.3) | copy-done | bytes 2097176
  81.0 8.3 %shard_map.65 = f32[8,1,128]{2,1,0:T(1,128)} custom-call(s32[8]{0:T(128)} %bitcast.24, s32[8]{0:T(128)} %bitcast.23, s32[1]{0:T(128)} %bitcast.15.count_ref, s32[1]{0:T(128)} %bitcast.6.section_ref, bf16[6,16,256,256]{3,2,1,0:T(8,128)(2,1)} %get-tuple-element.7.wave_ref, bf16[4096,256]{1,0:T(8,128)(2,1)} %bitcast.17, bf16[4096,256]{1,0:T(8,128)(2,1)} %copy-done.3), custom_call_target="tpu_custom_call" | custom-call | tf_op jit(solution)/shard_map/pallas_call | solution.py:539
  89.3 1.3 %reduce_sum.9 = f32[]{:T(128)} reduce(f32[8,1,128]{2,1,0:T(1,128)} %shard_map.65, f32[]{:T(128)} %constant.27.clone.1), dimensions={0,1,2}, to_apply=%region_1.2 | reduce | flops 1023 | bytes 4104 | tf_op jit(solution)/shard_map/reduce_sum | solution.py:86
  90.6 6.1 %scatter_custom_fusion = f32[8192]{0:T(1024)S(1)} fusion(s32[1024]{0:T(1024)S(1)} %bitcast.22, f32[1024]{0:T(1024)} %bitcast.20, f32[]{:T(128)} %constant.27.clone.1), kind=kCustom, calls=%fused_computation.62 | custom fusion | flops 1024 | bytes 33280 | tf_op jit(solution)/shard_map/scatter-add | solution.py:84
  96.7 1.3 %concatenate.3.payload_ref = f32[32,1,384]{2,1,0:T(1,128)} pad(f32[32,1,256]{2,1,0:T(1,128)S(1)} %bitcast.19, f32[]{:T(128)} %reduce_sum.9), padding=0_0x0_0x0_128 | pad | bytes 81924 | tf_op jit(solution)/shard_map/concatenate | solution.py:87
  98.0 23.3 %shard_map.66 = f32[1,256]{1,0:T(1,128)} custom-call(f32[32,1,384]{2,1,0:T(1,128)} %concatenate.3.payload_ref), custom_call_target="tpu_custom_call" | custom-call | tf_op jit(solution)/shard_map/pallas_call | solution.py:214
  121.3 1.2 copy.14
  (8 shorter events, 0.0 us)
Async XLA Ops:
  0.0 1.6 %copy-start = (bf16[256,256]{1,0:T(8,128)(2,1)S(1)}, bf16[256,256]{1,0:T(8,128)(2,1)}, u32[]{:S(2)}) copy-start(bf16[256,256]{1,0:T(8,128)(2,1)} %param.7) | copy-start | bytes 393220
  1.6 1.2 copy-start.2
  2.7 70.7 %copy-start.4 = (s32[1,1,8]{2,1,0:T(1,128)S(1)}, s32[1,1,8]{2,1,0:T(1,128)}, u32[]{:S(2)}) copy-start(s32[1,1,8]{2,1,0:T(1,128)} %param.8) | copy-start | bytes 100
  2.7 70.8 %copy-start.1 = (s32[8192]{0:T(1024)S(1)}, s32[8192]{0:T(1024)}, u32[]{:S(2)}) copy-start(s32[8192]{0:T(1024)} %param.11) | copy-start | bytes 98308
  71.1 8.6 %collective-permute-start = (bf16[4096,256]{1,0:T(8,128)(2,1)}, bf16[4096,256]{1,0:T(8,128)(2,1)S(1)}, u32[]{:S(2)}, u32[]{:S(2)}) collective-permute-start(bf16[4096,256]{1,0:T(8,128)(2,1)} %bitcast.16), channel_id=1, source_target_pairs={{0,128},{128,0},{1,129},{129,1},{2,130},{130,2},{3,131},{131,3},{4... | collective-permute-start | bytes 6291464 | tf_op jit(solution)/shard_map/ppermute | solution.py:72
  79.7 1.3 %copy-start.3 = (bf16[4096,256]{1,0:T(8,128)(2,1)}, bf16[4096,256]{1,0:T(8,128)(2,1)S(1)}, u32[]{:S(2)}) copy-start(bf16[4096,256]{1,0:T(8,128)(2,1)S(1)} %collective-permute-done.other_ref) | copy-start | bytes 6291460

commit v8 on v7

--- a/solution.py
+++ b/solution.py
@@ -318,6 +318,38 @@
     for step in range(1, n_dz):
         z_copy((dz + step) % n_dz, dz).start()
 
+    def y_copy(target, source, chunk):
+        slot = source * n_dz + chunk
+        return pltpu.make_async_remote_copy(
+            src_ref=out_ref.at[slot],
+            dst_ref=out_ref.at[slot],
+            send_sem=y_send.at[target * n_dz + chunk],
+            recv_sem=y_recv.at[slot],
+            device_id=(section, grp, target, dz),
+            device_id_type=pl.DeviceIdType.MESH,
+        )
+
+    def y_own(target):
+        return pltpu.make_async_remote_copy(
+            src_ref=half_ref,
+            dst_ref=out_ref.at[dev],
+            send_sem=y_send.at[target * n_dz + dz],
+            recv_sem=y_recv.at[dev],
+            device_id=(section, grp, target, dz),
+            device_id_type=pl.DeviceIdType.MESH,
+        )
+
+    for step in range(1, n_dy):
+        y_own((dy + step) % n_dy).start()
+    for step in range(1, n_dz):
+        source = (dz + n_dz - step) % n_dz
+        z_copy(source, source).wait_recv()
+        for hop in range(1, n_dy):
+            y_copy((dy + hop) % n_dy, dy, source).start()
+    own.wait()
+    for step in range(1, n_dz):
+        z_copy((dz + step) % n_dz, dz).wait_send()
+
     count_frames = frames_ref.shape[0]
 
     def to_left():
@@ -406,25 +438,6 @@
         device_id_type=pl.DeviceIdType.MESH,
     )
     swap.start()
-    own.wait()
-    for step in range(1, n_dz):
-        source = (dz + n_dz - step) % n_dz
-        z_copy(source, source).wait_recv()
-    for step in range(1, n_dz):
-        z_copy((dz + step) % n_dz, dz).wait_send()
-
-    def y_copy(target, source):
-        return pltpu.make_async_remote_copy(
-            src_ref=out_ref.at[pl.ds(source * n_dz, n_dz)],
-            dst_ref=out_ref.at[pl.ds(source * n_dz, n_dz)],
-            send_sem=y_send.at[target],
-            recv_sem=y_recv.at[source],
-            device_id=(section, grp, target, dz),
-            device_id_type=pl.DeviceIdType.MESH,
-        )
-
-    for step in range(1, n_dy):
-        y_copy((dy + step) % n_dy, dy).start()
     swap.wait()
 
     half = own_scans.shape[1]
@@ -443,9 +456,11 @@
 
     for step in range(1, n_dy):
         source = (dy + n_dy - step) % n_dy
-        y_copy(source, source).wait_recv()
+        for chunk in range(n_dz):
+            y_copy(source, source, chunk).wait_recv()
     for step in range(1, n_dy):
-        y_copy((dy + step) % n_dy, dy).wait_send()
+        for chunk in range(n_dz):
+            y_copy((dy + step) % n_dy, dy, chunk).wait_send()
 
 
 def frame_work(frames, kernels, half):
@@ -469,8 +484,8 @@
             pltpu.SemaphoreType.DMA(()),
             pltpu.SemaphoreType.DMA((n_dz,)),
             pltpu.SemaphoreType.DMA((n_dz,)),
-            pltpu.SemaphoreType.DMA((n_dy,)),
-            pltpu.SemaphoreType.DMA((n_dy,)),
+            pltpu.SemaphoreType.DMA((n_dy * n_dz,)),
+            pltpu.SemaphoreType.DMA((n_dy * n_dz,)),
             pltpu.SemaphoreType.DMA((2,)),
             pltpu.SemaphoreType.DMA((2,)),
             pltpu.SemaphoreType.DMA(()),

time: 123 us -> 113 us (0.919)
  Pallas kernels: 100 us -> 91.5 us
  starting transfers between devices: 1.66 us -> 0.23 us
    pallas_call x1, Pallas kernels: 68.3 us -> 58.8 us  [frame_work(): pl.pallas_call(functools.partial(frame_kernel, sizes), out_shape=(jax.Sha...]
    pallas_call x1, Pallas kernels: 23.3 us -> 25.8 us  [reduce_owned(): pl.pallas_call(functools.partial(reduce_kernel, sizes), out_shape=jax.Sha...]
    pallas_call x1, Pallas kernels: 8.32 us -> 6.87 us  [score_pairs(): pl.pallas_call(score_kernel, grid_spec=grid_spec, out_shape=jax.ShapeDtyp...]
    ppermute x1, starting transfers between devices: 1.66 us -> 0.23 us  [on_device(): lax.ppermute(my_rows, 'section', [(i, (i + 1) % section_count) for i in r...]
  transfers between devices with their start and end apart: 1 -> 1, of which waited for: 0 -> 0; matrix products, arithmetic and copies ran while one was open for 5% -> 6% of each run, Pallas kernels for 0% -> 0%
where the time goes in v8:
time: 113 us
  Pallas kernels  91.5 us (81%)
  local copies, waits for them, and re-layouts  11.1 us (10%)
  other arithmetic  8.98 us (8%)
    pallas_call x1, Pallas kernels, frame_work(): pl.pallas_call(functools.partial(frame_kernel, sizes), out_shape=(jax.Sha...  58.8 us
    pallas_call x1, Pallas kernels, reduce_owned(): pl.pallas_call(functools.partial(reduce_kernel, sizes), out_shape=jax.Sha...  25.8 us
    pallas_call x1, Pallas kernels, score_pairs(): pl.pallas_call(score_kernel, grid_spec=grid_spec, out_shape=jax.ShapeDtyp...  6.87 us
    gather x1, local copies, waits for them, and re-layouts, on_device(): positions = owner_order[precursors]  6.15 us
    scatter-add x1, other arithmetic, on_device(): jnp.zeros((PREC,), jnp.float32).at[positions.reshape(-1)]  6.1 us
    unnamed x11, local copies, waits for them, and re-layouts  3 us
  transfers between devices with their start and end apart: 1, of which 0 were waited for; matrix products, arithmetic and copies ran while one was open for 6% of the time, Pallas kernels for 0%

profile of v8, /device:TPU:1, one launch (start us, length us, event | category | flops | bytes accessed | tf_op | source)
XLA Modules:
  0.0 112.6 jit_solution(13833771722873774440)
XLA Ops:
  0.0 0.0 copy-start
  0.0 0.2 fusion.45
  0.3 0.3 fusion.40
  0.5 0.3 fusion.41
  0.8 0.3 fusion.42
  1.0 0.3 fusion.43
  1.3 0.3 fusion.44.kernels_ref
  1.6 0.0 copy-start.2
  1.6 0.0 copy-done
  1.6 0.7 constant_dynamic-slice_fusion.half_ref
  2.3 0.5 copy-done.2
  2.7 58.8 %shard_map.64 = (bf16[32,128,256]{2,1,0:T(8,128)(2,1)}, bf16[6,16,256,256]{3,2,1,0:T(8,128)(2,1)}) custom-call(bf16[16,256,256]{2,1,0:T(8,128)(2,1)} %bitcast.18, bf16[6,256,512]{2,1,0:T(8,128)(2,1)} %copy-done.2, bf16[128,256]{1,0:T(8,128)(2,1)} %constant_dynamic-slice_fusion.half_ref), custom_call_target="tpu_custom_call" | custom-call | tf_op jit(solution)/shard_map/pallas_call | solution.py:471
  61.5 0.2 collective-permute-start
  62.4 0.1 fusion.49
  62.5 0.0 copy-done.1
  62.5 6.1 %gather_fusion = s32[1024]{0:T(1024)S(1)} fusion(s32[8192]{0:T(1024)S(1)} %copy-done.1, s32[1024]{0:T(1024)S(1)} %fusion.49), kind=kCustom, calls=%fused_computation | custom fusion | bytes 12288 | tf_op jit(solution)/shard_map/gather | solution.py:83
  68.7 0.0 collective-permute-done.other_ref
  68.7 1.3 %copy-done.3 = bf16[4096,256]{1,0:T(8,128)(2,1)} copy-done((bf16[4096,256]{1,0:T(8,128)(2,1)}, bf16[4096,256]{1,0:T(8,128)(2,1)S(1)}, u32[]{:S(2)}) %copy-start.3) | copy-done | bytes 2097176
  70.0 6.9 %shard_map.65 = f32[8,1,128]{2,1,0:T(1,128)} custom-call(s32[8]{0:T(128)} %bitcast.24, s32[8]{0:T(128)} %bitcast.23, s32[1]{0:T(128)} %bitcast.15.count_ref, s32[1]{0:T(128)} %bitcast.6.section_ref, bf16[6,16,256,256]{3,2,1,0:T(8,128)(2,1)} %get-tuple-element.7.wave_ref, bf16[4096,256]{1,0:T(8,128)(2,1)} %bitcast.17, bf16[4096,256]{1,0:T(8,128)(2,1)} %copy-done.3), custom_call_target="tpu_custom_call" | custom-call | tf_op jit(solution)/shard_map/pallas_call | solution.py:554
  76.9 1.3 %reduce_sum.9 = f32[]{:T(128)} reduce(f32[8,1,128]{2,1,0:T(1,128)} %shard_map.65, f32[]{:T(128)} %constant.27.clone.1), dimensions={0,1,2}, to_apply=%region_1.2 | reduce | flops 1023 | bytes 4104 | tf_op jit(solution)/shard_map/reduce_sum | solution.py:86
  78.2 6.1 %scatter_custom_fusion = f32[8192]{0:T(1024)S(1)} fusion(s32[1024]{0:T(1024)S(1)} %bitcast.22, f32[1024]{0:T(1024)} %bitcast.20, f32[]{:T(128)} %constant.27.clone.1), kind=kCustom, calls=%fused_computation.62 | custom fusion | flops 1024 | bytes 33280 | tf_op jit(solution)/shard_map/scatter-add | solution.py:84
  84.3 1.3 %concatenate.3.payload_ref = f32[32,1,384]{2,1,0:T(1,128)} pad(f32[32,1,256]{2,1,0:T(1,128)S(1)} %bitcast.19, f32[]{:T(128)} %reduce_sum.9), padding=0_0x0_0x0_128 | pad | bytes 81924 | tf_op jit(solution)/shard_map/concatenate | solution.py:87
  85.6 25.8 %shard_map.66 = f32[1,256]{1,0:T(1,128)} custom-call(f32[32,1,384]{2,1,0:T(1,128)} %concatenate.3.payload_ref), custom_call_target="tpu_custom_call" | custom-call | tf_op jit(solution)/shard_map/pallas_call | solution.py:214
  111.4 1.2 %copy.14 = f32[1,256]{1,0:T(1,128)} copy(f32[1,256]{1,0:T(1,128)} %shard_map.66) | data formatting | bytes 2048
  (8 shorter events, 0.0 us)
Async XLA Ops:
  0.0 1.6 %copy-start = (bf16[256,256]{1,0:T(8,128)(2,1)S(1)}, bf16[256,256]{1,0:T(8,128)(2,1)}, u32[]{:S(2)}) copy-start(bf16[256,256]{1,0:T(8,128)(2,1)} %param.7) | copy-start | bytes 393220
  1.6 1.2 %copy-start.2 = (bf16[6,256,512]{2,1,0:T(8,128)(2,1)}, bf16[6,256,512]{2,1,0:T(8,128)(2,1)S(1)}, u32[]{:S(2)}) copy-start(bf16[6,256,512]{2,1,0:T(8,128)(2,1)S(1)} %fusion.44.kernels_ref) | copy-start | bytes 4718596
  2.7 59.7 %copy-start.4 = (s32[1,1,8]{2,1,0:T(1,128)S(1)}, s32[1,1,8]{2,1,0:T(1,128)}, u32[]{:S(2)}) copy-start(s32[1,1,8]{2,1,0:T(1,128)} %param.8) | copy-start | bytes 100
  2.7 59.7 %copy-start.1 = (s32[8192]{0:T(1024)S(1)}, s32[8192]{0:T(1024)}, u32[]{:S(2)}) copy-start(s32[8192]{0:T(1024)} %param.11) | copy-start | bytes 98308
  61.5 7.1 %collective-permute-start = (bf16[4096,256]{1,0:T(8,128)(2,1)}, bf16[4096,256]{1,0:T(8,128)(2,1)S(1)}, u32[]{:S(2)}, u32[]{:S(2)}) collective-permute-start(bf16[4096,256]{1,0:T(8,128)(2,1)} %bitcast.16), channel_id=1, source_target_pairs={{0,128},{128,0},{1,129},{129,1},{2,130},{130,2},{3,131},{131,3},{4... | collective-permute-start | bytes 6291464 | tf_op jit(solution)/shard_map/ppermute | solution.py:72
  68.7 1.3 %copy-start.3 = (bf16[4096,256]{1,0:T(8,128)(2,1)}, bf16[4096,256]{1,0:T(8,128)(2,1)S(1)}, u32[]{:S(2)}) copy-start(bf16[4096,256]{1,0:T(8,128)(2,1)S(1)} %collective-permute-done.other_ref) | copy-start | bytes 6291460

commit v9 on v8

--- a/solution.py
+++ b/solution.py
@@ -79,9 +79,23 @@
     responses = score_pairs(
         wavelet_stack, my_rows, other_rows, tile_ids, block_ids, live_pairs, section_index
     )
-    precursors = block_ids[:, None] * PB + jnp.arange(PB, dtype=jnp.int32)[None, :]
-    positions = owner_order[precursors]
-    placed = jnp.zeros((PREC,), jnp.float32).at[positions.reshape(-1)].add(responses.reshape(-1))
+    positions = jnp.take(owner_order.reshape(-1, PB), block_ids, axis=0).reshape(-1)
+    groups = PREC // PB
+    by_group = jnp.where(
+        (positions // PB)[:, None] == jnp.arange(groups, dtype=jnp.int32)[None, :],
+        responses.reshape(-1)[:, None],
+        0.0,
+    )
+    by_lane = ((positions % PB)[:, None] == jnp.arange(PB, dtype=jnp.int32)[None, :]).astype(
+        jnp.float32
+    )
+    placed = jnp.einsum(
+        "ka,kb->ab",
+        by_group,
+        by_lane,
+        precision=lax.Precision.HIGHEST,
+        preferred_element_type=jnp.float32,
+    ).reshape(-1)
     dev_count = lax.axis_size(DEV)
     local_total = jnp.sum(responses)
     payload = jnp.concatenate(

time: 113 us -> 107 us (0.947)
  other arithmetic: 8.98 us -> 2.89 us
  local copies, waits for them, and re-layouts: 11.1 us -> 5.57 us
  waiting for transfers between devices: 0.01 us -> 2.88 us
  matrix products: 0 us -> 1.74 us
    scatter-add x1 -> x0, other arithmetic: 6.1 us -> none  [on_device(): jnp.zeros((PREC,), jnp.float32).at[positions.reshape(-1)]]
    gather x1, local copies, waits for them, and re-layouts: 6.15 us -> 0.56 us  [on_device(): jnp.take(owner_order.reshape(-1, PB), block_ids, axis=0).reshape(-1)]
    ppermute x1, waiting for transfers between devices: 0.01 us -> 2.88 us  [on_device(): lax.ppermute(my_rows, 'section', [(i, (i + 1) % section_count) for i in r...]
    dot_general x0 -> x1, matrix products: none -> 1.74 us  [on_device(): jnp.einsum('ka,kb->ab', by_group, by_lane, precision=lax.Precision.HIGHES...]
  transfers between devices with their start and end apart: 1 -> 1, of which waited for: 0 -> 1; matrix products, arithmetic and copies ran while one was open for 6% -> 1% of each run, Pallas kernels for 0% -> 0%
where the time goes in v9:
time: 107 us; the launch traced here: 106 us
  Pallas kernels  92.4 us (86%)
  local copies, waits for them, and re-layouts  5.57 us (5%)
  other arithmetic  2.89 us (3%)
  waiting for transfers between devices  2.88 us (3%)
  matrix products  1.74 us (2%)
    pallas_call x1, Pallas kernels, frame_work(): pl.pallas_call(functools.partial(frame_kernel, sizes), out_shape=(jax.Sha...  58.7 us
    pallas_call x1, Pallas kernels, reduce_owned(): pl.pallas_call(functools.partial(reduce_kernel, sizes), out_shape=jax.Sha...  26.7 us
    pallas_call x1, Pallas kernels, score_pairs(): pl.pallas_call(score_kernel, grid_spec=grid_spec, out_shape=jax.ShapeDtyp...  6.9 us
    unnamed x11, local copies, waits for them, and re-layouts  3.02 us
    ppermute x1, waiting for transfers between devices, on_device(): lax.ppermute(my_rows, 'section', [(i, (i + 1) % section_count) for i in r...  2.88 us
  transfers between devices with their start and end apart: 1, of which 1 were waited for; matrix products, arithmetic and copies ran while one was open for 1% of the time, Pallas kernels for 0%

profile of v9, /device:TPU:1, one launch (start us, length us, event | category | flops | bytes accessed | tf_op | source)
XLA Modules:
  0.0 106.5 jit_solution(16517286549785259629)
XLA Ops:
  0.0 0.0 copy-start
  0.0 0.2 fusion.47
  0.3 0.3 fusion.42
  0.5 0.3 fusion.43
  0.8 0.3 fusion.44
  1.0 0.3 fusion.45
  1.3 0.3 fusion.46.kernels_ref
  1.6 0.0 copy-start.1
  1.6 0.0 copy-done
  1.6 0.7 constant_dynamic-slice_fusion.half_ref
  2.3 0.5 copy-done.1
  2.7 58.7 %shard_map.64 = (bf16[32,128,256]{2,1,0:T(8,128)(2,1)}, bf16[6,16,256,256]{3,2,1,0:T(8,128)(2,1)}) custom-call(bf16[16,256,256]{2,1,0:T(8,128)(2,1)} %bitcast.43, bf16[6,256,512]{2,1,0:T(8,128)(2,1)} %copy-done.1, bf16[128,256]{1,0:T(8,128)(2,1)} %constant_dynamic-slice_fusion.half_ref), custom_call_target="tpu_custom_call" | custom-call | tf_op jit(solution)/shard_map/pallas_call | solution.py:485
  61.5 0.2 collective-permute-start
  62.4 0.0 copy-done.3
  62.4 0.6 gather_fusion
  63.0 0.1 add_select_fusion.1
  63.1 2.9 %collective-permute-done.other_ref = bf16[4096,256]{1,0:T(8,128)(2,1)S(1)} collective-permute-done((bf16[4096,256]{1,0:T(8,128)(2,1)}, bf16[4096,256]{1,0:T(8,128)(2,1)S(1)}, u32[]{:S(2)}, u32[]{:S(2)}) %collective-permute-start) | collective-permute-done | bytes 2097184 | tf_op jit(solution)/shard_map/ppermute | solution.py:72
  65.9 1.3 %copy-done.2 = bf16[4096,256]{1,0:T(8,128)(2,1)} copy-done((bf16[4096,256]{1,0:T(8,128)(2,1)}, bf16[4096,256]{1,0:T(8,128)(2,1)S(1)}, u32[]{:S(2)}) %copy-start.2) | copy-done | bytes 2097176
  67.3 6.9 %shard_map.65 = f32[8,1,128]{2,1,0:T(1,128)} custom-call(s32[8]{0:T(128)} %bitcast.48, s32[8]{0:T(128)} %bitcast.47, s32[1]{0:T(128)} %bitcast.40.count_ref, s32[1]{0:T(128)} %bitcast.7.section_ref, bf16[6,16,256,256]{3,2,1,0:T(8,128)(2,1)} %get-tuple-element.7.wave_ref, bf16[4096,256]{1,0:T(8,128)(2,1)} %bitcast.42, bf16[4096,256]{1,0:T(8,128)(2,1)} %copy-done.2), custom_call_target="tpu_custom_call" | custom-call | tf_op jit(solution)/shard_map/pallas_call | solution.py:568
  74.2 1.3 %reduce_sum.9 = f32[]{:T(128)} reduce(f32[8,1,128]{2,1,0:T(1,128)} %shard_map.65, f32[]{:T(128)} %constant.114.clone.1), dimensions={0,1,2}, to_apply=%region_0.1 | reduce | flops 1023 | bytes 4104 | tf_op jit(solution)/shard_map/reduce_sum | solution.py:100
  75.5 1.7 %fusion.40 = f32[64,128]{1,0:T(8,128)S(1)} fusion(s32[1024]{0:T(1024)S(1)} %get-tuple-element.10, f32[1024]{0:T(1024)} %bitcast.46, s32[1024]{0:T(1024)S(1)} %get-tuple-element.9), kind=kOutput, calls=%fused_computation.55 | convolution fusion | flops 100925440 | bytes 45056 | tf_op jit(solution)/shard_map/ka,kb->ab/dot_general | solution.py:92
  77.2 1.3 %concatenate.3.payload_ref = f32[32,1,384]{2,1,0:T(1,128)} pad(f32[32,1,256]{2,1,0:T(1,128)S(1)} %bitcast.45, f32[]{:T(128)} %reduce_sum.9), padding=0_0x0_0x0_128 | pad | bytes 81924 | tf_op jit(solution)/shard_map/concatenate | solution.py:101
  78.5 26.7 %shard_map.66 = f32[1,256]{1,0:T(1,128)} custom-call(f32[32,1,384]{2,1,0:T(1,128)} %concatenate.3.payload_ref), custom_call_target="tpu_custom_call" | custom-call | tf_op jit(solution)/shard_map/pallas_call | solution.py:228
  105.2 1.2 %copy.14 = f32[1,256]{1,0:T(1,128)} copy(f32[1,256]{1,0:T(1,128)} %shard_map.66) | data formatting | bytes 2048
  (9 shorter events, 0.0 us)
Async XLA Ops:
  0.0 1.6 %copy-start = (bf16[256,256]{1,0:T(8,128)(2,1)S(1)}, bf16[256,256]{1,0:T(8,128)(2,1)}, u32[]{:S(2)}) copy-start(bf16[256,256]{1,0:T(8,128)(2,1)} %param.7) | copy-start | bytes 393220
  1.6 1.2 %copy-start.1 = (bf16[6,256,512]{2,1,0:T(8,128)(2,1)}, bf16[6,256,512]{2,1,0:T(8,128)(2,1)S(1)}, u32[]{:S(2)}) copy-start(bf16[6,256,512]{2,1,0:T(8,128)(2,1)S(1)} %fusion.46.kernels_ref) | copy-start | bytes 4718596
  2.7 59.6 %copy-start.4 = (s32[1,1,8]{2,1,0:T(1,128)S(1)}, s32[1,1,8]{2,1,0:T(1,128)}, u32[]{:S(2)}) copy-start(s32[1,1,8]{2,1,0:T(1,128)} %param.8) | copy-start | bytes 100
  2.7 59.7 %copy-start.3 = (s32[8192]{0:T(1024)S(1)}, s32[8192]{0:T(1024)}, u32[]{:S(2)}) copy-start(s32[8192]{0:T(1024)} %param.11) | copy-start | bytes 98308
  61.5 4.5 %collective-permute-start = (bf16[4096,256]{1,0:T(8,128)(2,1)}, bf16[4096,256]{1,0:T(8,128)(2,1)S(1)}, u32[]{:S(2)}, u32[]{:S(2)}) collective-permute-start(bf16[4096,256]{1,0:T(8,128)(2,1)} %bitcast.41), channel_id=1, source_target_pairs={{0,128},{128,0},{1,129},{129,1},{2,130},{130,2},{3,131},{131,3},{4... | collective-permute-start | bytes 6291464 | tf_op jit(solution)/shard_map/ppermute | solution.py:72
  65.9 1.3 %copy-start.2 = (bf16[4096,256]{1,0:T(8,128)(2,1)}, bf16[4096,256]{1,0:T(8,128)(2,1)S(1)}, u32[]{:S(2)}) copy-start(bf16[4096,256]{1,0:T(8,128)(2,1)S(1)} %collective-permute-done.other_ref) | copy-start | bytes 6291460

commit v10 on v9

--- a/solution.py
+++ b/solution.py
@@ -283,11 +283,13 @@
             device_id=(section, grp, dy, (dz + step) % n_dz),
             device_id_type=pl.DeviceIdType.MESH,
         )
-    for step in range(1, n_dy):
+    up = (dy + 1) % n_dy
+    down = (dy + n_dy - 1) % n_dy
+    for row in (up, down):
         pl.semaphore_signal(
             barrier,
             inc=1,
-            device_id=(section, grp, (dy + step) % n_dy, dz),
+            device_id=(section, grp, row, dz),
             device_id_type=pl.DeviceIdType.MESH,
         )
     pl.semaphore_signal(
@@ -314,7 +316,7 @@
         )
 
     extra = far_left.astype(jnp.int32) + far_right.astype(jnp.int32)
-    pl.semaphore_wait(barrier, n_dz - 1 + n_dy - 1 + 1 + extra)
+    pl.semaphore_wait(barrier, n_dz - 1 + 2 + 1 + extra)
 
     own = pltpu.make_async_copy(half_ref, out_ref.at[dev], own_sem)
     own.start()
@@ -332,34 +334,36 @@
     for step in range(1, n_dz):
         z_copy((dz + step) % n_dz, dz).start()
 
-    def y_copy(target, source, chunk):
-        slot = source * n_dz + chunk
+    def y_copy(direction, row, chunk):
+        slot = row * n_dz + chunk
+        target = up if direction == 0 else down
         return pltpu.make_async_remote_copy(
             src_ref=out_ref.at[slot],
             dst_ref=out_ref.at[slot],
-            send_sem=y_send.at[target * n_dz + chunk],
+            send_sem=y_send.at[direction * n_dy * n_dz + slot],
             recv_sem=y_recv.at[slot],
             device_id=(section, grp, target, dz),
             device_id_type=pl.DeviceIdType.MESH,
         )
 
-    def y_own(target):
+    def y_own(direction):
+        target = up if direction == 0 else down
         return pltpu.make_async_remote_copy(
             src_ref=half_ref,
             dst_ref=out_ref.at[dev],
-            send_sem=y_send.at[target * n_dz + dz],
+            send_sem=y_send.at[direction * n_dy * n_dz + dev],
             recv_sem=y_recv.at[dev],
             device_id=(section, grp, target, dz),
             device_id_type=pl.DeviceIdType.MESH,
         )
 
-    for step in range(1, n_dy):
-        y_own((dy + step) % n_dy).start()
+    for direction in (0, 1):
+        y_own(direction).start()
     for step in range(1, n_dz):
         source = (dz + n_dz - step) % n_dz
         z_copy(source, source).wait_recv()
-        for hop in range(1, n_dy):
-            y_copy((dy + hop) % n_dy, dy, source).start()
+        for direction in (0, 1):
+            y_copy(direction, dy, source).start()
     own.wait()
     for step in range(1, n_dz):
         z_copy((dz + step) % n_dz, dz).wait_send()
@@ -452,6 +456,14 @@
         device_id_type=pl.DeviceIdType.MESH,
     )
     swap.start()
+    relay = n_dz // 2
+    for chunk in range(n_dz):
+        y_copy(0, down, chunk).wait_recv()
+        if chunk < relay:
+            y_copy(0, down, chunk).start()
+        y_copy(1, up, chunk).wait_recv()
+        if chunk >= relay:
+            y_copy(1, up, chunk).start()
     swap.wait()
 
     half = own_scans.shape[1]
@@ -468,13 +480,16 @@
 
     lax.fori_loop(0, count_frames, level_frame, 0)
 
-    for step in range(1, n_dy):
-        source = (dy + n_dy - step) % n_dy
+    opposite = (dy + 2) % n_dy
+    for chunk in range(n_dz):
+        y_copy(0, opposite, chunk).wait_recv()
+    for direction in (0, 1):
         for chunk in range(n_dz):
-            y_copy(source, source, chunk).wait_recv()
-    for step in range(1, n_dy):
-        for chunk in range(n_dz):
-            y_copy((dy + step) % n_dy, dy, chunk).wait_send()
+            y_copy(direction, dy, chunk).wait_send()
+    for chunk in range(relay):
+        y_copy(0, down, chunk).wait_send()
+    for chunk in range(relay, n_dz):
+        y_copy(1, up, chunk).wait_send()
 
 
 def frame_work(frames, kernels, half):
@@ -498,7 +513,7 @@
             pltpu.SemaphoreType.DMA(()),
             pltpu.SemaphoreType.DMA((n_dz,)),
             pltpu.SemaphoreType.DMA((n_dz,)),
-            pltpu.SemaphoreType.DMA((n_dy * n_dz,)),
+            pltpu.SemaphoreType.DMA((2 * n_dy * n_dz,)),
             pltpu.SemaphoreType.DMA((n_dy * n_dz,)),
             pltpu.SemaphoreType.DMA((2,)),
             pltpu.SemaphoreType.DMA((2,)),

time: 107 us -> 108 us (level)
  Pallas kernels: 92.4 us -> 93.6 us
where the time goes in v10:
time: 108 us
  Pallas kernels  93.6 us (87%)
  local copies, waits for them, and re-layouts  5.57 us (5%)
  other arithmetic  2.89 us (3%)
  waiting for transfers between devices  2.88 us (3%)
  matrix products  1.74 us (2%)
    pallas_call x1, Pallas kernels, frame_work(): pl.pallas_call(functools.partial(frame_kernel, sizes), out_shape=(jax.Sha...  59 us
    pallas_call x1, Pallas kernels, reduce_owned(): pl.pallas_call(functools.partial(reduce_kernel, sizes), out_shape=jax.Sha...  26.9 us
    pallas_call x1, Pallas kernels, score_pairs(): pl.pallas_call(score_kernel, grid_spec=grid_spec, out_shape=jax.ShapeDtyp...  7.65 us
    unnamed x11, local copies, waits for them, and re-layouts  3.02 us
    ppermute x1, waiting for transfers between devices, on_device(): lax.ppermute(my_rows, 'section', [(i, (i + 1) % section_count) for i in r...  2.88 us
  transfers between devices with their start and end apart: 1, of which 1 were waited for; matrix products, arithmetic and copies ran while one was open for 1% of the time, Pallas kernels for 0%

profile of v10, /device:TPU:1, one launch (start us, length us, event | category | flops | bytes accessed | tf_op | source)
XLA Modules:
  0.0 107.7 jit_solution(15363765111358346036)
XLA Ops:
  0.0 0.0 copy-start
  0.0 0.2 fusion.47
  0.3 0.3 fusion.42
  0.5 0.3 fusion.43
  0.8 0.3 fusion.44
  1.0 0.3 fusion.45
  1.3 0.3 fusion.46.kernels_ref
  1.6 0.0 copy-start.1
  1.6 0.0 copy-done
  1.6 0.7 constant_dynamic-slice_fusion.half_ref
  2.3 0.5 copy-done.1
  2.7 59.0 %shard_map.64 = (bf16[32,128,256]{2,1,0:T(8,128)(2,1)}, bf16[6,16,256,256]{3,2,1,0:T(8,128)(2,1)}) custom-call(bf16[16,256,256]{2,1,0:T(8,128)(2,1)} %bitcast.43, bf16[6,256,512]{2,1,0:T(8,128)(2,1)} %copy-done.1, bf16[128,256]{1,0:T(8,128)(2,1)} %constant_dynamic-slice_fusion.half_ref), custom_call_target="tpu_custom_call" | custom-call | tf_op jit(solution)/shard_map/pallas_call | solution.py:500
  61.7 0.2 collective-permute-start
  62.6 0.0 copy-done.4
  62.7 0.6 gather_fusion
  63.2 0.1 add_select_fusion.1
  63.3 2.9 %collective-permute-done.other_ref = bf16[4096,256]{1,0:T(8,128)(2,1)S(1)} collective-permute-done((bf16[4096,256]{1,0:T(8,128)(2,1)}, bf16[4096,256]{1,0:T(8,128)(2,1)S(1)}, u32[]{:S(2)}, u32[]{:S(2)}) %collective-permute-start) | collective-permute-done | bytes 2097184 | tf_op jit(solution)/shard_map/ppermute | solution.py:72
  66.2 1.3 %copy-done.2 = bf16[4096,256]{1,0:T(8,128)(2,1)} copy-done((bf16[4096,256]{1,0:T(8,128)(2,1)}, bf16[4096,256]{1,0:T(8,128)(2,1)S(1)}, u32[]{:S(2)}) %copy-start.2) | copy-done | bytes 2097176
  67.5 7.7 %shard_map.65 = f32[8,1,128]{2,1,0:T(1,128)} custom-call(s32[8]{0:T(128)} %bitcast.48, s32[8]{0:T(128)} %bitcast.47, s32[1]{0:T(128)} %bitcast.40.count_ref, s32[1]{0:T(128)} %bitcast.7.section_ref, bf16[6,16,256,256]{3,2,1,0:T(8,128)(2,1)} %get-tuple-element.7.wave_ref, bf16[4096,256]{1,0:T(8,128)(2,1)} %bitcast.42, bf16[4096,256]{1,0:T(8,128)(2,1)} %copy-done.2), custom_call_target="tpu_custom_call" | custom-call | tf_op jit(solution)/shard_map/pallas_call | solution.py:583
  75.2 1.3 %reduce_sum.9 = f32[]{:T(128)} reduce(f32[8,1,128]{2,1,0:T(1,128)} %shard_map.65, f32[]{:T(128)} %constant.114.clone.1), dimensions={0,1,2}, to_apply=%region_0.1 | reduce | flops 1023 | bytes 4104 | tf_op jit(solution)/shard_map/reduce_sum | solution.py:100
  76.5 1.7 %fusion.40 = f32[64,128]{1,0:T(8,128)S(1)} fusion(s32[1024]{0:T(1024)S(1)} %get-tuple-element.10, f32[1024]{0:T(1024)} %bitcast.46, s32[1024]{0:T(1024)S(1)} %get-tuple-element.9), kind=kOutput, calls=%fused_computation.55 | convolution fusion | flops 100925440 | bytes 45056 | tf_op jit(solution)/shard_map/ka,kb->ab/dot_general | solution.py:92
  78.2 1.3 %concatenate.3.payload_ref = f32[32,1,384]{2,1,0:T(1,128)} pad(f32[32,1,256]{2,1,0:T(1,128)S(1)} %bitcast.45, f32[]{:T(128)} %reduce_sum.9), padding=0_0x0_0x0_128 | pad | bytes 81924 | tf_op jit(solution)/shard_map/concatenate | solution.py:101
  79.5 26.9 %shard_map.66 = f32[1,256]{1,0:T(1,128)} custom-call(f32[32,1,384]{2,1,0:T(1,128)} %concatenate.3.payload_ref), custom_call_target="tpu_custom_call" | custom-call | tf_op jit(solution)/shard_map/pallas_call | solution.py:228
  106.4 1.2 %copy.14 = f32[1,256]{1,0:T(1,128)} copy(f32[1,256]{1,0:T(1,128)} %shard_map.66) | data formatting | bytes 2048
  (9 shorter events, 0.0 us)
Async XLA Ops:
  0.0 1.6 %copy-start = (bf16[256,256]{1,0:T(8,128)(2,1)S(1)}, bf16[256,256]{1,0:T(8,128)(2,1)}, u32[]{:S(2)}) copy-start(bf16[256,256]{1,0:T(8,128)(2,1)} %param.7) | copy-start | bytes 393220
  1.6 1.2 %copy-start.1 = (bf16[6,256,512]{2,1,0:T(8,128)(2,1)}, bf16[6,256,512]{2,1,0:T(8,128)(2,1)S(1)}, u32[]{:S(2)}) copy-start(bf16[6,256,512]{2,1,0:T(8,128)(2,1)S(1)} %fusion.46.kernels_ref) | copy-start | bytes 4718596
  2.7 59.9 %copy-start.4 = (s32[1,1,8]{2,1,0:T(1,128)S(1)}, s32[1,1,8]{2,1,0:T(1,128)}, u32[]{:S(2)}) copy-start(s32[1,1,8]{2,1,0:T(1,128)} %param.8) | copy-start | bytes 100
  2.7 59.9 %copy-start.3 = (s32[8192]{0:T(1024)S(1)}, s32[8192]{0:T(1024)}, u32[]{:S(2)}) copy-start(s32[8192]{0:T(1024)} %param.11) | copy-start | bytes 98308
  61.7 4.5 %collective-permute-start = (bf16[4096,256]{1,0:T(8,128)(2,1)}, bf16[4096,256]{1,0:T(8,128)(2,1)S(1)}, u32[]{:S(2)}, u32[]{:S(2)}) collective-permute-start(bf16[4096,256]{1,0:T(8,128)(2,1)} %bitcast.41), channel_id=1, source_target_pairs={{0,128},{128,0},{1,129},{129,1},{2,130},{130,2},{3,131},{131,3},{4... | collective-permute-start | bytes 6291464 | tf_op jit(solution)/shard_map/ppermute | solution.py:72
  66.2 1.3 %copy-start.2 = (bf16[4096,256]{1,0:T(8,128)(2,1)}, bf16[4096,256]{1,0:T(8,128)(2,1)S(1)}, u32[]{:S(2)}) copy-start(bf16[4096,256]{1,0:T(8,128)(2,1)S(1)} %collective-permute-done.other_ref) | copy-start | bytes 6291460

commit v11 on v10

--- a/solution.py
+++ b/solution.py
@@ -434,18 +434,26 @@
 
     weights = retention_weights()
 
-    def padded_frame(place):
-        if place < RAD:
-            return halo_left[place]
-        if place < RAD + count_frames:
-            return frames_ref[place - RAD]
-        return halo_right[place - RAD - count_frames]
-
-    for frame in range(count_frames):
-        total = weights[0] * padded_frame(frame).astype(jnp.float32)
-        for offset in range(1, 2 * RAD + 1):
-            total = total + weights[offset] * padded_frame(frame + offset).astype(jnp.float32)
-        own_scans[frame] = total.astype(own_scans.dtype)
+    row_block = 32
+
+    def smooth_rows(block, carry):
+        rows = pl.ds(pl.multiple_of(block * row_block, row_block), row_block)
+
+        def padded_frame(place):
+            if place < RAD:
+                return halo_left[place, rows, :]
+            if place < RAD + count_frames:
+                return frames_ref[place - RAD, rows, :]
+            return halo_right[place - RAD - count_frames, rows, :]
+
+        for frame in range(count_frames):
+            total = weights[0] * padded_frame(frame).astype(jnp.float32)
+            for offset in range(1, 2 * RAD + 1):
+                total = total + weights[offset] * padded_frame(frame + offset).astype(jnp.float32)
+            own_scans[frame, rows, :] = total.astype(own_scans.dtype)
+        return carry
+
+    lax.fori_loop(0, own_scans.shape[1] // row_block, smooth_rows, 0)
 
     swap = pltpu.make_async_remote_copy(
         src_ref=own_scans,

time: 108 us -> 107 us (level)
  Pallas kernels: 93.6 us -> 92.2 us
    pallas_call x1, Pallas kernels: 26.9 us -> 24.6 us  [reduce_owned(): pl.pallas_call(functools.partial(reduce_kernel, sizes), out_shape=jax.Sha...]
    pallas_call x1, Pallas kernels: 7.65 us -> 9.29 us  [score_pairs(): pl.pallas_call(score_kernel, grid_spec=grid_spec, out_shape=jax.ShapeDtyp...]
where the time goes in v11:
time: 107 us; the launch traced here: 106 us
  Pallas kernels  92.2 us (86%)
  local copies, waits for them, and re-layouts  5.57 us (5%)
  other arithmetic  2.89 us (3%)
  waiting for transfers between devices  2.88 us (3%)
  matrix products  1.74 us (2%)
    pallas_call x1, Pallas kernels, frame_work(): pl.pallas_call(functools.partial(frame_kernel, sizes), out_shape=(jax.Sha...  58.3 us
    pallas_call x1, Pallas kernels, reduce_owned(): pl.pallas_call(functools.partial(reduce_kernel, sizes), out_shape=jax.Sha...  24.6 us
    pallas_call x1, Pallas kernels, score_pairs(): pl.pallas_call(score_kernel, grid_spec=grid_spec, out_shape=jax.ShapeDtyp...  9.29 us
    unnamed x11, local copies, waits for them, and re-layouts  3.02 us
    ppermute x1, waiting for transfers between devices, on_device(): lax.ppermute(my_rows, 'section', [(i, (i + 1) % section_count) for i in r...  2.88 us
  transfers between devices with their start and end apart: 1, of which 1 were waited for; matrix products, arithmetic and copies ran while one was open for 1% of the time, Pallas kernels for 0%

profile of v11, /device:TPU:1, one launch (start us, length us, event | category | flops | bytes accessed | tf_op | source)
XLA Modules:
  0.0 106.3 jit_solution(17477950891462929657)
XLA Ops:
  0.0 0.0 copy-start
  0.0 0.2 fusion.47
  0.3 0.3 fusion.42
  0.5 0.3 fusion.43
  0.8 0.3 fusion.44
  1.0 0.3 fusion.45
  1.3 0.3 fusion.46.kernels_ref
  1.6 0.0 copy-start.1
  1.6 0.0 copy-done
  1.6 0.7 constant_dynamic-slice_fusion.half_ref
  2.3 0.5 copy-done.1
  2.7 58.3 %shard_map.64 = (bf16[32,128,256]{2,1,0:T(8,128)(2,1)}, bf16[6,16,256,256]{3,2,1,0:T(8,128)(2,1)}) custom-call(bf16[16,256,256]{2,1,0:T(8,128)(2,1)} %bitcast.43, bf16[6,256,512]{2,1,0:T(8,128)(2,1)} %copy-done.1, bf16[128,256]{1,0:T(8,128)(2,1)} %constant_dynamic-slice_fusion.half_ref), custom_call_target="tpu_custom_call" | custom-call | tf_op jit(solution)/shard_map/pallas_call | solution.py:508
  61.1 0.2 collective-permute-start
  61.9 0.0 copy-done.4
  62.0 0.6 gather_fusion
  62.6 0.1 add_select_fusion.1
  62.6 2.9 %collective-permute-done.other_ref = bf16[4096,256]{1,0:T(8,128)(2,1)S(1)} collective-permute-done((bf16[4096,256]{1,0:T(8,128)(2,1)}, bf16[4096,256]{1,0:T(8,128)(2,1)S(1)}, u32[]{:S(2)}, u32[]{:S(2)}) %collective-permute-start) | collective-permute-done | bytes 2097184 | tf_op jit(solution)/shard_map/ppermute | solution.py:72
  65.5 1.3 %copy-done.2 = bf16[4096,256]{1,0:T(8,128)(2,1)} copy-done((bf16[4096,256]{1,0:T(8,128)(2,1)}, bf16[4096,256]{1,0:T(8,128)(2,1)S(1)}, u32[]{:S(2)}) %copy-start.2) | copy-done | bytes 2097176
  66.8 9.3 %shard_map.65 = f32[8,1,128]{2,1,0:T(1,128)} custom-call(s32[8]{0:T(128)} %bitcast.48, s32[8]{0:T(128)} %bitcast.47, s32[1]{0:T(128)} %bitcast.40.count_ref, s32[1]{0:T(128)} %bitcast.7.section_ref, bf16[6,16,256,256]{3,2,1,0:T(8,128)(2,1)} %get-tuple-element.7.wave_ref, bf16[4096,256]{1,0:T(8,128)(2,1)} %bitcast.42, bf16[4096,256]{1,0:T(8,128)(2,1)} %copy-done.2), custom_call_target="tpu_custom_call" | custom-call | tf_op jit(solution)/shard_map/pallas_call | solution.py:591
  76.1 1.3 %reduce_sum.9 = f32[]{:T(128)} reduce(f32[8,1,128]{2,1,0:T(1,128)} %shard_map.65, f32[]{:T(128)} %constant.114.clone.1), dimensions={0,1,2}, to_apply=%region_0.1 | reduce | flops 1023 | bytes 4104 | tf_op jit(solution)/shard_map/reduce_sum | solution.py:100
  77.4 1.7 %fusion.40 = f32[64,128]{1,0:T(8,128)S(1)} fusion(s32[1024]{0:T(1024)S(1)} %get-tuple-element.10, f32[1024]{0:T(1024)} %bitcast.46, s32[1024]{0:T(1024)S(1)} %get-tuple-element.9), kind=kOutput, calls=%fused_computation.55 | convolution fusion | flops 100925440 | bytes 45056 | tf_op jit(solution)/shard_map/ka,kb->ab/dot_general | solution.py:92
  79.2 1.3 %concatenate.3.payload_ref = f32[32,1,384]{2,1,0:T(1,128)} pad(f32[32,1,256]{2,1,0:T(1,128)S(1)} %bitcast.45, f32[]{:T(128)} %reduce_sum.9), padding=0_0x0_0x0_128 | pad | bytes 81924 | tf_op jit(solution)/shard_map/concatenate | solution.py:101
  80.5 24.6 %shard_map.66 = f32[1,256]{1,0:T(1,128)} custom-call(f32[32,1,384]{2,1,0:T(1,128)} %concatenate.3.payload_ref), custom_call_target="tpu_custom_call" | custom-call | tf_op jit(solution)/shard_map/pallas_call | solution.py:228
  105.0 1.2 %copy.14 = f32[1,256]{1,0:T(1,128)} copy(f32[1,256]{1,0:T(1,128)} %shard_map.66) | data formatting | bytes 2048
  (9 shorter events, 0.0 us)
Async XLA Ops:
  0.0 1.6 %copy-start = (bf16[256,256]{1,0:T(8,128)(2,1)S(1)}, bf16[256,256]{1,0:T(8,128)(2,1)}, u32[]{:S(2)}) copy-start(bf16[256,256]{1,0:T(8,128)(2,1)} %param.7) | copy-start | bytes 393220
  1.6 1.2 %copy-start.1 = (bf16[6,256,512]{2,1,0:T(8,128)(2,1)}, bf16[6,256,512]{2,1,0:T(8,128)(2,1)S(1)}, u32[]{:S(2)}) copy-start(bf16[6,256,512]{2,1,0:T(8,128)(2,1)S(1)} %fusion.46.kernels_ref) | copy-start | bytes 4718596
  2.7 59.2 %copy-start.4 = (s32[1,1,8]{2,1,0:T(1,128)S(1)}, s32[1,1,8]{2,1,0:T(1,128)}, u32[]{:S(2)}) copy-start(s32[1,1,8]{2,1,0:T(1,128)} %param.8) | copy-start | bytes 100
  2.7 59.2 %copy-start.3 = (s32[8192]{0:T(1024)S(1)}, s32[8192]{0:T(1024)}, u32[]{:S(2)}) copy-start(s32[8192]{0:T(1024)} %param.11) | copy-start | bytes 98308
  61.1 4.5 %collective-permute-start = (bf16[4096,256]{1,0:T(8,128)(2,1)}, bf16[4096,256]{1,0:T(8,128)(2,1)S(1)}, u32[]{:S(2)}, u32[]{:S(2)}) collective-permute-start(bf16[4096,256]{1,0:T(8,128)(2,1)} %bitcast.41), channel_id=1, source_target_pairs={{0,128},{128,0},{1,129},{129,1},{2,130},{130,2},{3,131},{131,3},{4... | collective-permute-start | bytes 6291464 | tf_op jit(solution)/shard_map/ppermute | solution.py:72
  65.5 1.3 %copy-start.2 = (bf16[4096,256]{1,0:T(8,128)(2,1)}, bf16[4096,256]{1,0:T(8,128)(2,1)S(1)}, u32[]{:S(2)}) copy-start(bf16[4096,256]{1,0:T(8,128)(2,1)S(1)} %collective-permute-done.other_ref) | copy-start | bytes 6291460

commit v12 on v11

--- a/solution.py
+++ b/solution.py
@@ -359,6 +359,102 @@
 
     for direction in (0, 1):
         y_own(direction).start()
+    count_frames = frames_ref.shape[0]
+
+    def to_left():
+        return pltpu.make_async_remote_copy(
+            src_ref=frames_ref.at[pl.ds(0, RAD)],
+            dst_ref=halo_right,
+            send_sem=halo_send.at[0],
+            recv_sem=halo_recv.at[1],
+            device_id=dev_peer(dev - 1),
+            device_id_type=pl.DeviceIdType.MESH,
+        )
+
+    def to_right():
+        return pltpu.make_async_remote_copy(
+            src_ref=frames_ref.at[pl.ds(count_frames - RAD, RAD)],
+            dst_ref=halo_left,
+            send_sem=halo_send.at[1],
+            recv_sem=halo_recv.at[0],
+            device_id=dev_peer(dev + 1),
+            device_id_type=pl.DeviceIdType.MESH,
+        )
+
+    @pl.when(has_left)
+    def _():
+        to_left().start()
+
+    @pl.when(has_right)
+    def _():
+        to_right().start()
+
+    @pl.when(jnp.logical_not(has_left))
+    def _():
+        halo_left[...] = jnp.zeros(halo_left.shape, halo_left.dtype)
+
+    @pl.when(jnp.logical_not(has_right))
+    def _():
+        halo_right[...] = jnp.zeros(halo_right.shape, halo_right.dtype)
+
+    @pl.when(has_left)
+    def _():
+        to_right_of_left = pltpu.make_async_remote_copy(
+            src_ref=frames_ref.at[pl.ds(0, RAD)],
+            dst_ref=halo_left,
+            send_sem=halo_send.at[1],
+            recv_sem=halo_recv.at[0],
+            device_id=dev_peer(dev - 1),
+            device_id_type=pl.DeviceIdType.MESH,
+        )
+        to_right_of_left.wait_recv()
+        to_left().wait_send()
+
+    @pl.when(has_right)
+    def _():
+        to_left_of_right = pltpu.make_async_remote_copy(
+            src_ref=frames_ref.at[pl.ds(0, RAD)],
+            dst_ref=halo_right,
+            send_sem=halo_send.at[0],
+            recv_sem=halo_recv.at[1],
+            device_id=dev_peer(dev + 1),
+            device_id_type=pl.DeviceIdType.MESH,
+        )
+        to_left_of_right.wait_recv()
+        to_right().wait_send()
+
+    weights = retention_weights()
+
+    row_block = 32
+
+    def smooth_rows(block, carry):
+        rows = pl.ds(pl.multiple_of(block * row_block, row_block), row_block)
+
+        def padded_frame(place):
+            if place < RAD:
+                return halo_left[place, rows, :]
+            if place < RAD + count_frames:
+                return frames_ref[place - RAD, rows, :]
+            return halo_right[place - RAD - count_frames, rows, :]
+
+        for frame in range(count_frames):
+            total = weights[0] * padded_frame(frame).astype(jnp.float32)
+            for offset in range(1, 2 * RAD + 1):
+                total = total + weights[offset] * padded_frame(frame + offset).astype(jnp.float32)
+            own_scans[frame, rows, :] = total.astype(own_scans.dtype)
+        return carry
+
+    lax.fori_loop(0, own_scans.shape[1] // row_block, smooth_rows, 0)
+
+    swap = pltpu.make_async_remote_copy(
+        src_ref=own_scans,
+        dst_ref=partner_scans,
+        send_sem=swap_send,
+        recv_sem=swap_recv,
+        device_id=(partner_section, grp, dy, dz),
+        device_id_type=pl.DeviceIdType.MESH,
+    )
+    swap.start()
     for step in range(1, n_dz):
         source = (dz + n_dz - step) % n_dz
         z_copy(source, source).wait_recv()
@@ -368,102 +464,6 @@
     for step in range(1, n_dz):
         z_copy((dz + step) % n_dz, dz).wait_send()
 
-    count_frames = frames_ref.shape[0]
-
-    def to_left():
-        return pltpu.make_async_remote_copy(
-            src_ref=frames_ref.at[pl.ds(0, RAD)],
-            dst_ref=halo_right,
-            send_sem=halo_send.at[0],
-            recv_sem=halo_recv.at[1],
-            device_id=dev_peer(dev - 1),
-            device_id_type=pl.DeviceIdType.MESH,
-        )
-
-    def to_right():
-        return pltpu.make_async_remote_copy(
-            src_ref=frames_ref.at[pl.ds(count_frames - RAD, RAD)],
-            dst_ref=halo_left,
-            send_sem=halo_send.at[1],
-            recv_sem=halo_recv.at[0],
-            device_id=dev_peer(dev + 1),
-            device_id_type=pl.DeviceIdType.MESH,
-        )
-
-    @pl.when(has_left)
-    def _():
-        to_left().start()
-
-    @pl.when(has_right)
-    def _():
-        to_right().start()
-
-    @pl.when(jnp.logical_not(has_left))
-    def _():
-        halo_left[...] = jnp.zeros(halo_left.shape, halo_left.dtype)
-
-    @pl.when(jnp.logical_not(has_right))
-    def _():
-        halo_right[...] = jnp.zeros(halo_right.shape, halo_right.dtype)
-
-    @pl.when(has_left)
-    def _():
-        to_right_of_left = pltpu.make_async_remote_copy(
-            src_ref=frames_ref.at[pl.ds(0, RAD)],
-            dst_ref=halo_left,
-            send_sem=halo_send.at[1],
-            recv_sem=halo_recv.at[0],
-            device_id=dev_peer(dev - 1),
-            device_id_type=pl.DeviceIdType.MESH,
-        )
-        to_right_of_left.wait_recv()
-        to_left().wait_send()
-
-    @pl.when(has_right)
-    def _():
-        to_left_of_right = pltpu.make_async_remote_copy(
-            src_ref=frames_ref.at[pl.ds(0, RAD)],
-            dst_ref=halo_right,
-            send_sem=halo_send.at[0],
-            recv_sem=halo_recv.at[1],
-            device_id=dev_peer(dev + 1),
-            device_id_type=pl.DeviceIdType.MESH,
-        )
-        to_left_of_right.wait_recv()
-        to_right().wait_send()
-
-    weights = retention_weights()
-
-    row_block = 32
-
-    def smooth_rows(block, carry):
-        rows = pl.ds(pl.multiple_of(block * row_block, row_block), row_block)
-
-        def padded_frame(place):
-            if place < RAD:
-                return halo_left[place, rows, :]
-            if place < RAD + count_frames:
-                return frames_ref[place - RAD, rows, :]
-            return halo_right[place - RAD - count_frames, rows, :]
-
-        for frame in range(count_frames):
-            total = weights[0] * padded_frame(frame).astype(jnp.float32)
-            for offset in range(1, 2 * RAD + 1):
-                total = total + weights[offset] * padded_frame(frame + offset).astype(jnp.float32)
-            own_scans[frame, rows, :] = total.astype(own_scans.dtype)
-        return carry
-
-    lax.fori_loop(0, own_scans.shape[1] // row_block, smooth_rows, 0)
-
-    swap = pltpu.make_async_remote_copy(
-        src_ref=own_scans,
-        dst_ref=partner_scans,
-        send_sem=swap_send,
-        recv_sem=swap_recv,
-        device_id=(partner_section, grp, dy, dz),
-        device_id_type=pl.DeviceIdType.MESH,
-    )
-    swap.start()
     relay = n_dz // 2
     for chunk in range(n_dz):
         y_copy(0, down, chunk).wait_recv()

time: 107 us -> 113 us (1.056)
  Pallas kernels: 92.2 us -> 96.8 us
  starting transfers between devices: 0.23 us -> 2.47 us
    pallas_call x1, Pallas kernels: 58.3 us -> 64.9 us  [frame_work(): pl.pallas_call(functools.partial(frame_kernel, sizes), out_shape=(jax.Sha...]
    ppermute x1, starting transfers between devices: 0.23 us -> 2.47 us  [on_device(): lax.ppermute(my_rows, 'section', [(i, (i + 1) % section_count) for i in r...]
    pallas_call x1, Pallas kernels: 24.6 us -> 22.3 us  [reduce_owned(): pl.pallas_call(functools.partial(reduce_kernel, sizes), out_shape=jax.Sha...]
where the time goes in v12:
time: 113 us
  Pallas kernels  96.8 us (86%)
  local copies, waits for them, and re-layouts  5.57 us (5%)
  other arithmetic  2.89 us (3%)
  waiting for transfers between devices  2.65 us (2%)
  starting transfers between devices  2.47 us (2%)
  matrix products  1.74 us (2%)
    pallas_call x1, Pallas kernels, frame_work(): pl.pallas_call(functools.partial(frame_kernel, sizes), out_shape=(jax.Sha...  64.9 us
    pallas_call x1, Pallas kernels, reduce_owned(): pl.pallas_call(functools.partial(reduce_kernel, sizes), out_shape=jax.Sha...  22.3 us
    pallas_call x1, Pallas kernels, score_pairs(): pl.pallas_call(score_kernel, grid_spec=grid_spec, out_shape=jax.ShapeDtyp...  9.58 us
    unnamed x11, local copies, waits for them, and re-layouts  3.02 us
    ppermute x1, waiting for transfers between devices, on_device(): lax.ppermute(my_rows, 'section', [(i, (i + 1) % section_count) for i in r...  2.65 us
    ppermute x1, starting transfers between devices, on_device(): lax.ppermute(my_rows, 'section', [(i, (i + 1) % section_count) for i in r...  2.47 us
  transfers between devices with their start and end apart: 1, of which 1 were waited for; matrix products, arithmetic and copies ran while one was open for 1% of the time, Pallas kernels for 0%

profile of v12, /device:TPU:1, one launch (start us, length us, event | category | flops | bytes accessed | tf_op | source)
XLA Modules:
  0.0 112.9 jit_solution(17127546154668562147)
XLA Ops:
  0.0 0.0 copy-start
  0.0 0.2 fusion.47
  0.3 0.3 fusion.42
  0.5 0.3 fusion.43
  0.8 0.3 fusion.44
  1.0 0.3 fusion.45
  1.3 0.3 fusion.46.kernels_ref
  1.6 0.0 copy-start.1
  1.6 0.0 copy-done
  1.6 0.7 constant_dynamic-slice_fusion.half_ref
  2.3 0.5 copy-done.1
  2.7 64.9 %shard_map.64 = (bf16[32,128,256]{2,1,0:T(8,128)(2,1)}, bf16[6,16,256,256]{3,2,1,0:T(8,128)(2,1)}) custom-call(bf16[16,256,256]{2,1,0:T(8,128)(2,1)} %bitcast.43, bf16[6,256,512]{2,1,0:T(8,128)(2,1)} %copy-done.1, bf16[128,256]{1,0:T(8,128)(2,1)} %constant_dynamic-slice_fusion.half_ref), custom_call_target="tpu_custom_call" | custom-call | tf_op jit(solution)/shard_map/pallas_call | solution.py:508
  67.6 2.5 %collective-permute-start = (bf16[4096,256]{1,0:T(8,128)(2,1)}, bf16[4096,256]{1,0:T(8,128)(2,1)S(1)}, u32[]{:S(2)}, u32[]{:S(2)}) collective-permute-start(bf16[4096,256]{1,0:T(8,128)(2,1)} %bitcast.41), channel_id=1, source_target_pairs={{0,128},{128,0},{1,129},{129,1},{2,130},{130,2},{3,131},{131,3},{4... | collective-permute-start | bytes 6291464 | tf_op jit(solution)/shard_map/ppermute | solution.py:72
  70.7 0.0 copy-done.4
  70.8 0.6 gather_fusion
  71.4 0.1 add_select_fusion.1
  71.4 2.6 %collective-permute-done.other_ref = bf16[4096,256]{1,0:T(8,128)(2,1)S(1)} collective-permute-done((bf16[4096,256]{1,0:T(8,128)(2,1)}, bf16[4096,256]{1,0:T(8,128)(2,1)S(1)}, u32[]{:S(2)}, u32[]{:S(2)}) %collective-permute-start) | collective-permute-done | bytes 2097184 | tf_op jit(solution)/shard_map/ppermute | solution.py:72
  74.1 1.3 %copy-done.2 = bf16[4096,256]{1,0:T(8,128)(2,1)} copy-done((bf16[4096,256]{1,0:T(8,128)(2,1)}, bf16[4096,256]{1,0:T(8,128)(2,1)S(1)}, u32[]{:S(2)}) %copy-start.2) | copy-done | bytes 2097176
  75.4 9.6 %shard_map.65 = f32[8,1,128]{2,1,0:T(1,128)} custom-call(s32[8]{0:T(128)} %bitcast.48, s32[8]{0:T(128)} %bitcast.47, s32[1]{0:T(128)} %bitcast.40.count_ref, s32[1]{0:T(128)} %bitcast.7.section_ref, bf16[6,16,256,256]{3,2,1,0:T(8,128)(2,1)} %get-tuple-element.7.wave_ref, bf16[4096,256]{1,0:T(8,128)(2,1)} %bitcast.42, bf16[4096,256]{1,0:T(8,128)(2,1)} %copy-done.2), custom_call_target="tpu_custom_call" | custom-call | tf_op jit(solution)/shard_map/pallas_call | solution.py:591
  85.0 1.3 %reduce_sum.9 = f32[]{:T(128)} reduce(f32[8,1,128]{2,1,0:T(1,128)} %shard_map.65, f32[]{:T(128)} %constant.114.clone.1), dimensions={0,1,2}, to_apply=%region_0.1 | reduce | flops 1023 | bytes 4104 | tf_op jit(solution)/shard_map/reduce_sum | solution.py:100
  86.3 1.7 %fusion.40 = f32[64,128]{1,0:T(8,128)S(1)} fusion(s32[1024]{0:T(1024)S(1)} %get-tuple-element.10, f32[1024]{0:T(1024)} %bitcast.46, s32[1024]{0:T(1024)S(1)} %get-tuple-element.9), kind=kOutput, calls=%fused_computation.55 | convolution fusion | flops 100925440 | bytes 45056 | tf_op jit(solution)/shard_map/ka,kb->ab/dot_general | solution.py:92
  88.0 1.3 %concatenate.3.payload_ref = f32[32,1,384]{2,1,0:T(1,128)} pad(f32[32,1,256]{2,1,0:T(1,128)S(1)} %bitcast.45, f32[]{:T(128)} %reduce_sum.9), padding=0_0x0_0x0_128 | pad | bytes 81924 | tf_op jit(solution)/shard_map/concatenate | solution.py:101
  89.3 22.3 %shard_map.66 = f32[1,256]{1,0:T(1,128)} custom-call(f32[32,1,384]{2,1,0:T(1,128)} %concatenate.3.payload_ref), custom_call_target="tpu_custom_call" | custom-call | tf_op jit(solution)/shard_map/pallas_call | solution.py:228
  111.7 1.2 %copy.14 = f32[1,256]{1,0:T(1,128)} copy(f32[1,256]{1,0:T(1,128)} %shard_map.66) | data formatting | bytes 2048
  (9 shorter events, 0.0 us)
Async XLA Ops:
  0.0 1.6 %copy-start = (bf16[256,256]{1,0:T(8,128)(2,1)S(1)}, bf16[256,256]{1,0:T(8,128)(2,1)}, u32[]{:S(2)}) copy-start(bf16[256,256]{1,0:T(8,128)(2,1)} %param.7) | copy-start | bytes 393220
  1.6 1.2 %copy-start.1 = (bf16[6,256,512]{2,1,0:T(8,128)(2,1)}, bf16[6,256,512]{2,1,0:T(8,128)(2,1)S(1)}, u32[]{:S(2)}) copy-start(bf16[6,256,512]{2,1,0:T(8,128)(2,1)S(1)} %fusion.46.kernels_ref) | copy-start | bytes 4718596
  2.7 68.0 %copy-start.4 = (s32[1,1,8]{2,1,0:T(1,128)S(1)}, s32[1,1,8]{2,1,0:T(1,128)}, u32[]{:S(2)}) copy-start(s32[1,1,8]{2,1,0:T(1,128)} %param.8) | copy-start | bytes 100
  2.7 68.0 %copy-start.3 = (s32[8192]{0:T(1024)S(1)}, s32[8192]{0:T(1024)}, u32[]{:S(2)}) copy-start(s32[8192]{0:T(1024)} %param.11) | copy-start | bytes 98308
  67.6 6.5 %collective-permute-start = (bf16[4096,256]{1,0:T(8,128)(2,1)}, bf16[4096,256]{1,0:T(8,128)(2,1)S(1)}, u32[]{:S(2)}, u32[]{:S(2)}) collective-permute-start(bf16[4096,256]{1,0:T(8,128)(2,1)} %bitcast.41), channel_id=1, source_target_pairs={{0,128},{128,0},{1,129},{129,1},{2,130},{130,2},{3,131},{131,3},{4... | collective-permute-start | bytes 6291464 | tf_op jit(solution)/shard_map/ppermute | solution.py:72
  74.1 1.3 %copy-start.2 = (bf16[4096,256]{1,0:T(8,128)(2,1)}, bf16[4096,256]{1,0:T(8,128)(2,1)S(1)}, u32[]{:S(2)}) copy-start(bf16[4096,256]{1,0:T(8,128)(2,1)S(1)} %collective-permute-done.other_ref) | copy-start | bytes 6291460

commit v13 on v12

--- a/solution.py
+++ b/solution.py
@@ -334,6 +334,44 @@
     for step in range(1, n_dz):
         z_copy((dz + step) % n_dz, dz).start()
 
+    count_frames = frames_ref.shape[0]
+
+    def to_left():
+        return pltpu.make_async_remote_copy(
+            src_ref=frames_ref.at[pl.ds(0, RAD)],
+            dst_ref=halo_right,
+            send_sem=halo_send.at[0],
+            recv_sem=halo_recv.at[1],
+            device_id=dev_peer(dev - 1),
+            device_id_type=pl.DeviceIdType.MESH,
+        )
+
+    def to_right():
+        return pltpu.make_async_remote_copy(
+            src_ref=frames_ref.at[pl.ds(count_frames - RAD, RAD)],
+            dst_ref=halo_left,
+            send_sem=halo_send.at[1],
+            recv_sem=halo_recv.at[0],
+            device_id=dev_peer(dev + 1),
+            device_id_type=pl.DeviceIdType.MESH,
+        )
+
+    @pl.when(has_left)
+    def _():
+        to_left().start()
+
+    @pl.when(has_right)
+    def _():
+        to_right().start()
+
+    @pl.when(jnp.logical_not(has_left))
+    def _():
+        halo_left[...] = jnp.zeros(halo_left.shape, halo_left.dtype)
+
+    @pl.when(jnp.logical_not(has_right))
+    def _():
+        halo_right[...] = jnp.zeros(halo_right.shape, halo_right.dtype)
+
     def y_copy(direction, row, chunk):
         slot = row * n_dz + chunk
         target = up if direction == 0 else down
@@ -359,102 +397,6 @@
 
     for direction in (0, 1):
         y_own(direction).start()
-    count_frames = frames_ref.shape[0]
-
-    def to_left():
-        return pltpu.make_async_remote_copy(
-            src_ref=frames_ref.at[pl.ds(0, RAD)],
-            dst_ref=halo_right,
-            send_sem=halo_send.at[0],
-            recv_sem=halo_recv.at[1],
-            device_id=dev_peer(dev - 1),
-            device_id_type=pl.DeviceIdType.MESH,
-        )
-
-    def to_right():
-        return pltpu.make_async_remote_copy(
-            src_ref=frames_ref.at[pl.ds(count_frames - RAD, RAD)],
-            dst_ref=halo_left,
-            send_sem=halo_send.at[1],
-            recv_sem=halo_recv.at[0],
-            device_id=dev_peer(dev + 1),
-            device_id_type=pl.DeviceIdType.MESH,
-        )
-
-    @pl.when(has_left)
-    def _():
-        to_left().start()
-
-    @pl.when(has_right)
-    def _():
-        to_right().start()
-
-    @pl.when(jnp.logical_not(has_left))
-    def _():
-        halo_left[...] = jnp.zeros(halo_left.shape, halo_left.dtype)
-
-    @pl.when(jnp.logical_not(has_right))
-    def _():
-        halo_right[...] = jnp.zeros(halo_right.shape, halo_right.dtype)
-
-    @pl.when(has_left)
-    def _():
-        to_right_of_left = pltpu.make_async_remote_copy(
-            src_ref=frames_ref.at[pl.ds(0, RAD)],
-            dst_ref=halo_left,
-            send_sem=halo_send.at[1],
-            recv_sem=halo_recv.at[0],
-            device_id=dev_peer(dev - 1),
-            device_id_type=pl.DeviceIdType.MESH,
-        )
-        to_right_of_left.wait_recv()
-        to_left().wait_send()
-
-    @pl.when(has_right)
-    def _():
-        to_left_of_right = pltpu.make_async_remote_copy(
-            src_ref=frames_ref.at[pl.ds(0, RAD)],
-            dst_ref=halo_right,
-            send_sem=halo_send.at[0],
-            recv_sem=halo_recv.at[1],
-            device_id=dev_peer(dev + 1),
-            device_id_type=pl.DeviceIdType.MESH,
-        )
-        to_left_of_right.wait_recv()
-        to_right().wait_send()
-
-    weights = retention_weights()
-
-    row_block = 32
-
-    def smooth_rows(block, carry):
-        rows = pl.ds(pl.multiple_of(block * row_block, row_block), row_block)
-
-        def padded_frame(place):
-            if place < RAD:
-                return halo_left[place, rows, :]
-            if place < RAD + count_frames:
-                return frames_ref[place - RAD, rows, :]
-            return halo_right[place - RAD - count_frames, rows, :]
-
-        for frame in range(count_frames):
-            total = weights[0] * padded_frame(frame).astype(jnp.float32)
-            for offset in range(1, 2 * RAD + 1):
-                total = total + weights[offset] * padded_frame(frame + offset).astype(jnp.float32)
-            own_scans[frame, rows, :] = total.astype(own_scans.dtype)
-        return carry
-
-    lax.fori_loop(0, own_scans.shape[1] // row_block, smooth_rows, 0)
-
-    swap = pltpu.make_async_remote_copy(
-        src_ref=own_scans,
-        dst_ref=partner_scans,
-        send_sem=swap_send,
-        recv_sem=swap_recv,
-        device_id=(partner_section, grp, dy, dz),
-        device_id_type=pl.DeviceIdType.MESH,
-    )
-    swap.start()
     for step in range(1, n_dz):
         source = (dz + n_dz - step) % n_dz
         z_copy(source, source).wait_recv()
@@ -464,6 +406,64 @@
     for step in range(1, n_dz):
         z_copy((dz + step) % n_dz, dz).wait_send()
 
+    @pl.when(has_left)
+    def _():
+        to_right_of_left = pltpu.make_async_remote_copy(
+            src_ref=frames_ref.at[pl.ds(0, RAD)],
+            dst_ref=halo_left,
+            send_sem=halo_send.at[1],
+            recv_sem=halo_recv.at[0],
+            device_id=dev_peer(dev - 1),
+            device_id_type=pl.DeviceIdType.MESH,
+        )
+        to_right_of_left.wait_recv()
+        to_left().wait_send()
+
+    @pl.when(has_right)
+    def _():
+        to_left_of_right = pltpu.make_async_remote_copy(
+            src_ref=frames_ref.at[pl.ds(0, RAD)],
+            dst_ref=halo_right,
+            send_sem=halo_send.at[0],
+            recv_sem=halo_recv.at[1],
+            device_id=dev_peer(dev + 1),
+            device_id_type=pl.DeviceIdType.MESH,
+        )
+        to_left_of_right.wait_recv()
+        to_right().wait_send()
+
+    weights = retention_weights()
+
+    row_block = 32
+
+    def smooth_rows(block, carry):
+        rows = pl.ds(pl.multiple_of(block * row_block, row_block), row_block)
+
+        def padded_frame(place):
+            if place < RAD:
+                return halo_left[place, rows, :]
+            if place < RAD + count_frames:
+                return frames_ref[place - RAD, rows, :]
+            return halo_right[place - RAD - count_frames, rows, :]
+
+        for frame in range(count_frames):
+            total = weights[0] * padded_frame(frame).astype(jnp.float32)
+            for offset in range(1, 2 * RAD + 1):
+                total = total + weights[offset] * padded_frame(frame + offset).astype(jnp.float32)
+            own_scans[frame, rows, :] = total.astype(own_scans.dtype)
+        return carry
+
+    lax.fori_loop(0, own_scans.shape[1] // row_block, smooth_rows, 0)
+
+    swap = pltpu.make_async_remote_copy(
+        src_ref=own_scans,
+        dst_ref=partner_scans,
+        send_sem=swap_send,
+        recv_sem=swap_recv,
+        device_id=(partner_section, grp, dy, dz),
+        device_id_type=pl.DeviceIdType.MESH,
+    )
+    swap.start()
     relay = n_dz // 2
     for chunk in range(n_dz):
         y_copy(0, down, chunk).wait_recv()

time: 113 us -> 105 us (0.929)
  Pallas kernels: 96.8 us -> 90.3 us
  starting transfers between devices: 2.47 us -> 0.23 us
    pallas_call x1, Pallas kernels: 64.9 us -> 56.8 us  [frame_work(): pl.pallas_call(functools.partial(frame_kernel, sizes), out_shape=(jax.Sha...]
    pallas_call x1, Pallas kernels: 9.58 us -> 13.2 us  [score_pairs(): pl.pallas_call(score_kernel, grid_spec=grid_spec, out_shape=jax.ShapeDtyp...]
    ppermute x1, starting transfers between devices: 2.47 us -> 0.23 us  [on_device(): lax.ppermute(my_rows, 'section', [(i, (i + 1) % section_count) for i in r...]
    pallas_call x1, Pallas kernels: 22.3 us -> 20.3 us  [reduce_owned(): pl.pallas_call(functools.partial(reduce_kernel, sizes), out_shape=jax.Sha...]
where the time goes in v13:
time: 105 us; the launch traced here: 104 us
  Pallas kernels  90.3 us (86%)
  local copies, waits for them, and re-layouts  5.57 us (5%)
  other arithmetic  2.89 us (3%)
  waiting for transfers between devices  2.88 us (3%)
  matrix products  1.74 us (2%)
    pallas_call x1, Pallas kernels, frame_work(): pl.pallas_call(functools.partial(frame_kernel, sizes), out_shape=(jax.Sha...  56.8 us
    pallas_call x1, Pallas kernels, reduce_owned(): pl.pallas_call(functools.partial(reduce_kernel, sizes), out_shape=jax.Sha...  20.3 us
    pallas_call x1, Pallas kernels, score_pairs(): pl.pallas_call(score_kernel, grid_spec=grid_spec, out_shape=jax.ShapeDtyp...  13.2 us
    unnamed x11, local copies, waits for them, and re-layouts  3.02 us
    ppermute x1, waiting for transfers between devices, on_device(): lax.ppermute(my_rows, 'section', [(i, (i + 1) % section_count) for i in r...  2.88 us
  transfers between devices with their start and end apart: 1, of which 1 were waited for; matrix products, arithmetic and copies ran while one was open for 1% of the time, Pallas kernels for 0%

profile of v13, /device:TPU:1, one launch (start us, length us, event | category | flops | bytes accessed | tf_op | source)
XLA Modules:
  0.0 104.4 jit_solution(9956116217260559405)
XLA Ops:
  0.0 0.0 copy-start
  0.0 0.2 fusion.47
  0.3 0.3 fusion.42
  0.5 0.3 fusion.43
  0.8 0.3 fusion.44
  1.0 0.3 fusion.45
  1.3 0.3 fusion.46.kernels_ref
  1.6 0.0 copy-start.1
  1.6 0.7 constant_dynamic-slice_fusion.half_ref
  2.3 0.5 copy-done.1
  2.7 56.8 %shard_map.64 = (bf16[32,128,256]{2,1,0:T(8,128)(2,1)}, bf16[6,16,256,256]{3,2,1,0:T(8,128)(2,1)}) custom-call(bf16[16,256,256]{2,1,0:T(8,128)(2,1)} %bitcast.43, bf16[6,256,512]{2,1,0:T(8,128)(2,1)} %copy-done.1, bf16[128,256]{1,0:T(8,128)(2,1)} %constant_dynamic-slice_fusion.half_ref), custom_call_target="tpu_custom_call" | custom-call | tf_op jit(solution)/shard_map/pallas_call | solution.py:508
  59.6 0.2 collective-permute-start
  60.5 0.0 copy-done.4
  60.5 0.0 copy-done.3
  60.5 0.6 gather_fusion
  61.1 0.1 add_select_fusion.1
  61.2 2.9 %collective-permute-done.other_ref = bf16[4096,256]{1,0:T(8,128)(2,1)S(1)} collective-permute-done((bf16[4096,256]{1,0:T(8,128)(2,1)}, bf16[4096,256]{1,0:T(8,128)(2,1)S(1)}, u32[]{:S(2)}, u32[]{:S(2)}) %collective-permute-start) | collective-permute-done | bytes 2097184 | tf_op jit(solution)/shard_map/ppermute | solution.py:72
  64.0 1.3 %copy-done.2 = bf16[4096,256]{1,0:T(8,128)(2,1)} copy-done((bf16[4096,256]{1,0:T(8,128)(2,1)}, bf16[4096,256]{1,0:T(8,128)(2,1)S(1)}, u32[]{:S(2)}) %copy-start.2) | copy-done | bytes 2097176
  65.4 13.2 %shard_map.65 = f32[8,1,128]{2,1,0:T(1,128)} custom-call(s32[8]{0:T(128)} %bitcast.48, s32[8]{0:T(128)} %bitcast.47, s32[1]{0:T(128)} %bitcast.40.count_ref, s32[1]{0:T(128)} %bitcast.7.section_ref, bf16[6,16,256,256]{3,2,1,0:T(8,128)(2,1)} %get-tuple-element.7.wave_ref, bf16[4096,256]{1,0:T(8,128)(2,1)} %bitcast.42, bf16[4096,256]{1,0:T(8,128)(2,1)} %copy-done.2), custom_call_target="tpu_custom_call" | custom-call | tf_op jit(solution)/shard_map/pallas_call | solution.py:591
  78.6 1.3 %reduce_sum.9 = f32[]{:T(128)} reduce(f32[8,1,128]{2,1,0:T(1,128)} %shard_map.65, f32[]{:T(128)} %constant.114.clone.1), dimensions={0,1,2}, to_apply=%region_0.1 | reduce | flops 1023 | bytes 4104 | tf_op jit(solution)/shard_map/reduce_sum | solution.py:100
  79.8 1.7 %fusion.40 = f32[64,128]{1,0:T(8,128)S(1)} fusion(s32[1024]{0:T(1024)S(1)} %get-tuple-element.10, f32[1024]{0:T(1024)} %bitcast.46, s32[1024]{0:T(1024)S(1)} %get-tuple-element.9), kind=kOutput, calls=%fused_computation.55 | convolution fusion | flops 100925440 | bytes 45056 | tf_op jit(solution)/shard_map/ka,kb->ab/dot_general | solution.py:92
  81.6 1.3 %concatenate.3.payload_ref = f32[32,1,384]{2,1,0:T(1,128)} pad(f32[32,1,256]{2,1,0:T(1,128)S(1)} %bitcast.45, f32[]{:T(128)} %reduce_sum.9), padding=0_0x0_0x0_128 | pad | bytes 81924 | tf_op jit(solution)/shard_map/concatenate | solution.py:101
  82.9 20.3 %shard_map.66 = f32[1,256]{1,0:T(1,128)} custom-call(f32[32,1,384]{2,1,0:T(1,128)} %concatenate.3.payload_ref), custom_call_target="tpu_custom_call" | custom-call | tf_op jit(solution)/shard_map/pallas_call | solution.py:228
  103.2 1.2 %copy.14 = f32[1,256]{1,0:T(1,128)} copy(f32[1,256]{1,0:T(1,128)} %shard_map.66) | data formatting | bytes 2048
  (9 shorter events, 0.0 us)
Async XLA Ops:
  0.0 1.6 %copy-start = (bf16[256,256]{1,0:T(8,128)(2,1)S(1)}, bf16[256,256]{1,0:T(8,128)(2,1)}, u32[]{:S(2)}) copy-start(bf16[256,256]{1,0:T(8,128)(2,1)} %param.7) | copy-start | bytes 393220
  1.6 1.2 %copy-start.1 = (bf16[6,256,512]{2,1,0:T(8,128)(2,1)}, bf16[6,256,512]{2,1,0:T(8,128)(2,1)S(1)}, u32[]{:S(2)}) copy-start(bf16[6,256,512]{2,1,0:T(8,128)(2,1)S(1)} %fusion.46.kernels_ref) | copy-start | bytes 4718596
  2.7 57.7 %copy-start.4 = (s32[1,1,8]{2,1,0:T(1,128)S(1)}, s32[1,1,8]{2,1,0:T(1,128)}, u32[]{:S(2)}) copy-start(s32[1,1,8]{2,1,0:T(1,128)} %param.8) | copy-start | bytes 100
  2.7 57.8 %copy-start.3 = (s32[8192]{0:T(1024)S(1)}, s32[8192]{0:T(1024)}, u32[]{:S(2)}) copy-start(s32[8192]{0:T(1024)} %param.11) | copy-start | bytes 98308
  59.6 4.5 %collective-permute-start = (bf16[4096,256]{1,0:T(8,128)(2,1)}, bf16[4096,256]{1,0:T(8,128)(2,1)S(1)}, u32[]{:S(2)}, u32[]{:S(2)}) collective-permute-start(bf16[4096,256]{1,0:T(8,128)(2,1)} %bitcast.41), channel_id=1, source_target_pairs={{0,128},{128,0},{1,129},{129,1},{2,130},{130,2},{3,131},{131,3},{4... | collective-permute-start | bytes 6291464 | tf_op jit(solution)/shard_map/ppermute | solution.py:72
  64.0 1.3 %copy-start.2 = (bf16[4096,256]{1,0:T(8,128)(2,1)}, bf16[4096,256]{1,0:T(8,128)(2,1)S(1)}, u32[]{:S(2)}) copy-start(bf16[4096,256]{1,0:T(8,128)(2,1)S(1)} %collective-permute-done.other_ref) | copy-start | bytes 6291460

commit v14 on v13

--- a/solution.py
+++ b/solution.py
@@ -535,8 +535,10 @@
     return rows_out.reshape(n_dy * n_dz * rows, channels), wave
 
 
-def score_kernel(tile_ref, block_ref, count_ref, section_ref, wave_ref, mine_ref, other_ref, out_ref):
-    slot = pl.program_id(0)
+def score_kernel(
+    order_ref, tile_ref, block_ref, count_ref, section_ref, wave_ref, mine_ref, other_ref, out_ref
+):
+    slot = order_ref[pl.program_id(0)]
     live = slot < count_ref[0]
     mine = block_ref[slot] % 2 == section_ref[0]
 
@@ -568,31 +570,32 @@
 def score_pairs(wavelet_stack, my_rows, other_rows, tile_ids, block_ids, live_pairs, section_index):
     slots = tile_ids.shape[0]
     scales, frames_local, mob_local, channels = wavelet_stack.shape
-
-    def last_live(k, count_ref):
-        return jnp.minimum(k, count_ref[0] - 1)
-
-    def rows_block(k, t, b, c, s):
-        return (b[last_live(k, c)] // 2, 0)
+    slot_ids = jnp.arange(slots, dtype=jnp.int32)
+    keys = jnp.where(slot_ids < live_pairs, tile_ids * slots + slot_ids, (mob_local // TM + 1) * slots + slot_ids)
+    order = jnp.argsort(keys).astype(jnp.int32)
+
+    def visited(k, o, c):
+        return o[jnp.minimum(k, c[0] - 1)]
 
     grid_spec = pltpu.PrefetchScalarGridSpec(
-        num_scalar_prefetch=4,
+        num_scalar_prefetch=5,
         grid=(slots,),
         in_specs=[
             pl.BlockSpec(
                 (scales, frames_local, TM, channels),
-                lambda k, t, b, c, s: (0, 0, t[last_live(k, c)], 0),
+                lambda k, o, t, b, c, s: (0, 0, t[visited(k, o, c)], 0),
             ),
-            pl.BlockSpec((PB, channels), rows_block),
-            pl.BlockSpec((PB, channels), rows_block),
+            pl.BlockSpec((PB, channels), lambda k, o, t, b, c, s: (b[visited(k, o, c)] // 2, 0)),
+            pl.BlockSpec((PB, channels), lambda k, o, t, b, c, s: (b[visited(k, o, c)] // 2, 0)),
         ],
-        out_specs=pl.BlockSpec((1, 1, PB), lambda k, t, b, c, s: (k, 0, 0)),
+        out_specs=pl.BlockSpec((1, 1, PB), lambda k, o, t, b, c, s: (o[k], 0, 0)),
     )
     out = pl.pallas_call(
         score_kernel,
         grid_spec=grid_spec,
         out_shape=jax.ShapeDtypeStruct((slots, 1, PB), jnp.float32),
     )(
+        order,
         tile_ids,
         block_ids,
         live_pairs.reshape(1),

time: 105 us -> 104 us (level)
  Pallas kernels: 90.3 us -> 89.2 us
    pallas_call x1, Pallas kernels: 13.2 us -> 6.94 us  [score_pairs(): pl.pallas_call(score_kernel, grid_spec=grid_spec, out_shape=jax.ShapeDtyp...]
    pallas_call x1, Pallas kernels: 20.3 us -> 25.4 us  [reduce_owned(): pl.pallas_call(functools.partial(reduce_kernel, sizes), out_shape=jax.Sha...]
    unnamed x11 -> x13, local copies, waits for them, and re-layouts: 3.02 us -> 3.05 us
  transfers between devices with their start and end apart: 1 -> 1, of which waited for: 1 -> 1; matrix products, arithmetic and copies ran while one was open for 1% -> 2% of each run, Pallas kernels for 0% -> 0%
where the time goes in v14:
time: 104 us; the launch traced here: 103 us
  Pallas kernels  89.2 us (86%)
  local copies, waits for them, and re-layouts  5.61 us (5%)
  other arithmetic  3.92 us (4%)
  waiting for transfers between devices  1.84 us (2%)
  matrix products  1.74 us (2%)
    pallas_call x1, Pallas kernels, frame_work(): pl.pallas_call(functools.partial(frame_kernel, sizes), out_shape=(jax.Sha...  56.9 us
    pallas_call x1, Pallas kernels, reduce_owned(): pl.pallas_call(functools.partial(reduce_kernel, sizes), out_shape=jax.Sha...  25.4 us
    pallas_call x1, Pallas kernels, score_pairs(): pl.pallas_call(score_kernel, grid_spec=grid_spec, out_shape=jax.ShapeDtyp...  6.94 us
    unnamed x13, local copies, waits for them, and re-layouts  3.05 us
  transfers between devices with their start and end apart: 1, of which 1 were waited for; matrix products, arithmetic and copies ran while one was open for 2% of the time, Pallas kernels for 0%

profile of v14, /device:TPU:1, one launch (start us, length us, event | category | flops | bytes accessed | tf_op | source)
XLA Modules:
  0.0 103.4 jit_solution(4640694967171315811)
XLA Ops:
  0.0 0.0 copy-start
  0.0 0.2 fusion.47
  0.3 0.3 fusion.42
  0.5 0.3 fusion.43
  0.8 0.3 fusion.44
  1.0 0.3 fusion.45
  1.3 0.3 fusion.46.kernels_ref
  1.6 0.0 copy-start.1
  1.6 0.7 constant_dynamic-slice_fusion.half_ref
  2.3 0.5 copy-done.1
  2.8 56.9 %shard_map.64 = (bf16[32,128,256]{2,1,0:T(8,128)(2,1)}, bf16[6,16,256,256]{3,2,1,0:T(8,128)(2,1)}) custom-call(bf16[16,256,256]{2,1,0:T(8,128)(2,1)} %bitcast.46, bf16[6,256,512]{2,1,0:T(8,128)(2,1)} %copy-done.1, bf16[128,256]{1,0:T(8,128)(2,1)} %constant_dynamic-slice_fusion.half_ref), custom_call_target="tpu_custom_call" | custom-call | tf_op jit(solution)/shard_map/pallas_call | solution.py:508
  59.6 0.2 collective-permute-start
  60.5 0.0 copy-done.5
  60.5 1.0 sort.17
  61.6 0.6 gather_fusion
  62.2 0.1 add_select_fusion.1
  62.3 1.8 %collective-permute-done.other_ref = bf16[4096,256]{1,0:T(8,128)(2,1)S(1)} collective-permute-done((bf16[4096,256]{1,0:T(8,128)(2,1)}, bf16[4096,256]{1,0:T(8,128)(2,1)S(1)}, u32[]{:S(2)}, u32[]{:S(2)}) %collective-permute-start) | collective-permute-done | bytes 2097184 | tf_op jit(solution)/shard_map/ppermute | solution.py:72
  64.1 1.3 %copy-done.2 = bf16[4096,256]{1,0:T(8,128)(2,1)} copy-done((bf16[4096,256]{1,0:T(8,128)(2,1)}, bf16[4096,256]{1,0:T(8,128)(2,1)S(1)}, u32[]{:S(2)}) %copy-start.2) | copy-done | bytes 2097176
  65.4 6.9 %shard_map.65 = f32[8,1,128]{2,1,0:T(1,128)} custom-call(s32[8]{0:T(128)} %get-tuple-element.8.order_ref, s32[8]{0:T(128)} %bitcast.51, s32[8]{0:T(128)} %bitcast.50, s32[1]{0:T(128)} %bitcast.43.count_ref, s32[1]{0:T(128)} %bitcast.8.section_ref, bf16[6,16,256,256]{3,2,1,0:T(8,128)(2,1)} %get-tuple-element.9.wave_ref, bf16[4096,256]{1,0:T(8,128)(2,1)} %bitcast.45, ...), custom_call_target="tpu_custom_call" | custom-call | tf_op jit(solution)/shard_map/pallas_call | solution.py:593
  72.4 1.3 %reduce_sum.9 = f32[]{:T(128)} reduce(f32[8,1,128]{2,1,0:T(1,128)} %shard_map.65, f32[]{:T(128)} %constant.118.clone.1), dimensions={0,1,2}, to_apply=%region_1.2 | reduce | flops 1023 | bytes 4104 | tf_op jit(solution)/shard_map/reduce_sum | solution.py:100
  73.7 1.7 %fusion.40 = f32[64,128]{1,0:T(8,128)S(1)} fusion(s32[1024]{0:T(1024)S(1)} %get-tuple-element.12, f32[1024]{0:T(1024)} %bitcast.49, s32[1024]{0:T(1024)S(1)} %get-tuple-element.11), kind=kOutput, calls=%fused_computation.55 | convolution fusion | flops 100925440 | bytes 45056 | tf_op jit(solution)/shard_map/ka,kb->ab/dot_general | solution.py:92
  75.4 1.3 %concatenate.3.payload_ref = f32[32,1,384]{2,1,0:T(1,128)} pad(f32[32,1,256]{2,1,0:T(1,128)S(1)} %bitcast.48, f32[]{:T(128)} %reduce_sum.9), padding=0_0x0_0x0_128 | pad | bytes 81924 | tf_op jit(solution)/shard_map/concatenate | solution.py:101
  76.7 25.4 %shard_map.66 = f32[1,256]{1,0:T(1,128)} custom-call(f32[32,1,384]{2,1,0:T(1,128)} %concatenate.3.payload_ref), custom_call_target="tpu_custom_call" | custom-call | tf_op jit(solution)/shard_map/pallas_call | solution.py:228
  102.1 1.2 %copy.14 = f32[1,256]{1,0:T(1,128)} copy(f32[1,256]{1,0:T(1,128)} %shard_map.66) | data formatting | bytes 2048
  (14 shorter events, 0.1 us)
Async XLA Ops:
  0.0 1.6 %copy-start = (bf16[256,256]{1,0:T(8,128)(2,1)S(1)}, bf16[256,256]{1,0:T(8,128)(2,1)}, u32[]{:S(2)}) copy-start(bf16[256,256]{1,0:T(8,128)(2,1)} %param.7) | copy-start | bytes 393220
  1.6 1.2 %copy-start.1 = (bf16[6,256,512]{2,1,0:T(8,128)(2,1)}, bf16[6,256,512]{2,1,0:T(8,128)(2,1)S(1)}, u32[]{:S(2)}) copy-start(bf16[6,256,512]{2,1,0:T(8,128)(2,1)S(1)} %fusion.46.kernels_ref) | copy-start | bytes 4718596
  2.8 57.8 %copy-start.5 = (s32[1,1,8]{2,1,0:T(1,128)S(1)}, s32[1,1,8]{2,1,0:T(1,128)}, u32[]{:S(2)}) copy-start(s32[1,1,8]{2,1,0:T(1,128)} %param.9) | copy-start | bytes 100
  2.8 58.8 %copy-start.4 = (s32[1,1,8]{2,1,0:T(1,128)S(1)}, s32[1,1,8]{2,1,0:T(1,128)}, u32[]{:S(2)}) copy-start(s32[1,1,8]{2,1,0:T(1,128)} %param.8) | copy-start | bytes 100
  2.8 58.8 %copy-start.3 = (s32[8192]{0:T(1024)S(1)}, s32[8192]{0:T(1024)}, u32[]{:S(2)}) copy-start(s32[8192]{0:T(1024)} %param.11) | copy-start | bytes 98308
  59.6 4.5 %collective-permute-start = (bf16[4096,256]{1,0:T(8,128)(2,1)}, bf16[4096,256]{1,0:T(8,128)(2,1)S(1)}, u32[]{:S(2)}, u32[]{:S(2)}) collective-permute-start(bf16[4096,256]{1,0:T(8,128)(2,1)} %bitcast.44), channel_id=1, source_target_pairs={{0,128},{128,0},{1,129},{129,1},{2,130},{130,2},{3,131},{131,3},{4... | collective-permute-start | bytes 6291464 | tf_op jit(solution)/shard_map/ppermute | solution.py:72
  64.1 1.3 %copy-start.2 = (bf16[4096,256]{1,0:T(8,128)(2,1)}, bf16[4096,256]{1,0:T(8,128)(2,1)S(1)}, u32[]{:S(2)}) copy-start(bf16[4096,256]{1,0:T(8,128)(2,1)S(1)} %collective-permute-done.other_ref) | copy-start | bytes 6291460

commit v15 on v14

--- a/solution.py
+++ b/solution.py
@@ -68,10 +68,7 @@
     kernels = mobility_kernels(section_index * mob_local, mob_local, section_index * mob_local)
     half_rows = templates.shape[0] // 2
     my_half = lax.dynamic_slice_in_dim(templates, section_index * half_rows, half_rows, 0)
-    my_rows, wavelet_stack = frame_work(frames[0], kernels, my_half)
-    other_rows = lax.ppermute(
-        my_rows, "section", [(i, (i + 1) % section_count) for i in range(section_count)]
-    )
+    my_rows, other_rows, wavelet_stack = frame_work(frames[0], kernels, my_half)
     slots = pair_block.shape[2]
     live_pairs = pair_count[0, 0, 0]
     block_ids = pair_block[0, 0]
@@ -248,6 +245,7 @@
     kernels_ref,
     half_ref,
     out_ref,
+    other_ref,
     wave_ref,
     halo_left,
     halo_right,
@@ -262,6 +260,8 @@
     halo_recv,
     swap_send,
     swap_recv,
+    pair_send,
+    pair_recv,
 ):
     n_section, n_dy, n_dz = sizes
     n_dev = n_dy * n_dz
@@ -321,6 +321,18 @@
     own = pltpu.make_async_copy(half_ref, out_ref.at[dev], own_sem)
     own.start()
 
+    def pair_copy(slot, source_ref):
+        return pltpu.make_async_remote_copy(
+            src_ref=source_ref,
+            dst_ref=other_ref.at[slot],
+            send_sem=pair_send.at[slot],
+            recv_sem=pair_recv.at[slot],
+            device_id=(partner_section, grp, dy, dz),
+            device_id_type=pl.DeviceIdType.MESH,
+        )
+
+    pair_copy(dev, half_ref).start()
+
     def z_copy(target, source):
         return pltpu.make_async_remote_copy(
             src_ref=half_ref,
@@ -402,6 +414,7 @@
         z_copy(source, source).wait_recv()
         for direction in (0, 1):
             y_copy(direction, dy, source).start()
+        pair_copy(dy * n_dz + source, out_ref.at[dy * n_dz + source]).start()
     own.wait()
     for step in range(1, n_dz):
         z_copy((dz + step) % n_dz, dz).wait_send()
@@ -469,9 +482,11 @@
         y_copy(0, down, chunk).wait_recv()
         if chunk < relay:
             y_copy(0, down, chunk).start()
+        pair_copy(down * n_dz + chunk, out_ref.at[down * n_dz + chunk]).start()
         y_copy(1, up, chunk).wait_recv()
         if chunk >= relay:
             y_copy(1, up, chunk).start()
+        pair_copy(up * n_dz + chunk, out_ref.at[up * n_dz + chunk]).start()
     swap.wait()
 
     half = own_scans.shape[1]
@@ -491,6 +506,7 @@
     opposite = (dy + 2) % n_dy
     for chunk in range(n_dz):
         y_copy(0, opposite, chunk).wait_recv()
+        pair_copy(opposite * n_dz + chunk, out_ref.at[opposite * n_dz + chunk]).start()
     for direction in (0, 1):
         for chunk in range(n_dz):
             y_copy(direction, dy, chunk).wait_send()
@@ -498,6 +514,10 @@
         y_copy(0, down, chunk).wait_send()
     for chunk in range(relay, n_dz):
         y_copy(1, up, chunk).wait_send()
+    for slot in range(n_dev):
+        pair_copy(slot, half_ref).wait_recv()
+    for slot in range(n_dev):
+        pair_copy(slot, half_ref).wait_send()
 
 
 def frame_work(frames, kernels, half):
@@ -505,14 +525,15 @@
     n_section, n_dy, n_dz = sizes
     rows, channels = half.shape
     count_frames, mob_local, _ = frames.shape
-    rows_out, wave = pl.pallas_call(
+    rows_out, other_out, wave = pl.pallas_call(
         functools.partial(frame_kernel, sizes),
         out_shape=(
+            jax.ShapeDtypeStruct((n_dy * n_dz, rows, channels), half.dtype),
             jax.ShapeDtypeStruct((n_dy * n_dz, rows, channels), half.dtype),
             jax.ShapeDtypeStruct((SCALES, count_frames, mob_local, channels), jnp.bfloat16),
         ),
         in_specs=[pl.BlockSpec(memory_space=pltpu.VMEM)] * 3,
-        out_specs=(pl.BlockSpec(memory_space=pltpu.VMEM), pl.BlockSpec(memory_space=pltpu.VMEM)),
+        out_specs=(pl.BlockSpec(memory_space=pltpu.VMEM),) * 3,
         scratch_shapes=[
             pltpu.VMEM((RAD, mob_local, channels), frames.dtype),
             pltpu.VMEM((RAD, mob_local, channels), frames.dtype),
@@ -527,12 +548,18 @@
             pltpu.SemaphoreType.DMA((2,)),
             pltpu.SemaphoreType.DMA(()),
             pltpu.SemaphoreType.DMA(()),
+            pltpu.SemaphoreType.DMA((n_dy * n_dz,)),
+            pltpu.SemaphoreType.DMA((n_dy * n_dz,)),
         ],
         compiler_params=pltpu.CompilerParams(
             collective_id=1, has_side_effects=True, vmem_limit_bytes=56 * 1024 * 1024
         ),
     )(frames, kernels, half)
-    return rows_out.reshape(n_dy * n_dz * rows, channels), wave
+    return (
+        rows_out.reshape(n_dy * n_dz * rows, channels),
+        other_out.reshape(n_dy * n_dz * rows, channels),
+        wave,
+    )
 
 
 def score_kernel(

time: 104 us -> 104 us (level)
  Pallas kernels: 89.2 us -> 92.9 us
  waiting for transfers between devices: 1.84 us -> 0 us
  local copies, waits for them, and re-layouts: 5.61 us -> 4.27 us
    pallas_call x1, Pallas kernels: 6.94 us -> 13.1 us  [score_pairs(): pl.pallas_call(score_kernel, grid_spec=grid_spec, out_shape=jax.ShapeDtyp...]
    pallas_call x1, Pallas kernels: 25.4 us -> 20.2 us  [reduce_owned(): pl.pallas_call(functools.partial(reduce_kernel, sizes), out_shape=jax.Sha...]
    pallas_call x1, Pallas kernels: 56.9 us -> 59.6 us  [frame_work(): pl.pallas_call(functools.partial(frame_kernel, sizes), out_shape=(jax.Sha...]
    ppermute x1 -> x0, waiting for transfers between devices: 1.84 us -> none  [on_device(): lax.ppermute(my_rows, 'section', [(i, (i + 1) % section_count) for i in r...]
    unnamed x13 -> x11, local copies, waits for them, and re-layouts: 3.05 us -> 1.73 us
  transfers between devices with their start and end apart: 1 -> 0, of which waited for: 1 -> 0; matrix products, arithmetic and copies ran while one was open for 2% -> 0% of each run, Pallas kernels for 0% -> 0%
where the time goes in v15:
time: 104 us
  Pallas kernels  92.9 us (89%)
  local copies, waits for them, and re-layouts  4.27 us (4%)
  other arithmetic  3.94 us (4%)
  matrix products  1.74 us (2%)
    pallas_call x1, Pallas kernels, frame_work(): pl.pallas_call(functools.partial(frame_kernel, sizes), out_shape=(jax.Sha...  59.6 us
    pallas_call x1, Pallas kernels, reduce_owned(): pl.pallas_call(functools.partial(reduce_kernel, sizes), out_shape=jax.Sha...  20.2 us
    pallas_call x1, Pallas kernels, score_pairs(): pl.pallas_call(score_kernel, grid_spec=grid_spec, out_shape=jax.ShapeDtyp...  13.1 us

profile of v15, /device:TPU:1, one launch (start us, length us, event | category | flops | bytes accessed | tf_op | source)
XLA Modules:
  0.0 103.6 jit_solution(13434121360339895513)
XLA Ops:
  0.0 0.0 copy-start
  0.0 0.2 fusion.47
  0.3 0.3 fusion.42
  0.5 0.3 fusion.43
  0.8 0.3 fusion.44
  1.0 0.3 fusion.45
  1.3 0.3 fusion.46.kernels_ref
  1.6 0.0 copy-start.1
  1.6 0.0 copy-done
  1.6 0.7 constant_dynamic-slice_fusion.half_ref
  2.3 0.5 copy-done.1
  2.7 59.6 %shard_map.64 = (bf16[32,128,256]{2,1,0:T(8,128)(2,1)}, bf16[32,128,256]{2,1,0:T(8,128)(2,1)}, bf16[6,16,256,256]{3,2,1,0:T(8,128)(2,1)}) custom-call(bf16[16,256,256]{2,1,0:T(8,128)(2,1)} %bitcast.47, bf16[6,256,512]{2,1,0:T(8,128)(2,1)} %copy-done.1, bf16[128,256]{1,0:T(8,128)(2,1)} %constant_dynamic-slice_fusion.half_ref), custom_call_target="tpu_custom_call" | custom-call | tf_op jit(solution)/shard_map/pallas_call | solution.py:528
  63.0 0.0 copy-done.3
  63.0 1.0 %sort.17 = (s32[8]{0:T(128)}, s32[8]{0:T(128)}) sort(s32[8]{0:T(128)S(1)} %compare_select_fusion.2, s32[8]{0:T(128)S(1)} %iota.32), dimensions={0}, to_apply=%region_0.1 | sort | flops 24 | bytes 128 | tf_op jit(solution)/shard_map/jit(argsort)/sort | solution.py:602
  64.1 13.1 %shard_map.65 = f32[8,1,128]{2,1,0:T(1,128)} custom-call(s32[8]{0:T(128)} %get-tuple-element.9.order_ref, s32[8]{0:T(128)} %bitcast.51, s32[8]{0:T(128)} %bitcast.52, s32[1]{0:T(128)} %bitcast.44.count_ref, s32[1]{0:T(128)} %bitcast.8.section_ref, bf16[6,16,256,256]{3,2,1,0:T(8,128)(2,1)} %get-tuple-element.10.wave_ref, bf16[4096,256]{1,0:T(8,128)(2,1)} %bitcast.45, ...), custom_call_target="tpu_custom_call" | custom-call | tf_op jit(solution)/shard_map/pallas_call | solution.py:620
  77.2 0.0 copy-done.4
  77.2 0.0 copy-done.2
  77.2 0.6 gather_fusion
  77.8 0.1 add_select_fusion.1
  77.9 1.7 %fusion.40 = f32[64,128]{1,0:T(8,128)S(1)} fusion(s32[1024]{0:T(1024)S(1)} %get-tuple-element.14, f32[1024]{0:T(1024)} %bitcast.50, s32[1024]{0:T(1024)S(1)} %get-tuple-element.13), kind=kOutput, calls=%fused_computation.55 | convolution fusion | flops 100925440 | bytes 45056 | tf_op jit(solution)/shard_map/ka,kb->ab/dot_general | solution.py:89
  79.6 1.3 %reduce_sum.9 = f32[]{:T(128)} reduce(f32[8,1,128]{2,1,0:T(1,128)} %shard_map.65, f32[]{:T(128)} %constant.118.clone.1), dimensions={0,1,2}, to_apply=%region_1.2 | reduce | flops 1023 | bytes 4104 | tf_op jit(solution)/shard_map/reduce_sum | solution.py:97
  80.9 1.3 %concatenate.3.payload_ref = f32[32,1,384]{2,1,0:T(1,128)} pad(f32[32,1,256]{2,1,0:T(1,128)S(1)} %bitcast.49, f32[]{:T(128)} %reduce_sum.9), padding=0_0x0_0x0_128 | pad | bytes 81924 | tf_op jit(solution)/shard_map/concatenate | solution.py:98
  82.2 20.2 %shard_map.66 = f32[1,256]{1,0:T(1,128)} custom-call(f32[32,1,384]{2,1,0:T(1,128)} %concatenate.3.payload_ref), custom_call_target="tpu_custom_call" | custom-call | tf_op jit(solution)/shard_map/pallas_call | solution.py:225
  102.4 1.2 %copy.14 = f32[1,256]{1,0:T(1,128)} copy(f32[1,256]{1,0:T(1,128)} %shard_map.66) | data formatting | bytes 2048
  (10 shorter events, 0.0 us)
Async XLA Ops:
  0.0 1.6 %copy-start = (bf16[256,256]{1,0:T(8,128)(2,1)S(1)}, bf16[256,256]{1,0:T(8,128)(2,1)}, u32[]{:S(2)}) copy-start(bf16[256,256]{1,0:T(8,128)(2,1)} %param.7) | copy-start | bytes 393220
  1.6 1.2 %copy-start.1 = (bf16[6,256,512]{2,1,0:T(8,128)(2,1)}, bf16[6,256,512]{2,1,0:T(8,128)(2,1)S(1)}, u32[]{:S(2)}) copy-start(bf16[6,256,512]{2,1,0:T(8,128)(2,1)S(1)} %fusion.46.kernels_ref) | copy-start | bytes 4718596
  2.7 60.3 %copy-start.3 = (s32[1,1,8]{2,1,0:T(1,128)S(1)}, s32[1,1,8]{2,1,0:T(1,128)}, u32[]{:S(2)}) copy-start(s32[1,1,8]{2,1,0:T(1,128)} %param.9) | copy-start | bytes 100
  64.1 13.1 %copy-start.4 = (s32[1,1,8]{2,1,0:T(1,128)S(1)}, s32[1,1,8]{2,1,0:T(1,128)}, u32[]{:S(2)}) copy-start(s32[1,1,8]{2,1,0:T(1,128)} %param.8) | copy-start | bytes 100
  64.1 13.1 %copy-start.2 = (s32[8192]{0:T(1024)S(1)}, s32[8192]{0:T(1024)}, u32[]{:S(2)}) copy-start(s32[8192]{0:T(1024)} %param.11) | copy-start | bytes 98308

commit v16 on v15

--- a/solution.py
+++ b/solution.py
@@ -105,83 +105,95 @@
     return reduce_owned(payload)
 
 
-def reduce_kernel(sizes, payload_ref, out_ref, gathered, totals, send_sems, recv_sems, total_send, total_recv):
+def reduce_kernel(
+    sizes,
+    payload_ref,
+    out_ref,
+    mixed,
+    line,
+    line_in,
+    column,
+    column_in,
+    totals,
+    pair_send,
+    pair_recv,
+    z_send,
+    z_recv,
+    y_send,
+    y_recv,
+    total_send,
+    total_recv,
+):
     n_section, n_grp, n_dy, n_dz = sizes
-    n_dev = n_dy * n_dz
     section = lax.axis_index("section")
     grp = lax.axis_index("grp")
     dy = lax.axis_index("dy")
     dz = lax.axis_index("dz")
-    dev = dy * n_dz + dz
-    me = section * n_dev + dev
-    peers = n_section * n_dev
+    partner = (section + 1) % n_section
     owned_width = out_ref.shape[1]
 
     barrier = pltpu.get_barrier_semaphore()
-
-    def greet(index, carry):
-        @pl.when(index != me)
-        def _():
-            pl.semaphore_signal(
-                barrier,
-                inc=1,
-                device_id=(index // n_dev, grp, index % n_dev // n_dz, index % n_dz),
-                device_id_type=pl.DeviceIdType.MESH,
-            )
-
-        return carry
-
-    lax.fori_loop(0, peers, greet, 0)
-    for step in range(1, n_grp):
-        pl.semaphore_signal(
-            barrier,
-            inc=1,
-            device_id=(section, (grp + step) % n_grp, dy, dz),
-            device_id_type=pl.DeviceIdType.MESH,
-        )
-    pl.semaphore_wait(barrier, peers - 1 + n_grp - 1)
-
-    def chunk_copy(index):
-        return pltpu.make_async_remote_copy(
-            src_ref=payload_ref.at[index % n_dev],
-            dst_ref=gathered.at[me],
-            send_sem=send_sems.at[index],
-            recv_sem=recv_sems.at[me],
-            device_id=(index // n_dev, grp, index % n_dev // n_dz, index % n_dz),
-            device_id_type=pl.DeviceIdType.MESH,
-        )
-
-    def send(index, carry):
-        @pl.when(index != me)
-        def _():
-            chunk_copy(index).start()
-
-        return carry
-
-    lax.fori_loop(0, peers, send, 0)
-    gathered[me] = payload_ref[dev]
-
-    def arrive(index, carry):
-        @pl.when(index != me)
-        def _():
-            pltpu.make_async_remote_copy(
-                src_ref=payload_ref.at[0],
-                dst_ref=gathered.at[index],
-                send_sem=send_sems.at[index],
-                recv_sem=recv_sems.at[index],
-                device_id=(index // n_dev, grp, index % n_dev // n_dz, index % n_dz),
-                device_id_type=pl.DeviceIdType.MESH,
-            ).wait_recv()
-            chunk_copy(index).wait_send()
-
-        return carry
-
-    lax.fori_loop(0, peers, arrive, 0)
-
-    def accumulate(index, acc):
-        return acc + gathered[index]
-
-    summed = lax.fori_loop(0, peers, accumulate, jnp.zeros(gathered.shape[1:], jnp.float32))
+    peers = [(partner, grp, dy, dz)]
+    peers += [(section, grp, dy, (dz + step) % n_dz) for step in range(1, n_dz)]
+    peers += [(section, grp, (dy + step) % n_dy, dz) for step in range(1, n_dy)]
+    peers += [(section, (grp + step) % n_grp, dy, dz) for step in range(1, n_grp)]
+    for peer in peers:
+        pl.semaphore_signal(barrier, inc=1, device_id=peer, device_id_type=pl.DeviceIdType.MESH)
+    pl.semaphore_wait(barrier, len(peers))
+
+    swap = pltpu.make_async_remote_copy(
+        src_ref=payload_ref,
+        dst_ref=mixed,
+        send_sem=pair_send,
+        recv_sem=pair_recv,
+        device_id=(partner, grp, dy, dz),
+        device_id_type=pl.DeviceIdType.MESH,
+    )
+    swap.start()
+    swap.wait()
+    line[...] = payload_ref[...] + mixed[...]
+    line_in[dz] = line[dz]
+
+    def z_copy(target, source):
+        return pltpu.make_async_remote_copy(
+            src_ref=line.at[target],
+            dst_ref=line_in.at[source],
+            send_sem=z_send.at[target],
+            recv_sem=z_recv.at[source],
+            device_id=(section, grp, dy, target),
+            device_id_type=pl.DeviceIdType.MESH,
+        )
+
+    for step in range(1, n_dz):
+        z_copy((dz + step) % n_dz, dz).start()
+    for step in range(1, n_dz):
+        source = (dz + n_dz - step) % n_dz
+        z_copy(source, source).wait_recv()
+    partial = line_in[0]
+    for index in range(1, n_dz):
+        partial = partial + line_in[index]
+    column[...] = partial
+    column_in[dy] = column[dy]
+
+    def y_copy(target, source):
+        return pltpu.make_async_remote_copy(
+            src_ref=column.at[target],
+            dst_ref=column_in.at[source],
+            send_sem=y_send.at[target],
+            recv_sem=y_recv.at[source],
+            device_id=(section, grp, target, dz),
+            device_id_type=pl.DeviceIdType.MESH,
+        )
+
+    for step in range(1, n_dy):
+        y_copy((dy + step) % n_dy, dy).start()
+    for step in range(1, n_dy):
+        source = (dy + n_dy - step) % n_dy
+        y_copy(source, source).wait_recv()
+    summed = column_in[0]
+    for index in range(1, n_dy):
+        summed = summed + column_in[index]
+    summed = summed.reshape(summed.shape[-2:])
     totals[grp] = summed[:, owned_width:]
 
     def total_copy(step):
@@ -208,6 +220,10 @@
             device_id_type=pl.DeviceIdType.MESH,
         ).wait_recv()
         total_copy(step).wait_send()
+    for step in range(1, n_dz):
+        z_copy((dz + step) % n_dz, dz).wait_send()
+    for step in range(1, n_dy):
+        y_copy((dy + step) % n_dy, dy).wait_send()
     run_sum = totals[0]
     for index in range(1, n_grp):
         run_sum = run_sum + totals[index]
@@ -219,24 +235,32 @@
 def reduce_owned(payload):
     sizes = (lax.axis_size("section"), lax.axis_size("grp"), lax.axis_size("dy"), lax.axis_size("dz"))
     n_section, n_grp, n_dy, n_dz = sizes
-    peers = n_section * n_dy * n_dz
     rows, one, width = payload.shape
     owned_width = width - 128
+    lines = payload.reshape(n_dy, n_dz, one, width).transpose(1, 0, 2, 3)
     return pl.pallas_call(
         functools.partial(reduce_kernel, sizes),
         out_shape=jax.ShapeDtypeStruct((1, owned_width), jnp.float32),
         in_specs=[pl.BlockSpec(memory_space=pltpu.VMEM)],
         out_specs=pl.BlockSpec(memory_space=pltpu.VMEM),
         scratch_shapes=[
-            pltpu.VMEM((peers, 1, width), jnp.float32),
+            pltpu.VMEM((n_dz, n_dy, one, width), jnp.float32),
+            pltpu.VMEM((n_dz, n_dy, one, width), jnp.float32),
+            pltpu.VMEM((n_dz, n_dy, one, width), jnp.float32),
+            pltpu.VMEM((n_dy, one, width), jnp.float32),
+            pltpu.VMEM((n_dy, one, width), jnp.float32),
             pltpu.VMEM((n_grp, 1, 128), jnp.float32),
-            pltpu.SemaphoreType.DMA((peers,)),
-            pltpu.SemaphoreType.DMA((peers,)),
+            pltpu.SemaphoreType.DMA(()),
+            pltpu.SemaphoreType.DMA(()),
+            pltpu.SemaphoreType.DMA((n_dz,)),
+            pltpu.SemaphoreType.DMA((n_dz,)),
+            pltpu.SemaphoreType.DMA((n_dy,)),
+            pltpu.SemaphoreType.DMA((n_dy,)),
             pltpu.SemaphoreType.DMA((n_grp,)),
             pltpu.SemaphoreType.DMA((n_grp,)),
         ],
         compiler_params=pltpu.CompilerParams(collective_id=0, has_side_effects=True),
-    )(payload)
+    )(lines)
 
 
 def frame_kernel(

time: 104 us -> 103 us (level); the launches traced: 104 us -> 101 us
  Pallas kernels: 92.9 us -> 90.4 us
    pallas_call x1, Pallas kernels: 20.2 us -> 17.7 us  [reduce_owned(): pl.pallas_call(functools.partial(reduce_kernel, sizes), out_shape=jax.Sha...]
    reshape x0 -> x2, local copies, waits for them, and re-layouts: none -> 1.32 us  [reduce_owned(): lines = payload.reshape(n_dy, n_dz, one, width).transpose(1, 0, 2, 3)]
    concatenate x1 -> x0, local copies, waits for them, and re-layouts: 1.29 us -> none  [on_device(): jnp.concatenate([placed.reshape(dev_count, 1, PREC // dev_count), jnp.bro...]
where the time goes in v16:
time: 103 us; the launch traced here: 101 us
  Pallas kernels  90.4 us (88%)
  local copies, waits for them, and re-layouts  4.31 us (4%)
  other arithmetic  3.94 us (4%)
  matrix products  1.73 us (2%)
    pallas_call x1, Pallas kernels, frame_work(): pl.pallas_call(functools.partial(frame_kernel, sizes), out_shape=(jax.Sha...  59.6 us
    pallas_call x1, Pallas kernels, reduce_owned(): pl.pallas_call(functools.partial(reduce_kernel, sizes), out_shape=jax.Sha...  17.7 us
    pallas_call x1, Pallas kernels, score_pairs(): pl.pallas_call(score_kernel, grid_spec=grid_spec, out_shape=jax.ShapeDtyp...  13.1 us

profile of v16, /device:TPU:1, one launch (start us, length us, event | category | flops | bytes accessed | tf_op | source)
XLA Modules:
  0.0 101.2 jit_solution(11663364671668850520)
XLA Ops:
  0.0 0.0 copy-start
  0.0 0.2 fusion.47
  0.3 0.3 fusion.42
  0.5 0.3 fusion.43
  0.8 0.3 fusion.44
  1.0 0.3 fusion.45
  1.3 0.3 fusion.46.kernels_ref
  1.6 0.0 copy-start.1
  1.6 0.0 copy-done
  1.6 0.7 constant_dynamic-slice_fusion.half_ref
  2.3 0.5 copy-done.1
  2.7 59.6 %shard_map.64 = (bf16[32,128,256]{2,1,0:T(8,128)(2,1)}, bf16[32,128,256]{2,1,0:T(8,128)(2,1)}, bf16[6,16,256,256]{3,2,1,0:T(8,128)(2,1)}) custom-call(bf16[16,256,256]{2,1,0:T(8,128)(2,1)} %bitcast.51, bf16[6,256,512]{2,1,0:T(8,128)(2,1)} %copy-done.1, bf16[128,256]{1,0:T(8,128)(2,1)} %constant_dynamic-slice_fusion.half_ref), custom_call_target="tpu_custom_call" | custom-call | tf_op jit(solution)/shard_map/pallas_call | solution.py:552
  63.0 0.0 copy-done.3
  63.0 1.0 %sort.17 = (s32[8]{0:T(128)}, s32[8]{0:T(128)}) sort(s32[8]{0:T(128)S(1)} %compare_select_fusion.2, s32[8]{0:T(128)S(1)} %iota.32), dimensions={0}, to_apply=%region_0.1 | sort | flops 24 | bytes 128 | tf_op jit(solution)/shard_map/jit(argsort)/sort | solution.py:626
  64.1 13.1 %shard_map.65 = f32[8,1,128]{2,1,0:T(1,128)} custom-call(s32[8]{0:T(128)} %get-tuple-element.9.order_ref, s32[8]{0:T(128)} %bitcast.55, s32[8]{0:T(128)} %bitcast.56, s32[1]{0:T(128)} %bitcast.48.count_ref, s32[1]{0:T(128)} %bitcast.8.section_ref, bf16[6,16,256,256]{3,2,1,0:T(8,128)(2,1)} %get-tuple-element.10.wave_ref, bf16[4096,256]{1,0:T(8,128)(2,1)} %bitcast.49, ...), custom_call_target="tpu_custom_call" | custom-call | tf_op jit(solution)/shard_map/pallas_call | solution.py:644
  77.2 0.0 copy-done.4
  77.2 0.6 gather_fusion
  77.8 0.1 add_select_fusion.1
  77.9 1.7 %fusion.40 = f32[64,128]{1,0:T(8,128)S(1)} fusion(s32[1024]{0:T(1024)S(1)} %get-tuple-element.14, f32[1024]{0:T(1024)} %bitcast.54, s32[1024]{0:T(1024)S(1)} %get-tuple-element.13), kind=kOutput, calls=%fused_computation.55 | convolution fusion | flops 100925440 | bytes 45056 | tf_op jit(solution)/shard_map/ka,kb->ab/dot_general | solution.py:89
  79.6 1.3 %reduce_sum.9 = f32[]{:T(128)} reduce(f32[8,1,128]{2,1,0:T(1,128)} %shard_map.65, f32[]{:T(128)} %constant.118.clone.1), dimensions={0,1,2}, to_apply=%region_1.2 | reduce | flops 1023 | bytes 4104 | tf_op jit(solution)/shard_map/reduce_sum | solution.py:97
  80.9 0.6 pad_bitcast_fusion
  81.6 0.7 copy.9
  82.2 17.7 %shard_map.66 = f32[1,256]{1,0:T(1,128)} custom-call(f32[8,4,1,384]{3,2,1,0:T(1,128)} %bitcast.52), custom_call_target="tpu_custom_call" | custom-call | tf_op jit(solution)/shard_map/pallas_call | solution.py:241
  100.0 1.2 %copy.17 = f32[1,256]{1,0:T(1,128)} copy(f32[1,256]{1,0:T(1,128)} %shard_map.66) | data formatting | bytes 2048
  (12 shorter events, 0.1 us)
Async XLA Ops:
  0.0 1.6 %copy-start = (bf16[256,256]{1,0:T(8,128)(2,1)S(1)}, bf16[256,256]{1,0:T(8,128)(2,1)}, u32[]{:S(2)}) copy-start(bf16[256,256]{1,0:T(8,128)(2,1)} %param.7) | copy-start | bytes 393220
  1.6 1.2 %copy-start.1 = (bf16[6,256,512]{2,1,0:T(8,128)(2,1)}, bf16[6,256,512]{2,1,0:T(8,128)(2,1)S(1)}, u32[]{:S(2)}) copy-start(bf16[6,256,512]{2,1,0:T(8,128)(2,1)S(1)} %fusion.46.kernels_ref) | copy-start | bytes 4718596
  2.7 60.3 %copy-start.3 = (s32[1,1,8]{2,1,0:T(1,128)S(1)}, s32[1,1,8]{2,1,0:T(1,128)}, u32[]{:S(2)}) copy-start(s32[1,1,8]{2,1,0:T(1,128)} %param.9) | copy-start | bytes 100
  64.1 13.1 %copy-start.4 = (s32[1,1,8]{2,1,0:T(1,128)S(1)}, s32[1,1,8]{2,1,0:T(1,128)}, u32[]{:S(2)}) copy-start(s32[1,1,8]{2,1,0:T(1,128)} %param.8) | copy-start | bytes 100
  64.1 13.1 %copy-start.2 = (s32[8192]{0:T(1024)S(1)}, s32[8192]{0:T(1024)}, u32[]{:S(2)}) copy-start(s32[8192]{0:T(1024)} %param.11) | copy-start | bytes 98308

commit v17 on v16

--- a/solution.py
+++ b/solution.py
@@ -94,15 +94,7 @@
         preferred_element_type=jnp.float32,
     ).reshape(-1)
     dev_count = lax.axis_size(DEV)
-    local_total = jnp.sum(responses)
-    payload = jnp.concatenate(
-        [
-            placed.reshape(dev_count, 1, PREC // dev_count),
-            jnp.broadcast_to(local_total, (dev_count, 1, 128)),
-        ],
-        axis=2,
-    )
-    return reduce_owned(payload)
+    return reduce_owned(placed.reshape(dev_count, 1, PREC // dev_count))
 
 
 def reduce_kernel(
@@ -151,7 +143,12 @@
     )
     swap.start()
     swap.wait()
-    line[...] = payload_ref[...] + mixed[...]
+    combined = payload_ref[...] + mixed[...]
+    line[:, :, :, :owned_width] = combined
+    chip_total = jnp.sum(jnp.sum(jnp.sum(combined, axis=0), axis=0), axis=1, keepdims=True)
+    line[:, :, :, owned_width:] = jnp.broadcast_to(
+        chip_total[None, None], line.shape[:3] + (line.shape[3] - owned_width,)
+    )
     line_in[dz] = line[dz]
 
     def z_copy(target, source):
@@ -235,16 +232,16 @@
 def reduce_owned(payload):
     sizes = (lax.axis_size("section"), lax.axis_size("grp"), lax.axis_size("dy"), lax.axis_size("dz"))
     n_section, n_grp, n_dy, n_dz = sizes
-    rows, one, width = payload.shape
-    owned_width = width - 128
-    lines = payload.reshape(n_dy, n_dz, one, width).transpose(1, 0, 2, 3)
+    rows, one, owned_width = payload.shape
+    width = owned_width + 128
+    lines = payload.reshape(n_dy, n_dz, one, owned_width).transpose(1, 0, 2, 3)
     return pl.pallas_call(
         functools.partial(reduce_kernel, sizes),
         out_shape=jax.ShapeDtypeStruct((1, owned_width), jnp.float32),
         in_specs=[pl.BlockSpec(memory_space=pltpu.VMEM)],
         out_specs=pl.BlockSpec(memory_space=pltpu.VMEM),
         scratch_shapes=[
-            pltpu.VMEM((n_dz, n_dy, one, width), jnp.float32),
+            pltpu.VMEM((n_dz, n_dy, one, owned_width), jnp.float32),
             pltpu.VMEM((n_dz, n_dy, one, width), jnp.float32),
             pltpu.VMEM((n_dz, n_dy, one, width), jnp.float32),
             pltpu.VMEM((n_dy, one, width), jnp.float32),

time: 103 us -> 101 us (0.981); the launches traced: 101 us -> 100 us
  other arithmetic: 3.94 us -> 2.65 us
  Pallas kernels: 90.4 us -> 91.6 us
    pallas_call x1, Pallas kernels: 17.7 us -> 24.9 us  [reduce_owned(): pl.pallas_call(functools.partial(reduce_kernel, sizes), out_shape=jax.Sha...]
    pallas_call x1, Pallas kernels: 13.1 us -> 7.08 us  [score_pairs(): pl.pallas_call(score_kernel, grid_spec=grid_spec, out_shape=jax.ShapeDtyp...]
    reshape x2 -> x0, local copies, waits for them, and re-layouts: 1.32 us -> none  [reduce_owned(): lines = payload.reshape(n_dy, n_dz, one, width).transpose(1, 0, 2, 3)]
    reduce_sum x1 -> x0, other arithmetic: 1.29 us -> none  [on_device(): local_total = jnp.sum(responses)]
where the time goes in v17:
time: 101 us; the launch traced here: 100 us
  Pallas kernels  91.6 us (91%)
  local copies, waits for them, and re-layouts  3.61 us (4%)
  other arithmetic  2.65 us (3%)
  matrix products  1.74 us (2%)
    pallas_call x1, Pallas kernels, frame_work(): pl.pallas_call(functools.partial(frame_kernel, sizes), out_shape=(jax.Sha...  59.6 us
    pallas_call x1, Pallas kernels, reduce_owned(): pl.pallas_call(functools.partial(reduce_kernel, sizes), out_shape=jax.Sha...  24.9 us
    pallas_call x1, Pallas kernels, score_pairs(): pl.pallas_call(score_kernel, grid_spec=grid_spec, out_shape=jax.ShapeDtyp...  7.08 us

profile of v17, /device:TPU:1, one launch (start us, length us, event | category | flops | bytes accessed | tf_op | source)
XLA Modules:
  0.0 100.4 jit_solution(1459757740147255314)
XLA Ops:
  0.0 0.0 copy-start
  0.0 0.2 fusion.47
  0.3 0.3 fusion.42
  0.5 0.3 fusion.43
  0.8 0.3 fusion.44
  1.0 0.3 fusion.45
  1.3 0.3 fusion.46.kernels_ref
  1.6 0.0 copy-start.1
  1.6 0.0 copy-done
  1.6 0.7 constant_dynamic-slice_fusion.half_ref
  2.3 0.5 copy-done.1
  2.7 0.0 copy-start.3
  2.7 59.6 %shard_map.64 = (bf16[32,128,256]{2,1,0:T(8,128)(2,1)}, bf16[32,128,256]{2,1,0:T(8,128)(2,1)}, bf16[6,16,256,256]{3,2,1,0:T(8,128)(2,1)}) custom-call(bf16[16,256,256]{2,1,0:T(8,128)(2,1)} %bitcast.49, bf16[6,256,512]{2,1,0:T(8,128)(2,1)} %copy-done.1, bf16[128,256]{1,0:T(8,128)(2,1)} %constant_dynamic-slice_fusion.half_ref), custom_call_target="tpu_custom_call" | custom-call | tf_op jit(solution)/shard_map/pallas_call | solution.py:549
  63.0 0.0 copy-done.3
  63.0 1.0 %sort.17 = (s32[8]{0:T(128)}, s32[8]{0:T(128)}) sort(s32[8]{0:T(128)S(1)} %compare_select_fusion.2, s32[8]{0:T(128)S(1)} %iota.32), dimensions={0}, to_apply=%region_0.1 | sort | flops 24 | bytes 128 | tf_op jit(solution)/shard_map/jit(argsort)/sort | solution.py:623
  64.1 7.1 %shard_map.65 = f32[8,1,128]{2,1,0:T(1,128)} custom-call(s32[8]{0:T(128)} %get-tuple-element.9.order_ref, s32[8]{0:T(128)} %bitcast.53, s32[8]{0:T(128)} %bitcast.54, s32[1]{0:T(128)} %bitcast.46.count_ref, s32[1]{0:T(128)} %bitcast.8.section_ref, bf16[6,16,256,256]{3,2,1,0:T(8,128)(2,1)} %get-tuple-element.10.wave_ref, bf16[4096,256]{1,0:T(8,128)(2,1)} %bitcast.47, ...), custom_call_target="tpu_custom_call" | custom-call | tf_op jit(solution)/shard_map/pallas_call | solution.py:641
  71.2 0.0 copy-done.4
  71.2 0.0 copy-done.2
  71.2 0.6 gather_fusion
  71.8 0.1 add_select_fusion.1
  71.9 1.7 %fusion.40 = f32[64,128]{1,0:T(8,128)S(1)} fusion(s32[1024]{0:T(1024)S(1)} %get-tuple-element.14, f32[1024]{0:T(1024)} %bitcast.52, s32[1024]{0:T(1024)S(1)} %get-tuple-element.13), kind=kOutput, calls=%fused_computation.55 | convolution fusion | flops 100925440 | bytes 45056 | tf_op jit(solution)/shard_map/ka,kb->ab/dot_general | solution.py:89
  73.6 0.6 copy.9
  74.3 24.9 %shard_map.66 = f32[1,256]{1,0:T(1,128)} custom-call(f32[8,4,1,256]{3,2,1,0:T(1,128)} %bitcast.50), custom_call_target="tpu_custom_call" | custom-call | tf_op jit(solution)/shard_map/pallas_call | solution.py:238
  99.1 1.2 %copy.17 = f32[1,256]{1,0:T(1,128)} copy(f32[1,256]{1,0:T(1,128)} %shard_map.66) | data formatting | bytes 2048
  (10 shorter events, 0.1 us)
Async XLA Ops:
  0.0 1.6 %copy-start = (bf16[256,256]{1,0:T(8,128)(2,1)S(1)}, bf16[256,256]{1,0:T(8,128)(2,1)}, u32[]{:S(2)}) copy-start(bf16[256,256]{1,0:T(8,128)(2,1)} %param.7) | copy-start | bytes 393220
  1.6 1.2 %copy-start.1 = (bf16[6,256,512]{2,1,0:T(8,128)(2,1)}, bf16[6,256,512]{2,1,0:T(8,128)(2,1)S(1)}, u32[]{:S(2)}) copy-start(bf16[6,256,512]{2,1,0:T(8,128)(2,1)S(1)} %fusion.46.kernels_ref) | copy-start | bytes 4718596
  2.7 60.3 %copy-start.3 = (s32[1,1,8]{2,1,0:T(1,128)S(1)}, s32[1,1,8]{2,1,0:T(1,128)}, u32[]{:S(2)}) copy-start(s32[1,1,8]{2,1,0:T(1,128)} %param.9) | copy-start | bytes 100
  64.1 7.1 %copy-start.4 = (s32[1,1,8]{2,1,0:T(1,128)S(1)}, s32[1,1,8]{2,1,0:T(1,128)}, u32[]{:S(2)}) copy-start(s32[1,1,8]{2,1,0:T(1,128)} %param.8) | copy-start | bytes 100
  64.1 7.1 %copy-start.2 = (s32[8192]{0:T(1024)S(1)}, s32[8192]{0:T(1024)}, u32[]{:S(2)}) copy-start(s32[8192]{0:T(1024)} %param.11) | copy-start | bytes 98308

commit v18 on v17

--- a/solution.py
+++ b/solution.py
@@ -513,12 +513,9 @@
     half = own_scans.shape[1]
 
     def level_frame(frame, carry):
+        scans = jnp.concatenate([own_scans[frame], partner_scans[frame]], axis=0)
         for level in range(SCALES):
-            table = kernels_ref[level]
-            acc = jnp.dot(table[:, :half], own_scans[frame], preferred_element_type=jnp.float32)
-            acc = acc + jnp.dot(
-                table[:, half:], partner_scans[frame], preferred_element_type=jnp.float32
-            )
+            acc = jnp.dot(kernels_ref[level], scans, preferred_element_type=jnp.float32)
             wave_ref[level, frame] = acc.astype(wave_ref.dtype)
         return carry
 

time: 101 us -> 101 us (level)
    pallas_call x1, Pallas kernels: 24.9 us -> 21.6 us  [reduce_owned(): pl.pallas_call(functools.partial(reduce_kernel, sizes), out_shape=jax.Sha...]
    pallas_call x1, Pallas kernels: 7.08 us -> 9.75 us  [score_pairs(): pl.pallas_call(score_kernel, grid_spec=grid_spec, out_shape=jax.ShapeDtyp...]
where the time goes in v18:
time: 101 us; the launch traced here: 99.8 us
  Pallas kernels  91 us (90%)
  local copies, waits for them, and re-layouts  3.61 us (4%)
  other arithmetic  2.65 us (3%)
  matrix products  1.74 us (2%)
    pallas_call x1, Pallas kernels, frame_work(): pl.pallas_call(functools.partial(frame_kernel, sizes), out_shape=(jax.Sha...  59.6 us
    pallas_call x1, Pallas kernels, reduce_owned(): pl.pallas_call(functools.partial(reduce_kernel, sizes), out_shape=jax.Sha...  21.6 us
    pallas_call x1, Pallas kernels, score_pairs(): pl.pallas_call(score_kernel, grid_spec=grid_spec, out_shape=jax.ShapeDtyp...  9.75 us

profile of v18, /device:TPU:1, one launch (start us, length us, event | category | flops | bytes accessed | tf_op | source)
XLA Modules:
  0.0 99.8 jit_solution(549969339183762167)
XLA Ops:
  0.0 0.0 copy-start
  0.0 0.2 fusion.47
  0.3 0.3 fusion.42
  0.5 0.3 fusion.43
  0.8 0.3 fusion.44
  1.0 0.3 fusion.45
  1.3 0.3 fusion.46.kernels_ref
  1.6 0.0 copy-start.1
  1.6 0.0 copy-done
  1.6 0.7 constant_dynamic-slice_fusion.half_ref
  2.3 0.5 copy-done.1
  2.7 0.0 copy-start.3
  2.7 59.6 %shard_map.64 = (bf16[32,128,256]{2,1,0:T(8,128)(2,1)}, bf16[32,128,256]{2,1,0:T(8,128)(2,1)}, bf16[6,16,256,256]{3,2,1,0:T(8,128)(2,1)}) custom-call(bf16[16,256,256]{2,1,0:T(8,128)(2,1)} %bitcast.49, bf16[6,256,512]{2,1,0:T(8,128)(2,1)} %copy-done.1, bf16[128,256]{1,0:T(8,128)(2,1)} %constant_dynamic-slice_fusion.half_ref), custom_call_target="tpu_custom_call" | custom-call | tf_op jit(solution)/shard_map/pallas_call | solution.py:546
  63.0 0.0 copy-done.3
  63.1 1.0 %sort.17 = (s32[8]{0:T(128)}, s32[8]{0:T(128)}) sort(s32[8]{0:T(128)S(1)} %compare_select_fusion.2, s32[8]{0:T(128)S(1)} %iota.32), dimensions={0}, to_apply=%region_0.1 | sort | flops 24 | bytes 128 | tf_op jit(solution)/shard_map/jit(argsort)/sort | solution.py:620
  64.1 9.7 %shard_map.65 = f32[8,1,128]{2,1,0:T(1,128)} custom-call(s32[8]{0:T(128)} %get-tuple-element.9.order_ref, s32[8]{0:T(128)} %bitcast.53, s32[8]{0:T(128)} %bitcast.54, s32[1]{0:T(128)} %bitcast.46.count_ref, s32[1]{0:T(128)} %bitcast.8.section_ref, bf16[6,16,256,256]{3,2,1,0:T(8,128)(2,1)} %get-tuple-element.10.wave_ref, bf16[4096,256]{1,0:T(8,128)(2,1)} %bitcast.47, ...), custom_call_target="tpu_custom_call" | custom-call | tf_op jit(solution)/shard_map/pallas_call | solution.py:638
  73.9 0.0 copy-done.4
  73.9 0.0 copy-done.2
  73.9 0.6 gather_fusion
  74.5 0.1 add_select_fusion.1
  74.5 1.7 %fusion.40 = f32[64,128]{1,0:T(8,128)S(1)} fusion(s32[1024]{0:T(1024)S(1)} %get-tuple-element.14, f32[1024]{0:T(1024)} %bitcast.52, s32[1024]{0:T(1024)S(1)} %get-tuple-element.13), kind=kOutput, calls=%fused_computation.55 | convolution fusion | flops 100925440 | bytes 45056 | tf_op jit(solution)/shard_map/ka,kb->ab/dot_general | solution.py:89
  76.3 0.6 copy.9
  76.9 21.6 %shard_map.66 = f32[1,256]{1,0:T(1,128)} custom-call(f32[8,4,1,256]{3,2,1,0:T(1,128)} %bitcast.50), custom_call_target="tpu_custom_call" | custom-call | tf_op jit(solution)/shard_map/pallas_call | solution.py:238
  98.5 1.2 %copy.17 = f32[1,256]{1,0:T(1,128)} copy(f32[1,256]{1,0:T(1,128)} %shard_map.66) | data formatting | bytes 2048
  (10 shorter events, 0.1 us)
Async XLA Ops:
  0.0 1.6 %copy-start = (bf16[256,256]{1,0:T(8,128)(2,1)S(1)}, bf16[256,256]{1,0:T(8,128)(2,1)}, u32[]{:S(2)}) copy-start(bf16[256,256]{1,0:T(8,128)(2,1)} %param.7) | copy-start | bytes 393220
  1.6 1.2 %copy-start.1 = (bf16[6,256,512]{2,1,0:T(8,128)(2,1)}, bf16[6,256,512]{2,1,0:T(8,128)(2,1)S(1)}, u32[]{:S(2)}) copy-start(bf16[6,256,512]{2,1,0:T(8,128)(2,1)S(1)} %fusion.46.kernels_ref) | copy-start | bytes 4718596
  2.7 60.3 %copy-start.3 = (s32[1,1,8]{2,1,0:T(1,128)S(1)}, s32[1,1,8]{2,1,0:T(1,128)}, u32[]{:S(2)}) copy-start(s32[1,1,8]{2,1,0:T(1,128)} %param.9) | copy-start | bytes 100
  64.1 9.8 %copy-start.4 = (s32[1,1,8]{2,1,0:T(1,128)S(1)}, s32[1,1,8]{2,1,0:T(1,128)}, u32[]{:S(2)}) copy-start(s32[1,1,8]{2,1,0:T(1,128)} %param.8) | copy-start | bytes 100
  64.1 9.8 %copy-start.2 = (s32[8192]{0:T(1024)S(1)}, s32[8192]{0:T(1024)}, u32[]{:S(2)}) copy-start(s32[8192]{0:T(1024)} %param.11) | copy-start | bytes 98308

commit v19 on v17

--- a/solution.py
+++ b/solution.py
@@ -620,7 +620,10 @@
     scales, frames_local, mob_local, channels = wavelet_stack.shape
     slot_ids = jnp.arange(slots, dtype=jnp.int32)
     keys = jnp.where(slot_ids < live_pairs, tile_ids * slots + slot_ids, (mob_local // TM + 1) * slots + slot_ids)
-    order = jnp.argsort(keys).astype(jnp.int32)
+    ranks = jnp.sum((keys[None, :] < keys[:, None]).astype(jnp.int32), axis=1)
+    order = jnp.sum(
+        jnp.where(ranks[None, :] == slot_ids[:, None], slot_ids[None, :], 0), axis=1
+    ).astype(jnp.int32)
 
     def visited(k, o, c):
         return o[jnp.minimum(k, c[0] - 1)]

time: 101 us -> 100 us (0.990)
    sort x1 -> x0, other arithmetic: 1.04 us -> none  [score_pairs(): order = jnp.argsort(keys).astype(jnp.int32)]
where the time goes in v19:
time: 100 us; the launch traced here: 99.3 us
  Pallas kernels  90.8 us (91%)
  local copies, waits for them, and re-layouts  3.58 us (4%)
  other arithmetic  2.45 us (2%)
  matrix products  1.74 us (2%)
    pallas_call x1, Pallas kernels, frame_work(): pl.pallas_call(functools.partial(frame_kernel, sizes), out_shape=(jax.Sha...  59.6 us
    pallas_call x1, Pallas kernels, reduce_owned(): pl.pallas_call(functools.partial(reduce_kernel, sizes), out_shape=jax.Sha...  24.1 us
    pallas_call x1, Pallas kernels, score_pairs(): pl.pallas_call(score_kernel, grid_spec=grid_spec, out_shape=jax.ShapeDtyp...  7.05 us

profile of v19, /device:TPU:1, one launch (start us, length us, event | category | flops | bytes accessed | tf_op | source)
XLA Modules:
  0.0 99.3 jit_solution(10584124455343871076)
XLA Ops:
  0.0 0.0 copy-start
  0.0 0.2 fusion.47
  0.3 0.3 fusion.42
  0.5 0.3 fusion.43
  0.8 0.3 fusion.44
  1.0 0.3 fusion.45
  1.3 0.3 fusion.46.kernels_ref
  1.6 0.0 copy-start.1
  1.6 0.0 copy-done
  1.6 0.7 constant_dynamic-slice_fusion.half_ref
  2.3 0.5 copy-done.1
  2.7 59.6 %shard_map.64 = (bf16[32,128,256]{2,1,0:T(8,128)(2,1)}, bf16[32,128,256]{2,1,0:T(8,128)(2,1)}, bf16[6,16,256,256]{3,2,1,0:T(8,128)(2,1)}) custom-call(bf16[16,256,256]{2,1,0:T(8,128)(2,1)} %bitcast.49, bf16[6,256,512]{2,1,0:T(8,128)(2,1)} %copy-done.1, bf16[128,256]{1,0:T(8,128)(2,1)} %constant_dynamic-slice_fusion.half_ref), custom_call_target="tpu_custom_call" | custom-call | tf_op jit(solution)/shard_map/pallas_call | solution.py:549
  63.0 0.0 copy-done.3
  63.0 0.2 convert_reduce_fusion
  63.2 0.7 select_reduce_fusion.order_ref
  63.9 7.1 %shard_map.65 = f32[8,1,128]{2,1,0:T(1,128)} custom-call(s32[8]{0:T(128)} %select_reduce_fusion.order_ref, s32[8]{0:T(128)} %bitcast.53, s32[8]{0:T(128)} %bitcast.54, s32[1]{0:T(128)} %bitcast.46.count_ref, s32[1]{0:T(128)} %bitcast.8.section_ref, bf16[6,16,256,256]{3,2,1,0:T(8,128)(2,1)} %get-tuple-element.8.wave_ref, bf16[4096,256]{1,0:T(8,128)(2,1)} %bitcast.47, ...), custom_call_target="tpu_custom_call" | custom-call | tf_op jit(solution)/shard_map/pallas_call | solution.py:644
  70.9 0.0 copy-done.4
  70.9 0.0 copy-done.2
  70.9 0.6 gather_fusion
  71.5 0.1 add_select_fusion.1
  71.6 1.7 %fusion.40 = f32[64,128]{1,0:T(8,128)S(1)} fusion(s32[1024]{0:T(1024)S(1)} %get-tuple-element.12, f32[1024]{0:T(1024)} %bitcast.52, s32[1024]{0:T(1024)S(1)} %get-tuple-element.11), kind=kOutput, calls=%fused_computation.55 | convolution fusion | flops 100925440 | bytes 45056 | tf_op jit(solution)/shard_map/ka,kb->ab/dot_general | solution.py:89
  73.4 0.6 copy.10
  74.0 24.1 %shard_map.66 = f32[1,256]{1,0:T(1,128)} custom-call(f32[8,4,1,256]{3,2,1,0:T(1,128)} %bitcast.50), custom_call_target="tpu_custom_call" | custom-call | tf_op jit(solution)/shard_map/pallas_call | solution.py:238
  98.1 1.2 %copy.18 = f32[1,256]{1,0:T(1,128)} copy(f32[1,256]{1,0:T(1,128)} %shard_map.66) | data formatting | bytes 2048
  (10 shorter events, 0.1 us)
Async XLA Ops:
  0.0 1.6 %copy-start = (bf16[256,256]{1,0:T(8,128)(2,1)S(1)}, bf16[256,256]{1,0:T(8,128)(2,1)}, u32[]{:S(2)}) copy-start(bf16[256,256]{1,0:T(8,128)(2,1)} %param.7) | copy-start | bytes 393220
  1.6 1.2 %copy-start.1 = (bf16[6,256,512]{2,1,0:T(8,128)(2,1)}, bf16[6,256,512]{2,1,0:T(8,128)(2,1)S(1)}, u32[]{:S(2)}) copy-start(bf16[6,256,512]{2,1,0:T(8,128)(2,1)S(1)} %fusion.46.kernels_ref) | copy-start | bytes 4718596
  2.7 60.3 %copy-start.3 = (s32[1,1,8]{2,1,0:T(1,128)S(1)}, s32[1,1,8]{2,1,0:T(1,128)}, u32[]{:S(2)}) copy-start(s32[1,1,8]{2,1,0:T(1,128)} %param.9) | copy-start | bytes 100
  63.9 7.1 %copy-start.4 = (s32[1,1,8]{2,1,0:T(1,128)S(1)}, s32[1,1,8]{2,1,0:T(1,128)}, u32[]{:S(2)}) copy-start(s32[1,1,8]{2,1,0:T(1,128)} %param.8) | copy-start | bytes 100
  63.9 7.1 %copy-start.2 = (s32[8192]{0:T(1024)S(1)}, s32[8192]{0:T(1024)}, u32[]{:S(2)}) copy-start(s32[8192]{0:T(1024)} %param.11) | copy-start | bytes 98308

commit v20 on v17

--- a/solution.py
+++ b/solution.py
@@ -117,6 +117,7 @@
     total_recv,
 ):
     n_section, n_grp, n_dy, n_dz = sizes
+    cores = totals
     section = lax.axis_index("section")
     grp = lax.axis_index("grp")
     dy = lax.axis_index("dy")
@@ -128,7 +129,9 @@
     peers = [(partner, grp, dy, dz)]
     peers += [(section, grp, dy, (dz + step) % n_dz) for step in range(1, n_dz)]
     peers += [(section, grp, (dy + step) % n_dy, dz) for step in range(1, n_dy)]
-    peers += [(section, (grp + step) % n_grp, dy, dz) for step in range(1, n_grp)]
+    peers += [
+        (side, (grp + step) % n_grp, dy, dz) for side in range(n_section) for step in range(1, n_grp)
+    ]
     for peer in peers:
         pl.semaphore_signal(barrier, inc=1, device_id=peer, device_id_type=pl.DeviceIdType.MESH)
     pl.semaphore_wait(barrier, len(peers))
@@ -142,13 +145,48 @@
         device_id_type=pl.DeviceIdType.MESH,
     )
     swap.start()
+    own_slot = section * n_grp + grp
+    own_sum = jnp.sum(jnp.sum(jnp.sum(payload_ref[...], axis=0), axis=0), axis=1, keepdims=True)
+    cores[own_slot] = jnp.broadcast_to(own_sum, (1, 128))
+    cores[partner * n_grp + grp] = jnp.zeros((1, 128), jnp.float32)
+
+    def core_copy(side, other):
+        return pltpu.make_async_remote_copy(
+            src_ref=cores.at[own_slot],
+            dst_ref=cores.at[own_slot],
+            send_sem=total_send.at[side * n_grp + other],
+            recv_sem=total_recv.at[own_slot],
+            device_id=(side, other, dy, dz),
+            device_id_type=pl.DeviceIdType.MESH,
+        )
+
+    def core_arrival(side, other):
+        slot = side * n_grp + other
+        return pltpu.make_async_remote_copy(
+            src_ref=cores.at[slot],
+            dst_ref=cores.at[slot],
+            send_sem=total_send.at[slot],
+            recv_sem=total_recv.at[slot],
+            device_id=(side, other, dy, dz),
+            device_id_type=pl.DeviceIdType.MESH,
+        )
+
+    for side in range(n_section):
+        for step in range(1, n_grp):
+            core_copy(side, (grp + step) % n_grp).start()
     swap.wait()
     combined = payload_ref[...] + mixed[...]
     line[:, :, :, :owned_width] = combined
     chip_total = jnp.sum(jnp.sum(jnp.sum(combined, axis=0), axis=0), axis=1, keepdims=True)
-    line[:, :, :, owned_width:] = jnp.broadcast_to(
-        chip_total[None, None], line.shape[:3] + (line.shape[3] - owned_width,)
-    )
+    for side in range(n_section):
+        for step in range(1, n_grp):
+            core_arrival(side, (grp + step) % n_grp).wait_recv()
+    lanes = lax.broadcasted_iota(jnp.int32, (1, line.shape[3] - owned_width), 1)
+    spread = jnp.where(lanes == grp, chip_total, 0.0)
+    for other in range(n_grp):
+        other_total = cores[other] + cores[n_grp + other]
+        spread = jnp.where(jnp.logical_and(lanes == other, other != grp), other_total, spread)
+    line[:, :, :, owned_width:] = jnp.broadcast_to(spread[None, None], line.shape[:3] + spread.shape[1:])
     line_in[dz] = line[dz]
 
     def z_copy(target, source):
@@ -191,41 +229,17 @@
     for index in range(1, n_dy):
         summed = summed + column_in[index]
     summed = summed.reshape(summed.shape[-2:])
-    totals[grp] = summed[:, owned_width:]
-
-    def total_copy(step):
-        target = (grp + step) % n_grp
-        return pltpu.make_async_remote_copy(
-            src_ref=totals.at[grp],
-            dst_ref=totals.at[grp],
-            send_sem=total_send.at[target],
-            recv_sem=total_recv.at[grp],
-            device_id=(section, target, dy, dz),
-            device_id_type=pl.DeviceIdType.MESH,
-        )
-
-    for step in range(1, n_grp):
-        total_copy(step).start()
-    for step in range(1, n_grp):
-        source = (grp + step) % n_grp
-        pltpu.make_async_remote_copy(
-            src_ref=totals.at[source],
-            dst_ref=totals.at[source],
-            send_sem=total_send.at[source],
-            recv_sem=total_recv.at[source],
-            device_id=(section, source, dy, dz),
-            device_id_type=pl.DeviceIdType.MESH,
-        ).wait_recv()
-        total_copy(step).wait_send()
     for step in range(1, n_dz):
         z_copy((dz + step) % n_dz, dz).wait_send()
     for step in range(1, n_dy):
         y_copy((dy + step) % n_dy, dy).wait_send()
-    run_sum = totals[0]
-    for index in range(1, n_grp):
-        run_sum = run_sum + totals[index]
-    own_total = summed[:, owned_width : owned_width + 1]
-    factor = (run_sum[:, 0:1] / n_grp) / own_total
+    for side in range(n_section):
+        for step in range(1, n_grp):
+            core_copy(side, (grp + step) % n_grp).wait_send()
+    run_totals = summed[:, owned_width:]
+    run_sum = jnp.sum(run_totals, axis=1, keepdims=True)
+    own_total = jnp.sum(jnp.where(lanes == grp, run_totals, 0.0), axis=1, keepdims=True)
+    factor = (run_sum / n_grp) / own_total
     out_ref[...] = summed[:, :owned_width] * factor
 
 
@@ -246,15 +260,15 @@
             pltpu.VMEM((n_dz, n_dy, one, width), jnp.float32),
             pltpu.VMEM((n_dy, one, width), jnp.float32),
             pltpu.VMEM((n_dy, one, width), jnp.float32),
-            pltpu.VMEM((n_grp, 1, 128), jnp.float32),
+            pltpu.VMEM((n_section * n_grp, 1, 128), jnp.float32),
             pltpu.SemaphoreType.DMA(()),
             pltpu.SemaphoreType.DMA(()),
             pltpu.SemaphoreType.DMA((n_dz,)),
             pltpu.SemaphoreType.DMA((n_dz,)),
             pltpu.SemaphoreType.DMA((n_dy,)),
             pltpu.SemaphoreType.DMA((n_dy,)),
-            pltpu.SemaphoreType.DMA((n_grp,)),
-            pltpu.SemaphoreType.DMA((n_grp,)),
+            pltpu.SemaphoreType.DMA((n_section * n_grp,)),
+            pltpu.SemaphoreType.DMA((n_section * n_grp,)),
         ],
         compiler_params=pltpu.CompilerParams(collective_id=0, has_side_effects=True),
     )(lines)

time: 101 us -> 99.3 us (0.983)
  Pallas kernels: 91.6 us -> 89.7 us
    pallas_call x1, Pallas kernels: 24.9 us -> 23 us  [reduce_owned(): pl.pallas_call(functools.partial(reduce_kernel, sizes), out_shape=jax.Sha...]
where the time goes in v20:
time: 99.3 us; the launch traced here: 98.5 us
  Pallas kernels  89.7 us (90%)
  local copies, waits for them, and re-layouts  3.61 us (4%)
  other arithmetic  2.65 us (3%)
  matrix products  1.74 us (2%)
    pallas_call x1, Pallas kernels, frame_work(): pl.pallas_call(functools.partial(frame_kernel, sizes), out_shape=(jax.Sha...  59.6 us
    pallas_call x1, Pallas kernels, reduce_owned(): pl.pallas_call(functools.partial(reduce_kernel, sizes), out_shape=jax.Sha...  23 us
    pallas_call x1, Pallas kernels, score_pairs(): pl.pallas_call(score_kernel, grid_spec=grid_spec, out_shape=jax.ShapeDtyp...  7.08 us

profile of v20, /device:TPU:1, one launch (start us, length us, event | category | flops | bytes accessed | tf_op | source)
XLA Modules:
  0.0 98.5 jit_solution(2478805979634509812)
XLA Ops:
  0.0 0.0 copy-start
  0.0 0.2 fusion.47
  0.3 0.3 fusion.42
  0.5 0.3 fusion.43
  0.8 0.3 fusion.44
  1.0 0.3 fusion.45
  1.3 0.3 fusion.46.kernels_ref
  1.6 0.0 copy-start.1
  1.6 0.0 copy-done
  1.6 0.7 constant_dynamic-slice_fusion.half_ref
  2.3 0.5 copy-done.1
  2.7 0.0 copy-start.3
  2.7 59.6 %shard_map.64 = (bf16[32,128,256]{2,1,0:T(8,128)(2,1)}, bf16[32,128,256]{2,1,0:T(8,128)(2,1)}, bf16[6,16,256,256]{3,2,1,0:T(8,128)(2,1)}) custom-call(bf16[16,256,256]{2,1,0:T(8,128)(2,1)} %bitcast.49, bf16[6,256,512]{2,1,0:T(8,128)(2,1)} %copy-done.1, bf16[128,256]{1,0:T(8,128)(2,1)} %constant_dynamic-slice_fusion.half_ref), custom_call_target="tpu_custom_call" | custom-call | tf_op jit(solution)/shard_map/pallas_call | solution.py:563
  63.0 0.0 copy-done.3
  63.0 1.0 %sort.17 = (s32[8]{0:T(128)}, s32[8]{0:T(128)}) sort(s32[8]{0:T(128)S(1)} %compare_select_fusion.2, s32[8]{0:T(128)S(1)} %iota.32), dimensions={0}, to_apply=%region_0.1 | sort | flops 24 | bytes 128 | tf_op jit(solution)/shard_map/jit(argsort)/sort | solution.py:637
  64.1 7.1 %shard_map.65 = f32[8,1,128]{2,1,0:T(1,128)} custom-call(s32[8]{0:T(128)} %get-tuple-element.9.order_ref, s32[8]{0:T(128)} %bitcast.53, s32[8]{0:T(128)} %bitcast.54, s32[1]{0:T(128)} %bitcast.46.count_ref, s32[1]{0:T(128)} %bitcast.8.section_ref, bf16[6,16,256,256]{3,2,1,0:T(8,128)(2,1)} %get-tuple-element.10.wave_ref, bf16[4096,256]{1,0:T(8,128)(2,1)} %bitcast.47, ...), custom_call_target="tpu_custom_call" | custom-call | tf_op jit(solution)/shard_map/pallas_call | solution.py:655
  71.2 0.0 copy-done.4
  71.2 0.0 copy-done.2
  71.2 0.6 gather_fusion
  71.8 0.1 add_select_fusion.1
  71.9 1.7 %fusion.40 = f32[64,128]{1,0:T(8,128)S(1)} fusion(s32[1024]{0:T(1024)S(1)} %get-tuple-element.14, f32[1024]{0:T(1024)} %bitcast.52, s32[1024]{0:T(1024)S(1)} %get-tuple-element.13), kind=kOutput, calls=%fused_computation.55 | convolution fusion | flops 100925440 | bytes 45056 | tf_op jit(solution)/shard_map/ka,kb->ab/dot_general | solution.py:89
  73.6 0.6 copy.9
  74.3 23.0 %shard_map.66 = f32[1,256]{1,0:T(1,128)} custom-call(f32[8,4,1,256]{3,2,1,0:T(1,128)} %bitcast.50), custom_call_target="tpu_custom_call" | custom-call | tf_op jit(solution)/shard_map/pallas_call | solution.py:252
  97.3 1.2 %copy.17 = f32[1,256]{1,0:T(1,128)} copy(f32[1,256]{1,0:T(1,128)} %shard_map.66) | data formatting | bytes 2048
  (10 shorter events, 0.1 us)
Async XLA Ops:
  0.0 1.6 %copy-start = (bf16[256,256]{1,0:T(8,128)(2,1)S(1)}, bf16[256,256]{1,0:T(8,128)(2,1)}, u32[]{:S(2)}) copy-start(bf16[256,256]{1,0:T(8,128)(2,1)} %param.7) | copy-start | bytes 393220
  1.6 1.2 %copy-start.1 = (bf16[6,256,512]{2,1,0:T(8,128)(2,1)}, bf16[6,256,512]{2,1,0:T(8,128)(2,1)S(1)}, u32[]{:S(2)}) copy-start(bf16[6,256,512]{2,1,0:T(8,128)(2,1)S(1)} %fusion.46.kernels_ref) | copy-start | bytes 4718596
  2.7 60.3 %copy-start.3 = (s32[1,1,8]{2,1,0:T(1,128)S(1)}, s32[1,1,8]{2,1,0:T(1,128)}, u32[]{:S(2)}) copy-start(s32[1,1,8]{2,1,0:T(1,128)} %param.9) | copy-start | bytes 100
  64.1 7.1 %copy-start.4 = (s32[1,1,8]{2,1,0:T(1,128)S(1)}, s32[1,1,8]{2,1,0:T(1,128)}, u32[]{:S(2)}) copy-start(s32[1,1,8]{2,1,0:T(1,128)} %param.8) | copy-start | bytes 100
  64.1 7.1 %copy-start.2 = (s32[8192]{0:T(1024)S(1)}, s32[8192]{0:T(1024)}, u32[]{:S(2)}) copy-start(s32[8192]{0:T(1024)} %param.11) | copy-start | bytes 98308

commit v21 on v20

--- a/solution.py
+++ b/solution.py
@@ -65,10 +65,9 @@
     section_index = lax.axis_index("section")
     mob_local = frames.shape[2]
     section_count = lax.axis_size("section")
-    kernels = mobility_kernels(section_index * mob_local, mob_local, section_index * mob_local)
     half_rows = templates.shape[0] // 2
     my_half = lax.dynamic_slice_in_dim(templates, section_index * half_rows, half_rows, 0)
-    my_rows, other_rows, wavelet_stack = frame_work(frames[0], kernels, my_half)
+    my_rows, other_rows, wavelet_stack = frame_work(frames[0], my_half)
     slots = pair_block.shape[2]
     live_pairs = pair_count[0, 0, 0]
     block_ids = pair_block[0, 0]
@@ -277,11 +276,11 @@
 def frame_kernel(
     sizes,
     frames_ref,
-    kernels_ref,
     half_ref,
     out_ref,
     other_ref,
     wave_ref,
+    kernels_ref,
     halo_left,
     halo_right,
     own_scans,
@@ -480,6 +479,24 @@
         to_left_of_right.wait_recv()
         to_right().wait_send()
 
+    mob_rows = kernels_ref.shape[1]
+    mob_all = kernels_ref.shape[2]
+    row_place = (
+        section * mob_rows + lax.broadcasted_iota(jnp.int32, (mob_rows, mob_all), 0)
+    ).astype(jnp.float32)
+    col_place = (
+        (section * mob_rows + lax.broadcasted_iota(jnp.int32, (mob_rows, mob_all), 1)) % mob_all
+    ).astype(jnp.float32)
+    distance = row_place - col_place
+    for level in range(SCALES):
+        spread_scans = 2.0**level
+        scaled = distance / spread_scans
+        kernels_ref[level] = (
+            (1.0 - scaled * scaled)
+            * jnp.exp(-0.5 * scaled * scaled)
+            / math.sqrt(0.75 * math.sqrt(math.pi) * spread_scans)
+        ).astype(kernels_ref.dtype)
+
     weights = retention_weights()
 
     row_block = 32
@@ -555,7 +572,7 @@
         pair_copy(slot, half_ref).wait_send()
 
 
-def frame_work(frames, kernels, half):
+def frame_work(frames, half):
     sizes = (lax.axis_size("section"), lax.axis_size("dy"), lax.axis_size("dz"))
     n_section, n_dy, n_dz = sizes
     rows, channels = half.shape
@@ -567,9 +584,10 @@
             jax.ShapeDtypeStruct((n_dy * n_dz, rows, channels), half.dtype),
             jax.ShapeDtypeStruct((SCALES, count_frames, mob_local, channels), jnp.bfloat16),
         ),
-        in_specs=[pl.BlockSpec(memory_space=pltpu.VMEM)] * 3,
+        in_specs=[pl.BlockSpec(memory_space=pltpu.VMEM)] * 2,
         out_specs=(pl.BlockSpec(memory_space=pltpu.VMEM),) * 3,
         scratch_shapes=[
+            pltpu.VMEM((SCALES, mob_local, 2 * mob_local), jnp.bfloat16),
             pltpu.VMEM((RAD, mob_local, channels), frames.dtype),
             pltpu.VMEM((RAD, mob_local, channels), frames.dtype),
             pltpu.VMEM((count_frames, mob_local, channels), jnp.bfloat16),
@@ -589,7 +607,7 @@
         compiler_params=pltpu.CompilerParams(
             collective_id=1, has_side_effects=True, vmem_limit_bytes=56 * 1024 * 1024
         ),
-    )(frames, kernels, half)
+    )(frames, half)
     return (
         rows_out.reshape(n_dy * n_dz * rows, channels),
         other_out.reshape(n_dy * n_dz * rows, channels),

time: 99.3 us -> 99.3 us (level)
  Pallas kernels: 89.7 us -> 91.4 us
  other arithmetic: 2.65 us -> 1.15 us
    unnamed x5 -> x0, other arithmetic: 1.23 us -> none
    pallas_call x1, Pallas kernels: 23 us -> 24.2 us  [reduce_owned(): pl.pallas_call(functools.partial(reduce_kernel, sizes), out_shape=jax.Sha...]
    unnamed x11 -> x9, local copies, waits for them, and re-layouts: 1.72 us -> 2.13 us
where the time goes in v21:
time: 99.3 us; the launch traced here: 99 us
  Pallas kernels  91.4 us (92%)
  local copies, waits for them, and re-layouts  3.96 us (4%)
  matrix products  1.73 us (2%)
  other arithmetic  1.15 us (1%)
    pallas_call x1, Pallas kernels, frame_work(): pl.pallas_call(functools.partial(frame_kernel, sizes), out_shape=(jax.Sha...  60.1 us
    pallas_call x1, Pallas kernels, reduce_owned(): pl.pallas_call(functools.partial(reduce_kernel, sizes), out_shape=jax.Sha...  24.2 us
    pallas_call x1, Pallas kernels, score_pairs(): pl.pallas_call(score_kernel, grid_spec=grid_spec, out_shape=jax.ShapeDtyp...  7.07 us
    unnamed x9, local copies, waits for them, and re-layouts  2.13 us

profile of v21, /device:TPU:1, one launch (start us, length us, event | category | flops | bytes accessed | tf_op | source)
XLA Modules:
  0.0 99.0 jit_solution(3402052574426186118)
XLA Ops:
  0.0 0.0 copy-start
  0.0 0.0 copy-start.2
  0.0 0.9 copy-done
  0.9 0.6 constant_dynamic-slice_fusion.half_ref
  1.5 60.1 %shard_map.64 = (bf16[32,128,256]{2,1,0:T(8,128)(2,1)}, bf16[32,128,256]{2,1,0:T(8,128)(2,1)}, bf16[6,16,256,256]{3,2,1,0:T(8,128)(2,1)}) custom-call(bf16[16,256,256]{2,1,0:T(8,128)(2,1)} %bitcast.49, bf16[128,256]{1,0:T(8,128)(2,1)} %constant_dynamic-slice_fusion.half_ref), custom_call_target="tpu_custom_call" | custom-call | tf_op jit(solution)/shard_map/pallas_call | solution.py:580
  62.3 0.0 copy-done.2
  62.3 1.0 %sort.17 = (s32[8]{0:T(128)}, s32[8]{0:T(128)}) sort(s32[8]{0:T(128)S(1)} %compare_select_fusion.2, s32[8]{0:T(128)S(1)} %iota.22), dimensions={0}, to_apply=%region_0.1 | sort | flops 24 | bytes 128 | tf_op jit(solution)/shard_map/jit(argsort)/sort | solution.py:655
  63.4 0.0 copy-start.3
  63.4 0.0 copy-start.1
  63.4 7.1 %shard_map.65 = f32[8,1,128]{2,1,0:T(1,128)} custom-call(s32[8]{0:T(128)} %get-tuple-element.9.order_ref, s32[8]{0:T(128)} %bitcast.53, s32[8]{0:T(128)} %bitcast.54, s32[1]{0:T(128)} %bitcast.46.count_ref, s32[1]{0:T(128)} %bitcast.8.section_ref, bf16[6,16,256,256]{3,2,1,0:T(8,128)(2,1)} %get-tuple-element.10.wave_ref, bf16[4096,256]{1,0:T(8,128)(2,1)} %bitcast.47, ...), custom_call_target="tpu_custom_call" | custom-call | tf_op jit(solution)/shard_map/pallas_call | solution.py:673
  70.4 0.0 copy-done.3
  70.5 0.0 copy-done.1
  70.5 0.6 gather_fusion
  71.1 0.1 add_select_fusion.1
  71.1 1.7 %fusion = f32[64,128]{1,0:T(8,128)S(1)} fusion(s32[1024]{0:T(1024)S(1)} %get-tuple-element.14, f32[1024]{0:T(1024)} %bitcast.52, s32[1024]{0:T(1024)S(1)} %get-tuple-element.13), kind=kOutput, calls=%fused_computation.2 | convolution fusion | flops 100925440 | bytes 45056 | tf_op jit(solution)/shard_map/ka,kb->ab/dot_general | solution.py:88
  72.9 0.6 copy.9
  73.5 24.2 %shard_map.66 = f32[1,256]{1,0:T(1,128)} custom-call(f32[8,4,1,256]{3,2,1,0:T(1,128)} %bitcast.50), custom_call_target="tpu_custom_call" | custom-call | tf_op jit(solution)/shard_map/pallas_call | solution.py:251
  97.7 1.2 %copy.12 = f32[1,256]{1,0:T(1,128)} copy(f32[1,256]{1,0:T(1,128)} %shard_map.66) | data formatting | bytes 2048
  (6 shorter events, 0.0 us)
Async XLA Ops:
  0.0 0.9 copy-start
  0.0 62.3 %copy-start.2 = (s32[1,1,8]{2,1,0:T(1,128)S(1)}, s32[1,1,8]{2,1,0:T(1,128)}, u32[]{:S(2)}) copy-start(s32[1,1,8]{2,1,0:T(1,128)} %param.9) | copy-start | bytes 100
  63.4 7.1 %copy-start.3 = (s32[1,1,8]{2,1,0:T(1,128)S(1)}, s32[1,1,8]{2,1,0:T(1,128)}, u32[]{:S(2)}) copy-start(s32[1,1,8]{2,1,0:T(1,128)} %param.8) | copy-start | bytes 100
  63.4 7.1 %copy-start.1 = (s32[8192]{0:T(1024)S(1)}, s32[8192]{0:T(1024)}, u32[]{:S(2)}) copy-start(s32[8192]{0:T(1024)} %param.11) | copy-start | bytes 98308

commit v22 on v21

--- a/solution.py
+++ b/solution.py
@@ -65,9 +65,7 @@
     section_index = lax.axis_index("section")
     mob_local = frames.shape[2]
     section_count = lax.axis_size("section")
-    half_rows = templates.shape[0] // 2
-    my_half = lax.dynamic_slice_in_dim(templates, section_index * half_rows, half_rows, 0)
-    my_rows, other_rows, wavelet_stack = frame_work(frames[0], my_half)
+    my_rows, other_rows, wavelet_stack = frame_work(frames[0], templates)
     slots = pair_block.shape[2]
     live_pairs = pair_count[0, 0, 0]
     block_ids = pair_block[0, 0]
@@ -276,7 +274,7 @@
 def frame_kernel(
     sizes,
     frames_ref,
-    half_ref,
+    templates_ref,
     out_ref,
     other_ref,
     wave_ref,
@@ -305,6 +303,8 @@
     dz = lax.axis_index("dz")
     dev = dy * n_dz + dz
     partner_section = (section + 1) % n_section
+    half_rows = out_ref.shape[1]
+    half_src = templates_ref.at[pl.ds(section * half_rows, half_rows)]
 
     def dev_peer(index):
         return (section, grp, index // n_dz, index % n_dz)
@@ -352,7 +352,7 @@
     extra = far_left.astype(jnp.int32) + far_right.astype(jnp.int32)
     pl.semaphore_wait(barrier, n_dz - 1 + 2 + 1 + extra)
 
-    own = pltpu.make_async_copy(half_ref, out_ref.at[dev], own_sem)
+    own = pltpu.make_async_copy(half_src, out_ref.at[dev], own_sem)
     own.start()
 
     def pair_copy(slot, source_ref):
@@ -365,11 +365,11 @@
             device_id_type=pl.DeviceIdType.MESH,
         )
 
-    pair_copy(dev, half_ref).start()
+    pair_copy(dev, half_src).start()
 
     def z_copy(target, source):
         return pltpu.make_async_remote_copy(
-            src_ref=half_ref,
+            src_ref=half_src,
             dst_ref=out_ref.at[dy * n_dz + source],
             send_sem=z_send.at[target],
             recv_sem=z_recv.at[source],
@@ -433,7 +433,7 @@
     def y_own(direction):
         target = up if direction == 0 else down
         return pltpu.make_async_remote_copy(
-            src_ref=half_ref,
+            src_ref=half_src,
             dst_ref=out_ref.at[dev],
             send_sem=y_send.at[direction * n_dy * n_dz + dev],
             recv_sem=y_recv.at[dev],
@@ -567,15 +567,16 @@
     for chunk in range(relay, n_dz):
         y_copy(1, up, chunk).wait_send()
     for slot in range(n_dev):
-        pair_copy(slot, half_ref).wait_recv()
+        pair_copy(slot, half_src).wait_recv()
     for slot in range(n_dev):
-        pair_copy(slot, half_ref).wait_send()
-
-
-def frame_work(frames, half):
+        pair_copy(slot, half_src).wait_send()
+
+
+def frame_work(frames, templates):
     sizes = (lax.axis_size("section"), lax.axis_size("dy"), lax.axis_size("dz"))
     n_section, n_dy, n_dz = sizes
-    rows, channels = half.shape
+    rows, channels = templates.shape[0] // 2, templates.shape[1]
+    half = templates
     count_frames, mob_local, _ = frames.shape
     rows_out, other_out, wave = pl.pallas_call(
         functools.partial(frame_kernel, sizes),
@@ -607,7 +608,7 @@
         compiler_params=pltpu.CompilerParams(
             collective_id=1, has_side_effects=True, vmem_limit_bytes=56 * 1024 * 1024
         ),
-    )(frames, half)
+    )(frames, templates)
     return (
         rows_out.reshape(n_dy * n_dz * rows, channels),
         other_out.reshape(n_dy * n_dz * rows, channels),

time: 99.3 us -> 97.8 us (0.985)
  local copies, waits for them, and re-layouts: 3.96 us -> 2.43 us
    unnamed x9 -> x7, local copies, waits for them, and re-layouts: 2.13 us -> 1.23 us
where the time goes in v22:
time: 97.8 us; the launch traced here: 97.3 us
  Pallas kernels  91.3 us (93%)
  local copies, waits for them, and re-layouts  2.43 us (2%)
  matrix products  1.73 us (2%)
  other arithmetic  1.15 us (1%)
    pallas_call x1, Pallas kernels, frame_work(): pl.pallas_call(functools.partial(frame_kernel, sizes), out_shape=(jax.Sha...  60.1 us
    pallas_call x1, Pallas kernels, reduce_owned(): pl.pallas_call(functools.partial(reduce_kernel, sizes), out_shape=jax.Sha...  24.1 us
    pallas_call x1, Pallas kernels, score_pairs(): pl.pallas_call(score_kernel, grid_spec=grid_spec, out_shape=jax.ShapeDtyp...  7.01 us

profile of v22, /device:TPU:1, one launch (start us, length us, event | category | flops | bytes accessed | tf_op | source)
XLA Modules:
  0.0 97.3 jit_solution(16179319836595340004)
XLA Ops:
  0.0 0.0 copy-start
  0.0 0.0 copy-start.1
  0.0 60.1 %shard_map.64 = (bf16[32,128,256]{2,1,0:T(8,128)(2,1)}, bf16[32,128,256]{2,1,0:T(8,128)(2,1)}, bf16[6,16,256,256]{3,2,1,0:T(8,128)(2,1)}) custom-call(bf16[16,256,256]{2,1,0:T(8,128)(2,1)} %bitcast.50, bf16[256,256]{1,0:T(8,128)(2,1)} %templates_ref.1), custom_call_target="tpu_custom_call" | custom-call | tf_op jit(solution)/shard_map/pallas_call | solution.py:581
  60.8 0.0 copy-done.1
  60.8 1.0 %sort.17 = (s32[8]{0:T(128)}, s32[8]{0:T(128)}) sort(s32[8]{0:T(128)S(1)} %compare_select_fusion.2, s32[8]{0:T(128)S(1)} %iota.22), dimensions={0}, to_apply=%region_0.1 | sort | flops 24 | bytes 128 | tf_op jit(solution)/shard_map/jit(argsort)/sort | solution.py:656
  61.9 0.0 copy-start.2
  61.9 7.0 %shard_map.65 = f32[8,1,128]{2,1,0:T(1,128)} custom-call(s32[8]{0:T(128)} %get-tuple-element.9.order_ref, s32[8]{0:T(128)} %bitcast.53, s32[8]{0:T(128)} %bitcast.54, s32[1]{0:T(128)} %bitcast.46.count_ref, s32[1]{0:T(128)} %bitcast.8.section_ref, bf16[6,16,256,256]{3,2,1,0:T(8,128)(2,1)} %get-tuple-element.10.wave_ref, bf16[4096,256]{1,0:T(8,128)(2,1)} %bitcast.48, ...), custom_call_target="tpu_custom_call" | custom-call | tf_op jit(solution)/shard_map/pallas_call | solution.py:674
  68.9 0.0 copy-done.2
  68.9 0.0 copy-done
  68.9 0.6 gather_fusion
  69.5 0.1 add_select_fusion.1
  69.6 1.7 %fusion = f32[64,128]{1,0:T(8,128)S(1)} fusion(s32[1024]{0:T(1024)S(1)} %get-tuple-element.14, f32[1024]{0:T(1024)} %bitcast.52, s32[1024]{0:T(1024)S(1)} %get-tuple-element.13), kind=kOutput, calls=%fused_computation.2 | convolution fusion | flops 100925440 | bytes 45056 | tf_op jit(solution)/shard_map/ka,kb->ab/dot_general | solution.py:86
  71.3 0.6 copy.9
  72.0 24.1 %shard_map.66 = f32[1,256]{1,0:T(1,128)} custom-call(f32[8,4,1,256]{3,2,1,0:T(1,128)} %bitcast.51), custom_call_target="tpu_custom_call" | custom-call | tf_op jit(solution)/shard_map/pallas_call | solution.py:249
  96.1 1.2 %copy.12 = f32[1,256]{1,0:T(1,128)} copy(f32[1,256]{1,0:T(1,128)} %shard_map.66) | data formatting | bytes 2048
  (6 shorter events, 0.0 us)
Async XLA Ops:
  0.0 68.9 %copy-start = (s32[8192]{0:T(1024)S(1)}, s32[8192]{0:T(1024)}, u32[]{:S(2)}) copy-start(s32[8192]{0:T(1024)} %param.11) | copy-start | bytes 98308
  0.0 60.8 %copy-start.1 = (s32[1,1,8]{2,1,0:T(1,128)S(1)}, s32[1,1,8]{2,1,0:T(1,128)}, u32[]{:S(2)}) copy-start(s32[1,1,8]{2,1,0:T(1,128)} %param.9) | copy-start | bytes 100
  61.9 7.0 %copy-start.2 = (s32[1,1,8]{2,1,0:T(1,128)S(1)}, s32[1,1,8]{2,1,0:T(1,128)}, u32[]{:S(2)}) copy-start(s32[1,1,8]{2,1,0:T(1,128)} %param.8) | copy-start | bytes 100

commit v23 on v22

--- a/solution.py
+++ b/solution.py
@@ -75,8 +75,12 @@
     )
     positions = jnp.take(owner_order.reshape(-1, PB), block_ids, axis=0).reshape(-1)
     groups = PREC // PB
+    n_dy, n_dz = lax.axis_size("dy"), lax.axis_size("dz")
+    shard = PREC // (n_dy * n_dz)
+    owner = positions // shard
+    line_group = ((owner % n_dz) * n_dy + owner // n_dz) * (shard // PB) + positions % shard // PB
     by_group = jnp.where(
-        (positions // PB)[:, None] == jnp.arange(groups, dtype=jnp.int32)[None, :],
+        line_group[:, None] == jnp.arange(groups, dtype=jnp.int32)[None, :],
         responses.reshape(-1)[:, None],
         0.0,
     )
@@ -90,8 +94,7 @@
         precision=lax.Precision.HIGHEST,
         preferred_element_type=jnp.float32,
     ).reshape(-1)
-    dev_count = lax.axis_size(DEV)
-    return reduce_owned(placed.reshape(dev_count, 1, PREC // dev_count))
+    return reduce_owned(placed.reshape(n_dz, n_dy, 1, shard))
 
 
 def reduce_kernel(
@@ -243,9 +246,9 @@
 def reduce_owned(payload):
     sizes = (lax.axis_size("section"), lax.axis_size("grp"), lax.axis_size("dy"), lax.axis_size("dz"))
     n_section, n_grp, n_dy, n_dz = sizes
-    rows, one, owned_width = payload.shape
+    lines = payload
+    one, owned_width = payload.shape[2:]
     width = owned_width + 128
-    lines = payload.reshape(n_dy, n_dz, one, owned_width).transpose(1, 0, 2, 3)
     return pl.pallas_call(
         functools.partial(reduce_kernel, sizes),
         out_shape=jax.ShapeDtypeStruct((1, owned_width), jnp.float32),

time: 97.8 us -> 97.8 us (level)
    pallas_call x1, Pallas kernels: 7.01 us -> 13.6 us  [score_pairs(): pl.pallas_call(score_kernel, grid_spec=grid_spec, out_shape=jax.ShapeDtyp...]
    pallas_call x1, Pallas kernels: 24.1 us -> 17.8 us  [reduce_owned(): pl.pallas_call(functools.partial(reduce_kernel, sizes), out_shape=jax.Sha...]
where the time goes in v23:
time: 97.8 us; the launch traced here: 97.6 us
  Pallas kernels  91.6 us (94%)
  matrix products  2.35 us (2%)
  local copies, waits for them, and re-layouts  1.79 us (2%)
  other arithmetic  1.16 us (1%)
    pallas_call x1, Pallas kernels, frame_work(): pl.pallas_call(functools.partial(frame_kernel, sizes), out_shape=(jax.Sha...  60.1 us
    pallas_call x1, Pallas kernels, reduce_owned(): pl.pallas_call(functools.partial(reduce_kernel, sizes), out_shape=jax.Sha...  17.8 us
    pallas_call x1, Pallas kernels, score_pairs(): pl.pallas_call(score_kernel, grid_spec=grid_spec, out_shape=jax.ShapeDtyp...  13.6 us
    dot_general x1, matrix products, on_device(): jnp.einsum('ka,kb->ab', by_group, by_lane, precision=lax.Precision.HIGHES...  2.35 us

profile of v23, /device:TPU:1, one launch (start us, length us, event | category | flops | bytes accessed | tf_op | source)
XLA Modules:
  0.0 97.6 jit_solution(17904477728927353326)
XLA Ops:
  0.0 0.0 copy-start
  0.0 0.0 copy-start.1
  0.0 60.1 %shard_map.64 = (bf16[32,128,256]{2,1,0:T(8,128)(2,1)}, bf16[32,128,256]{2,1,0:T(8,128)(2,1)}, bf16[6,16,256,256]{3,2,1,0:T(8,128)(2,1)}) custom-call(bf16[16,256,256]{2,1,0:T(8,128)(2,1)} %bitcast.42, bf16[256,256]{1,0:T(8,128)(2,1)} %templates_ref.1), custom_call_target="tpu_custom_call" | custom-call | tf_op jit(solution)/shard_map/pallas_call | solution.py:584
  60.8 0.0 copy-done.1
  60.8 1.0 %sort.17 = (s32[8]{0:T(128)}, s32[8]{0:T(128)}) sort(s32[8]{0:T(128)S(1)} %compare_select_fusion.2, s32[8]{0:T(128)S(1)} %iota.22), dimensions={0}, to_apply=%region_0.1 | sort | flops 24 | bytes 128 | tf_op jit(solution)/shard_map/jit(argsort)/sort | solution.py:659
  61.9 0.0 copy-start.2
  61.9 13.6 %shard_map.65 = f32[8,1,128]{2,1,0:T(1,128)} custom-call(s32[8]{0:T(128)} %get-tuple-element.9.order_ref, s32[8]{0:T(128)} %bitcast.45, s32[8]{0:T(128)} %bitcast.46, s32[1]{0:T(128)} %bitcast.38.count_ref, s32[1]{0:T(128)} %bitcast.8.section_ref, bf16[6,16,256,256]{3,2,1,0:T(8,128)(2,1)} %get-tuple-element.10.wave_ref, bf16[4096,256]{1,0:T(8,128)(2,1)} %bitcast.40, ...), custom_call_target="tpu_custom_call" | custom-call | tf_op jit(solution)/shard_map/pallas_call | solution.py:677
  75.5 0.0 copy-done.2
  75.5 0.0 copy-done
  75.5 0.6 gather_fusion
  76.1 0.1 fusion.9
  76.2 2.3 %fusion = f32[64,128]{1,0:T(8,128)} fusion(s32[1024]{0:T(1024)S(1)} %get-tuple-element.14, f32[1024]{0:T(1024)} %bitcast.44, s32[1024]{0:T(1024)S(1)} %get-tuple-element.13), kind=kOutput, calls=%fused_computation.2 | convolution fusion | flops 100925440 | bytes 45056 | tf_op jit(solution)/shard_map/ka,kb->ab/dot_general | solution.py:90
  78.6 17.8 %shard_map.66 = f32[1,256]{1,0:T(1,128)} custom-call(f32[8,4,1,256]{3,2,1,0:T(1,128)} %bitcast.43), custom_call_target="tpu_custom_call" | custom-call | tf_op jit(solution)/shard_map/pallas_call | solution.py:252
  96.3 1.2 %copy.9 = f32[1,256]{1,0:T(1,128)} copy(f32[1,256]{1,0:T(1,128)} %shard_map.66) | data formatting | bytes 2048
  (5 shorter events, 0.0 us)
Async XLA Ops:
  0.0 75.5 %copy-start = (s32[8192]{0:T(1024)S(1)}, s32[8192]{0:T(1024)}, u32[]{:S(2)}) copy-start(s32[8192]{0:T(1024)} %param.11) | copy-start | bytes 98308
  0.0 60.8 %copy-start.1 = (s32[1,1,8]{2,1,0:T(1,128)S(1)}, s32[1,1,8]{2,1,0:T(1,128)}, u32[]{:S(2)}) copy-start(s32[1,1,8]{2,1,0:T(1,128)} %param.9) | copy-start | bytes 100
  61.9 13.6 %copy-start.2 = (s32[1,1,8]{2,1,0:T(1,128)S(1)}, s32[1,1,8]{2,1,0:T(1,128)}, u32[]{:S(2)}) copy-start(s32[1,1,8]{2,1,0:T(1,128)} %param.8) | copy-start | bytes 100

commit v24 on v22

--- a/solution.py
+++ b/solution.py
@@ -625,15 +625,15 @@
 
     def score(rows_ref):
         rows = rows_ref[...]
-        acc = jnp.zeros((1, PB), jnp.float32)
+        acc = jnp.zeros((8, PB), jnp.float32)
         for level in range(SCALES):
             cells = wave_ref[level].reshape(-1, rows.shape[1])
             scores = lax.dot_general(
                 cells, rows, (((1,), (1,)), ((), ())), preferred_element_type=jnp.float32
             )
-            acc = acc + jnp.sum(jnp.maximum(scores, 0.0), axis=0, keepdims=True)
+            acc = acc + jnp.sum(jnp.maximum(scores, 0.0).reshape(-1, 8, PB), axis=0)
         cell_count = SCALES * wave_ref.shape[1] * wave_ref.shape[2]
-        out_ref[0] = acc / cell_count
+        out_ref[0] = jnp.sum(acc, axis=0, keepdims=True) / cell_count
 
     @pl.when(jnp.logical_and(live, mine))
     def _():

time: 97.8 us -> 96.8 us (0.990)
  no operation moved by 1% of the time
where the time goes in v24:
time: 96.8 us; the launch traced here: 96.5 us
  Pallas kernels  90.5 us (93%)
  local copies, waits for them, and re-layouts  2.43 us (3%)
  matrix products  1.74 us (2%)
  other arithmetic  1.15 us (1%)
    pallas_call x1, Pallas kernels, frame_work(): pl.pallas_call(functools.partial(frame_kernel, sizes), out_shape=(jax.Sha...  60.1 us
    pallas_call x1, Pallas kernels, reduce_owned(): pl.pallas_call(functools.partial(reduce_kernel, sizes), out_shape=jax.Sha...  23.3 us
    pallas_call x1, Pallas kernels, score_pairs(): pl.pallas_call(score_kernel, grid_spec=grid_spec, out_shape=jax.ShapeDtyp...  7.06 us

profile of v24, /device:TPU:1, one launch (start us, length us, event | category | flops | bytes accessed | tf_op | source)
XLA Modules:
  0.0 96.5 jit_solution(9713188801329877965)
XLA Ops:
  0.0 0.0 copy-start
  0.0 0.0 copy-start.1
  0.0 60.1 %shard_map.64 = (bf16[32,128,256]{2,1,0:T(8,128)(2,1)}, bf16[32,128,256]{2,1,0:T(8,128)(2,1)}, bf16[6,16,256,256]{3,2,1,0:T(8,128)(2,1)}) custom-call(bf16[16,256,256]{2,1,0:T(8,128)(2,1)} %bitcast.50, bf16[256,256]{1,0:T(8,128)(2,1)} %templates_ref.1), custom_call_target="tpu_custom_call" | custom-call | tf_op jit(solution)/shard_map/pallas_call | solution.py:581
  60.8 0.0 copy-done.1
  60.8 1.0 %sort.17 = (s32[8]{0:T(128)}, s32[8]{0:T(128)}) sort(s32[8]{0:T(128)S(1)} %compare_select_fusion.2, s32[8]{0:T(128)S(1)} %iota.22), dimensions={0}, to_apply=%region_0.1 | sort | flops 24 | bytes 128 | tf_op jit(solution)/shard_map/jit(argsort)/sort | solution.py:656
  61.9 0.0 copy-start.2
  61.9 7.1 %shard_map.65 = f32[8,1,128]{2,1,0:T(1,128)} custom-call(s32[8]{0:T(128)} %get-tuple-element.9.order_ref, s32[8]{0:T(128)} %bitcast.53, s32[8]{0:T(128)} %bitcast.54, s32[1]{0:T(128)} %bitcast.46.count_ref, s32[1]{0:T(128)} %bitcast.8.section_ref, bf16[6,16,256,256]{3,2,1,0:T(8,128)(2,1)} %get-tuple-element.10.wave_ref, bf16[4096,256]{1,0:T(8,128)(2,1)} %bitcast.48, ...), custom_call_target="tpu_custom_call" | custom-call | tf_op jit(solution)/shard_map/pallas_call | solution.py:674
  68.9 0.0 copy-done.2
  69.0 0.0 copy-done
  69.0 0.6 gather_fusion
  69.5 0.1 add_select_fusion.1
  69.6 1.7 %fusion = f32[64,128]{1,0:T(8,128)S(1)} fusion(s32[1024]{0:T(1024)S(1)} %get-tuple-element.14, f32[1024]{0:T(1024)} %bitcast.52, s32[1024]{0:T(1024)S(1)} %get-tuple-element.13), kind=kOutput, calls=%fused_computation.2 | convolution fusion | flops 100925440 | bytes 45056 | tf_op jit(solution)/shard_map/ka,kb->ab/dot_general | solution.py:86
  71.4 0.6 copy.9
  72.0 23.3 %shard_map.66 = f32[1,256]{1,0:T(1,128)} custom-call(f32[8,4,1,256]{3,2,1,0:T(1,128)} %bitcast.51), custom_call_target="tpu_custom_call" | custom-call | tf_op jit(solution)/shard_map/pallas_call | solution.py:249
  95.3 1.2 %copy.12 = f32[1,256]{1,0:T(1,128)} copy(f32[1,256]{1,0:T(1,128)} %shard_map.66) | data formatting | bytes 2048
  (6 shorter events, 0.0 us)
Async XLA Ops:
  0.0 69.0 %copy-start = (s32[8192]{0:T(1024)S(1)}, s32[8192]{0:T(1024)}, u32[]{:S(2)}) copy-start(s32[8192]{0:T(1024)} %param.11) | copy-start | bytes 98308
  0.0 60.8 %copy-start.1 = (s32[1,1,8]{2,1,0:T(1,128)S(1)}, s32[1,1,8]{2,1,0:T(1,128)}, u32[]{:S(2)}) copy-start(s32[1,1,8]{2,1,0:T(1,128)} %param.9) | copy-start | bytes 100
  61.9 7.1 %copy-start.2 = (s32[1,1,8]{2,1,0:T(1,128)S(1)}, s32[1,1,8]{2,1,0:T(1,128)}, u32[]{:S(2)}) copy-start(s32[1,1,8]{2,1,0:T(1,128)} %param.8) | copy-start | bytes 100

commit v25 on v22

--- a/solution.py
+++ b/solution.py
@@ -91,7 +91,16 @@
         preferred_element_type=jnp.float32,
     ).reshape(-1)
     dev_count = lax.axis_size(DEV)
-    return reduce_owned(placed.reshape(dev_count, 1, PREC // dev_count))
+    summed = reduce_owned(placed.reshape(dev_count, 1, PREC // dev_count))
+    owned_width = PREC // dev_count
+    run_totals = summed[:, owned_width:]
+    lanes = jnp.arange(run_totals.shape[1], dtype=jnp.int32)[None, :]
+    run_sum = jnp.sum(run_totals, axis=1, keepdims=True)
+    own_total = jnp.sum(
+        jnp.where(lanes == lax.axis_index("grp"), run_totals, 0.0), axis=1, keepdims=True
+    )
+    factor = (run_sum / lax.axis_size("grp")) / own_total
+    return summed[:, :owned_width] * factor
 
 
 def reduce_kernel(
@@ -120,7 +129,7 @@
     dy = lax.axis_index("dy")
     dz = lax.axis_index("dz")
     partner = (section + 1) % n_section
-    owned_width = out_ref.shape[1]
+    owned_width = mixed.shape[3]
 
     barrier = pltpu.get_barrier_semaphore()
     peers = [(partner, grp, dy, dz)]
@@ -233,11 +242,7 @@
     for side in range(n_section):
         for step in range(1, n_grp):
             core_copy(side, (grp + step) % n_grp).wait_send()
-    run_totals = summed[:, owned_width:]
-    run_sum = jnp.sum(run_totals, axis=1, keepdims=True)
-    own_total = jnp.sum(jnp.where(lanes == grp, run_totals, 0.0), axis=1, keepdims=True)
-    factor = (run_sum / n_grp) / own_total
-    out_ref[...] = summed[:, :owned_width] * factor
+    out_ref[...] = summed
 
 
 def reduce_owned(payload):
@@ -248,7 +253,7 @@
     lines = payload.reshape(n_dy, n_dz, one, owned_width).transpose(1, 0, 2, 3)
     return pl.pallas_call(
         functools.partial(reduce_kernel, sizes),
-        out_shape=jax.ShapeDtypeStruct((1, owned_width), jnp.float32),
+        out_shape=jax.ShapeDtypeStruct((1, width), jnp.float32),
         in_specs=[pl.BlockSpec(memory_space=pltpu.VMEM)],
         out_specs=pl.BlockSpec(memory_space=pltpu.VMEM),
         scratch_shapes=[

time: 97.8 us -> 99.7 us (1.019)
  other arithmetic: 1.15 us -> 3.69 us
  between operations: 0.73 us -> 2.12 us
  local copies, waits for them, and re-layouts: 2.43 us -> 1.22 us
    pallas_call x1, Pallas kernels: 24.1 us -> 16.8 us  [reduce_owned(): pl.pallas_call(functools.partial(reduce_kernel, sizes), out_shape=jax.Sha...]
    pallas_call x1, Pallas kernels: 7.01 us -> 13.8 us  [score_pairs(): pl.pallas_call(score_kernel, grid_spec=grid_spec, out_shape=jax.ShapeDtyp...]
    reduce_sum x0 -> x1, other arithmetic: none -> 1.32 us  [on_device(): jnp.sum(jnp.where(lanes == lax.axis_index('grp'), run_totals, 0.0), axis=...]
    mul x0 -> x1, other arithmetic: none -> 1.22 us  [on_device(): return summed[:, :owned_width] * factor]
    unnamed x7 -> x6, local copies, waits for them, and re-layouts: 1.23 us -> 0.01 us
where the time goes in v25:
time: 99.7 us; the launch traced here: 99.4 us
  Pallas kernels  90.7 us (91%)
  other arithmetic  3.69 us (4%)
  between operations  2.12 us (2%)
  matrix products  1.74 us (2%)
  local copies, waits for them, and re-layouts  1.22 us (1%)
    pallas_call x1, Pallas kernels, frame_work(): pl.pallas_call(functools.partial(frame_kernel, sizes), out_shape=(jax.Sha...  60.1 us
    pallas_call x1, Pallas kernels, reduce_owned(): pl.pallas_call(functools.partial(reduce_kernel, sizes), out_shape=jax.Sha...  16.8 us
    pallas_call x1, Pallas kernels, score_pairs(): pl.pallas_call(score_kernel, grid_spec=grid_spec, out_shape=jax.ShapeDtyp...  13.8 us

profile of v25, /device:TPU:1, one launch (start us, length us, event | category | flops | bytes accessed | tf_op | source)
XLA Modules:
  0.0 99.4 jit_solution(3058817605318897383)
XLA Ops:
  0.0 0.0 copy-start
  0.0 0.0 copy-start.1
  0.0 60.1 %shard_map.64 = (bf16[32,128,256]{2,1,0:T(8,128)(2,1)}, bf16[32,128,256]{2,1,0:T(8,128)(2,1)}, bf16[6,16,256,256]{3,2,1,0:T(8,128)(2,1)}) custom-call(bf16[16,256,256]{2,1,0:T(8,128)(2,1)} %bitcast.50, bf16[256,256]{1,0:T(8,128)(2,1)} %templates_ref.1), custom_call_target="tpu_custom_call" | custom-call | tf_op jit(solution)/shard_map/pallas_call | solution.py:586
  60.8 0.0 copy-done.1
  60.8 1.0 %sort.17 = (s32[8]{0:T(128)}, s32[8]{0:T(128)}) sort(s32[8]{0:T(128)S(1)} %compare_select_fusion.3, s32[8]{0:T(128)S(1)} %iota.25), dimensions={0}, to_apply=%region_0.1 | sort | flops 24 | bytes 128 | tf_op jit(solution)/shard_map/jit(argsort)/sort | solution.py:661
  61.9 0.0 copy-start.2
  61.9 13.8 %shard_map.65 = f32[8,1,128]{2,1,0:T(1,128)} custom-call(s32[8]{0:T(128)} %get-tuple-element.9.order_ref, s32[8]{0:T(128)} %bitcast.53, s32[8]{0:T(128)} %bitcast.54, s32[1]{0:T(128)} %bitcast.46.count_ref, s32[1]{0:T(128)} %bitcast.8.section_ref, bf16[6,16,256,256]{3,2,1,0:T(8,128)(2,1)} %get-tuple-element.10.wave_ref, bf16[4096,256]{1,0:T(8,128)(2,1)} %bitcast.48, ...), custom_call_target="tpu_custom_call" | custom-call | tf_op jit(solution)/shard_map/pallas_call | solution.py:679
  75.6 0.0 copy-done.2
  75.7 0.0 copy-done
  75.7 0.6 gather_fusion
  76.3 0.1 add_select_fusion.1
  76.3 1.7 %fusion = f32[64,128]{1,0:T(8,128)S(1)} fusion(s32[1024]{0:T(1024)S(1)} %get-tuple-element.16, f32[1024]{0:T(1024)} %bitcast.52, s32[1024]{0:T(1024)S(1)} %get-tuple-element.15), kind=kOutput, calls=%fused_computation.2 | convolution fusion | flops 100925440 | bytes 45056 | tf_op jit(solution)/shard_map/ka,kb->ab/dot_general | solution.py:86
  78.1 0.6 copy.9
  78.7 16.8 %shard_map.66 = f32[1,384]{1,0:T(1,128)} custom-call(f32[8,4,1,256]{3,2,1,0:T(1,128)} %bitcast.51), custom_call_target="tpu_custom_call" | custom-call | tf_op jit(solution)/shard_map/pallas_call | solution.py:254
  95.5 1.3 %fusion.9 = (f32[]{:T(128)}, f32[]{:T(128)}) fusion(f32[1,384]{1,0:T(1,128)} %shard_map.66, s32[]{:T(128)S(6)} %axis_index.28), kind=kLoop, calls=%fused_computation.27 | loop fusion | flops 510 | bytes 524 | tf_op jit(solution)/shard_map/reduce_sum | solution.py:99
  98.2 1.2 %slice_multiply_fusion = f32[1,256]{1,0:T(1,128)} fusion(f32[1,384]{1,0:T(1,128)} %shard_map.66, f32[]{:T(128)S(6)} %div.24), kind=kLoop, calls=%fused_computation.26 | loop fusion | flops 256 | bytes 2052 | tf_op jit(solution)/shard_map/mul | solution.py:103
  (6 shorter events, 0.0 us)
Async XLA Ops:
  0.0 75.7 %copy-start = (s32[8192]{0:T(1024)S(1)}, s32[8192]{0:T(1024)}, u32[]{:S(2)}) copy-start(s32[8192]{0:T(1024)} %param.11) | copy-start | bytes 98308
  0.0 60.8 %copy-start.1 = (s32[1,1,8]{2,1,0:T(1,128)S(1)}, s32[1,1,8]{2,1,0:T(1,128)}, u32[]{:S(2)}) copy-start(s32[1,1,8]{2,1,0:T(1,128)} %param.9) | copy-start | bytes 100
  61.9 13.8 %copy-start.2 = (s32[1,1,8]{2,1,0:T(1,128)S(1)}, s32[1,1,8]{2,1,0:T(1,128)}, u32[]{:S(2)}) copy-start(s32[1,1,8]{2,1,0:T(1,128)} %param.8) | copy-start | bytes 100

commit v26 on v22

--- a/solution.py
+++ b/solution.py
@@ -450,8 +450,6 @@
             y_copy(direction, dy, source).start()
         pair_copy(dy * n_dz + source, out_ref.at[dy * n_dz + source]).start()
     own.wait()
-    for step in range(1, n_dz):
-        z_copy((dz + step) % n_dz, dz).wait_send()
 
     @pl.when(has_left)
     def _():
@@ -570,6 +568,8 @@
         pair_copy(slot, half_src).wait_recv()
     for slot in range(n_dev):
         pair_copy(slot, half_src).wait_send()
+    for step in range(1, n_dz):
+        z_copy((dz + step) % n_dz, dz).wait_send()
 
 
 def frame_work(frames, templates):

time: 97.8 us -> 97.7 us (level)
    pallas_call x1, Pallas kernels: 24.1 us -> 18.4 us  [reduce_owned(): pl.pallas_call(functools.partial(reduce_kernel, sizes), out_shape=jax.Sha...]
    pallas_call x1, Pallas kernels: 7.01 us -> 12.1 us  [score_pairs(): pl.pallas_call(score_kernel, grid_spec=grid_spec, out_shape=jax.ShapeDtyp...]
where the time goes in v26:
time: 97.7 us; the launch traced here: 96.6 us
  Pallas kernels  90.6 us (93%)
  local copies, waits for them, and re-layouts  2.43 us (2%)
  matrix products  1.74 us (2%)
  other arithmetic  1.15 us (1%)
    pallas_call x1, Pallas kernels, frame_work(): pl.pallas_call(functools.partial(frame_kernel, sizes), out_shape=(jax.Sha...  60.1 us
    pallas_call x1, Pallas kernels, reduce_owned(): pl.pallas_call(functools.partial(reduce_kernel, sizes), out_shape=jax.Sha...  18.4 us
    pallas_call x1, Pallas kernels, score_pairs(): pl.pallas_call(score_kernel, grid_spec=grid_spec, out_shape=jax.ShapeDtyp...  12.1 us

profile of v26, /device:TPU:1, one launch (start us, length us, event | category | flops | bytes accessed | tf_op | source)
XLA Modules:
  0.0 96.6 jit_solution(15461214873077418952)
XLA Ops:
  0.0 0.0 copy-start
  0.0 0.0 copy-start.1
  0.0 60.1 %shard_map.64 = (bf16[32,128,256]{2,1,0:T(8,128)(2,1)}, bf16[32,128,256]{2,1,0:T(8,128)(2,1)}, bf16[6,16,256,256]{3,2,1,0:T(8,128)(2,1)}) custom-call(bf16[16,256,256]{2,1,0:T(8,128)(2,1)} %bitcast.50, bf16[256,256]{1,0:T(8,128)(2,1)} %templates_ref.1), custom_call_target="tpu_custom_call" | custom-call | tf_op jit(solution)/shard_map/pallas_call | solution.py:581
  60.8 0.0 copy-done.1
  60.8 1.0 %sort.17 = (s32[8]{0:T(128)}, s32[8]{0:T(128)}) sort(s32[8]{0:T(128)S(1)} %compare_select_fusion.2, s32[8]{0:T(128)S(1)} %iota.22), dimensions={0}, to_apply=%region_0.1 | sort | flops 24 | bytes 128 | tf_op jit(solution)/shard_map/jit(argsort)/sort | solution.py:656
  61.9 0.0 copy-start.2
  61.9 12.1 %shard_map.65 = f32[8,1,128]{2,1,0:T(1,128)} custom-call(s32[8]{0:T(128)} %get-tuple-element.9.order_ref, s32[8]{0:T(128)} %bitcast.53, s32[8]{0:T(128)} %bitcast.54, s32[1]{0:T(128)} %bitcast.46.count_ref, s32[1]{0:T(128)} %bitcast.8.section_ref, bf16[6,16,256,256]{3,2,1,0:T(8,128)(2,1)} %get-tuple-element.10.wave_ref, bf16[4096,256]{1,0:T(8,128)(2,1)} %bitcast.48, ...), custom_call_target="tpu_custom_call" | custom-call | tf_op jit(solution)/shard_map/pallas_call | solution.py:674
  74.0 0.0 copy-done.2
  74.0 0.0 copy-done
  74.0 0.6 gather_fusion
  74.6 0.1 add_select_fusion.1
  74.7 1.7 %fusion = f32[64,128]{1,0:T(8,128)S(1)} fusion(s32[1024]{0:T(1024)S(1)} %get-tuple-element.14, f32[1024]{0:T(1024)} %bitcast.52, s32[1024]{0:T(1024)S(1)} %get-tuple-element.13), kind=kOutput, calls=%fused_computation.2 | convolution fusion | flops 100925440 | bytes 45056 | tf_op jit(solution)/shard_map/ka,kb->ab/dot_general | solution.py:86
  76.4 0.6 copy.9
  77.1 18.4 %shard_map.66 = f32[1,256]{1,0:T(1,128)} custom-call(f32[8,4,1,256]{3,2,1,0:T(1,128)} %bitcast.51), custom_call_target="tpu_custom_call" | custom-call | tf_op jit(solution)/shard_map/pallas_call | solution.py:249
  95.4 1.2 %copy.12 = f32[1,256]{1,0:T(1,128)} copy(f32[1,256]{1,0:T(1,128)} %shard_map.66) | data formatting | bytes 2048
  (6 shorter events, 0.0 us)
Async XLA Ops:
  0.0 74.0 %copy-start = (s32[8192]{0:T(1024)S(1)}, s32[8192]{0:T(1024)}, u32[]{:S(2)}) copy-start(s32[8192]{0:T(1024)} %param.11) | copy-start | bytes 98308
  0.0 60.8 %copy-start.1 = (s32[1,1,8]{2,1,0:T(1,128)S(1)}, s32[1,1,8]{2,1,0:T(1,128)}, u32[]{:S(2)}) copy-start(s32[1,1,8]{2,1,0:T(1,128)} %param.9) | copy-start | bytes 100
  61.9 12.1 %copy-start.2 = (s32[1,1,8]{2,1,0:T(1,128)S(1)}, s32[1,1,8]{2,1,0:T(1,128)}, u32[]{:S(2)}) copy-start(s32[1,1,8]{2,1,0:T(1,128)} %param.8) | copy-start | bytes 100

commit v27 on v26

--- a/solution.py
+++ b/solution.py
@@ -449,7 +449,6 @@
         for direction in (0, 1):
             y_copy(direction, dy, source).start()
         pair_copy(dy * n_dz + source, out_ref.at[dy * n_dz + source]).start()
-    own.wait()
 
     @pl.when(has_left)
     def _():
@@ -570,6 +569,7 @@
         pair_copy(slot, half_src).wait_send()
     for step in range(1, n_dz):
         z_copy((dz + step) % n_dz, dz).wait_send()
+    own.wait()
 
 
 def frame_work(frames, templates):

time: 97.7 us -> 97.3 us (level)
    pallas_call x1, Pallas kernels: 18.4 us -> 23.4 us  [reduce_owned(): pl.pallas_call(functools.partial(reduce_kernel, sizes), out_shape=jax.Sha...]
    pallas_call x1, Pallas kernels: 12.1 us -> 7.08 us  [score_pairs(): pl.pallas_call(score_kernel, grid_spec=grid_spec, out_shape=jax.ShapeDtyp...]
where the time goes in v27:
time: 97.3 us; the launch traced here: 96.7 us
  Pallas kernels  90.6 us (93%)
  local copies, waits for them, and re-layouts  2.43 us (2%)
  matrix products  1.73 us (2%)
  other arithmetic  1.15 us (1%)
    pallas_call x1, Pallas kernels, frame_work(): pl.pallas_call(functools.partial(frame_kernel, sizes), out_shape=(jax.Sha...  60.1 us
    pallas_call x1, Pallas kernels, reduce_owned(): pl.pallas_call(functools.partial(reduce_kernel, sizes), out_shape=jax.Sha...  23.4 us
    pallas_call x1, Pallas kernels, score_pairs(): pl.pallas_call(score_kernel, grid_spec=grid_spec, out_shape=jax.ShapeDtyp...  7.08 us

profile of v27, /device:TPU:1, one launch (start us, length us, event | category | flops | bytes accessed | tf_op | source)
XLA Modules:
  0.0 96.7 jit_solution(15444520237156833533)
XLA Ops:
  0.0 0.0 copy-start
  0.0 0.0 copy-start.1
  0.0 60.1 %shard_map.64 = (bf16[32,128,256]{2,1,0:T(8,128)(2,1)}, bf16[32,128,256]{2,1,0:T(8,128)(2,1)}, bf16[6,16,256,256]{3,2,1,0:T(8,128)(2,1)}) custom-call(bf16[16,256,256]{2,1,0:T(8,128)(2,1)} %bitcast.50, bf16[256,256]{1,0:T(8,128)(2,1)} %templates_ref.1), custom_call_target="tpu_custom_call" | custom-call | tf_op jit(solution)/shard_map/pallas_call | solution.py:581
  60.8 0.0 copy-done.1
  60.8 1.0 %sort.17 = (s32[8]{0:T(128)}, s32[8]{0:T(128)}) sort(s32[8]{0:T(128)S(1)} %compare_select_fusion.2, s32[8]{0:T(128)S(1)} %iota.22), dimensions={0}, to_apply=%region_0.1 | sort | flops 24 | bytes 128 | tf_op jit(solution)/shard_map/jit(argsort)/sort | solution.py:656
  61.9 0.0 copy-start.2
  61.9 7.1 %shard_map.65 = f32[8,1,128]{2,1,0:T(1,128)} custom-call(s32[8]{0:T(128)} %get-tuple-element.9.order_ref, s32[8]{0:T(128)} %bitcast.53, s32[8]{0:T(128)} %bitcast.54, s32[1]{0:T(128)} %bitcast.46.count_ref, s32[1]{0:T(128)} %bitcast.8.section_ref, bf16[6,16,256,256]{3,2,1,0:T(8,128)(2,1)} %get-tuple-element.10.wave_ref, bf16[4096,256]{1,0:T(8,128)(2,1)} %bitcast.48, ...), custom_call_target="tpu_custom_call" | custom-call | tf_op jit(solution)/shard_map/pallas_call | solution.py:674
  69.0 0.0 copy-done.2
  69.0 0.0 copy-done
  69.0 0.6 gather_fusion
  69.6 0.1 add_select_fusion.1
  69.7 1.7 %fusion = f32[64,128]{1,0:T(8,128)S(1)} fusion(s32[1024]{0:T(1024)S(1)} %get-tuple-element.14, f32[1024]{0:T(1024)} %bitcast.52, s32[1024]{0:T(1024)S(1)} %get-tuple-element.13), kind=kOutput, calls=%fused_computation.2 | convolution fusion | flops 100925440 | bytes 45056 | tf_op jit(solution)/shard_map/ka,kb->ab/dot_general | solution.py:86
  71.4 0.6 copy.9
  72.0 23.4 %shard_map.66 = f32[1,256]{1,0:T(1,128)} custom-call(f32[8,4,1,256]{3,2,1,0:T(1,128)} %bitcast.51), custom_call_target="tpu_custom_call" | custom-call | tf_op jit(solution)/shard_map/pallas_call | solution.py:249
  95.5 1.2 %copy.12 = f32[1,256]{1,0:T(1,128)} copy(f32[1,256]{1,0:T(1,128)} %shard_map.66) | data formatting | bytes 2048
  (6 shorter events, 0.0 us)
Async XLA Ops:
  0.0 69.0 %copy-start = (s32[8192]{0:T(1024)S(1)}, s32[8192]{0:T(1024)}, u32[]{:S(2)}) copy-start(s32[8192]{0:T(1024)} %param.11) | copy-start | bytes 98308
  0.0 60.8 %copy-start.1 = (s32[1,1,8]{2,1,0:T(1,128)S(1)}, s32[1,1,8]{2,1,0:T(1,128)}, u32[]{:S(2)}) copy-start(s32[1,1,8]{2,1,0:T(1,128)} %param.9) | copy-start | bytes 100
  61.9 7.1 %copy-start.2 = (s32[1,1,8]{2,1,0:T(1,128)S(1)}, s32[1,1,8]{2,1,0:T(1,128)}, u32[]{:S(2)}) copy-start(s32[1,1,8]{2,1,0:T(1,128)} %param.8) | copy-start | bytes 100
